TPU v7x, 32 devices: a whole 2x2x4 slice. The times are simulated.
32 devices in a mesh: dp: 4 (over y, x), seq: 8 (over z, core).
Axes of the slice: x: 2, y: 2, z: 4, core: 2. Of those that a mesh axis runs over, the one named last changes fastest.
Arguments:
- tokens: float32 [16, 2048, 768], P('dp', 'seq')
- lengths: int32 [16], P('dp'), may hold values from 1024 to 2048
- keep: int32 [16, 2048], P('dp', 'seq'), may hold values from 0 to 1, as said below
- w_query: float32 [768, 768], replicated, may hold values from -0.21875 to 0.21875
- b_query: float32 [768], replicated, may hold values from -3 to 3
- w_key: float32 [768, 768], replicated, may hold values from -0.21875 to 0.21875
- w_value: float32 [768, 768], replicated, may hold values from -0.21875 to 0.21875
- b_value: float32 [768], replicated, may hold values from -3 to 3
- conv_weight: float32 [12, 33], replicated, may hold values from -0.5 to 0.5
- w_out: float32 [768, 768], replicated, may hold values from -0.4375 to 0.4375
- b_out: float32 [768], replicated, may hold values from -2 to 2
- gain_one: float32 [768], replicated, may hold values from 0.5 to 1.5
- shift_one: float32 [768], replicated, may hold values from -2 to 2
- w_up: float32 [768, 3072], replicated, may hold values from -0.21875 to 0.21875
- b_up: float32 [3072], replicated, may hold values from -2 to 2
- w_down: float32 [3072, 768], replicated, may hold values from -0.109375 to 0.109375
- b_down: float32 [768], replicated, may hold values from -2 to 2
- gain_two: float32 [768], replicated, may hold values from 0.5 to 1.5
- shift_two: float32 [768], replicated, may hold values from -2 to 2
- cotangent: float32 [16, 2048, 768], P('dp', 'seq'), may hold values from -6 to 6
Outputs:
- output: float32 [16, 2048, 768], P('dp', 'seq')
- grad_tokens: float32 [16, 2048, 768], P('dp', 'seq')
- grad_w_query: float32 [768, 768], P('dp', 'seq')
- grad_b_query: float32 [768], replicated
- grad_w_key: float32 [768, 768], P('dp', 'seq')
- grad_w_value: float32 [768, 768], P('dp', 'seq')
- grad_b_value: float32 [768], replicated
- grad_conv: float32 [12, 33], replicated
- grad_w_out: float32 [768, 768], P('dp', 'seq')
- grad_b_out: float32 [768], replicated
- grad_gain_one: float32 [768], replicated
- grad_shift_one: float32 [768], replicated
- grad_w_up: float32 [768, 3072], P('dp', 'seq')
- grad_b_up: float32 [3072], replicated
- grad_w_down: float32 [3072, 768], P('dp', 'seq')
- grad_b_down: float32 [768], replicated
- grad_gain_two: float32 [768], replicated
- grad_shift_two: float32 [768], replicated
Inputs may be any that keep to these rules, and one draw needn't show every extreme that they name: `keep`: in every item, a run of 66 consecutive positions within the first 1024 positions is 0; elsewhere a position is 1 with probability 17 / 20.
All inputs are finite; a program needn't handle non-finite values.
Results may differ from a plain program's by a relative error of at most 0.0003.
Values sent between devices are 32-bit elements; how exact they have to be, the bound alone decides.
A program may use at most 384 MiB of HBM per device.

v0:
```python
import jax
import jax.numpy as jnp
from jax import lax
from jax.sharding import PartitionSpec as P

MARKS = 64
NEWTON = 6


highest = lax.Precision.HIGHEST
epsilon = 1e-05


def merged(x, axis, combine):
    everything = jax.tree.map(lambda part: lax.all_gather(part, axis), x)
    initial = jax.tree.map(lambda part: part[0], everything)

    def lap(k, so_far):
        return combine(so_far, jax.tree.map(lambda part: part[k], everything))

    return lax.fori_loop(1, lax.axis_size(axis), lap, initial)


def padded_2(cells, sides, width):
    for axis, dim in sides:
        count = lax.axis_size(axis)
        ends = count - 1
        head = lax.slice_in_dim(cells, 0, width, axis=dim)
        tail = lax.slice_in_dim(cells, cells.shape[dim] - width, cells.shape[dim], axis=dim)
        cells = jnp.concatenate(
            [
                lax.ppermute(tail, axis, [(i, (i + 1) % count) for i in range(ends)]),
                cells,
                lax.ppermute(head, axis, [((i + 1) % count, i) for i in range(ends)]),
            ],
            axis=dim,
        )
    return cells


def newton(kernel):
    identity = jnp.eye(kernel.shape[-1], dtype=jnp.float32)
    approx = jnp.swapaxes(kernel, -1, -2) / jnp.sum(kernel * kernel, axis=(-2, -1), keepdims=True)
    for iteration in range(NEWTON):
        product = jnp.einsum("...ij,...jk->...ik", kernel, approx, precision=highest)
        nested = 7.0 * identity - product
        nested = 15.0 * identity - jnp.einsum(
            "...ij,...jk->...ik", product, nested, precision=highest
        )
        nested = 13.0 * identity - jnp.einsum(
            "...ij,...jk->...ik", product, nested, precision=highest
        )
        approx = 0.25 * jnp.einsum("...ij,...jk->...ik", approx, nested, precision=highest)
    return approx


def normalize(inputs):
    center = inputs - jnp.mean(inputs, axis=-1, keepdims=True)
    inv_root = lax.rsqrt(jnp.mean(center * center, axis=-1, keepdims=True) + epsilon)
    return (center * inv_root, inv_root)


def norm_back(grad_scaled, scaled, inv_root):
    first_mean = jnp.mean(grad_scaled, axis=-1, keepdims=True)
    second_mean = jnp.mean(grad_scaled * scaled, axis=-1, keepdims=True)
    return inv_root * (grad_scaled - first_mean - scaled * second_mean)


def gelu_exact(inputs):
    return jax.nn.gelu(inputs, approximate=False)


def softmax_merge(earlier, later):
    top_a, total_a, weighted_a = earlier
    top_b, total_b, weighted_b = later
    largest = jnp.maximum(top_a, top_b)
    scale_a = jnp.exp(top_a - largest)
    scale_b = jnp.exp(top_b - largest)
    return (
        largest,
        total_a * scale_a + total_b * scale_b,
        weighted_a * scale_a[..., None] + weighted_b * scale_b[..., None],
    )


def row_sums(array_in):
    return jnp.sum(array_in, axis=(0, 1))


def on_device(
    tokens,
    lengths,
    keep,
    w_query,
    b_query,
    w_key,
    w_value,
    b_value,
    conv_weight,
    w_out,
    b_out,
    gain_one,
    shift_one,
    w_up,
    b_up,
    w_down,
    b_down,
    gain_two,
    shift_two,
    cotangent,
):
    items, span, width = tokens.shape
    heads, taps = conv_weight.shape
    head_size = width // heads
    margin = taps // 2
    factor = head_size ** (-0.25)
    offset = lax.axis_index("seq") * span
    position = offset + jnp.arange(span, dtype=jnp.int32)
    inside = position[None, :] < lengths[:, None]
    usable = (inside & (keep > 0)).astype(jnp.float32)
    segment = jnp.where(inside, position[None, :] * MARKS // lengths[:, None], MARKS)
    member = (segment[:, :, None] == jnp.arange(MARKS, dtype=jnp.int32)[None, None, :]).astype(
        jnp.float32
    )
    member = member * usable[:, :, None]
    local_counts = jnp.sum(member, axis=1)
    queries = (jnp.einsum("itd,de->ite", tokens, w_query, precision=highest) + b_query) * factor
    key_rows = jnp.einsum("itd,de->ite", tokens, w_key, precision=highest) * factor
    values = jnp.einsum("itd,de->ite", tokens, w_value, precision=highest) + b_value
    sum_query = jnp.einsum("itm,ite->ime", member, queries, precision=highest)
    sum_key = jnp.einsum("itm,ite->ime", member, key_rows, precision=highest)
    sum_query, sum_key, counts = lax.psum((sum_query, sum_key, local_counts), "seq")
    divisor = jnp.maximum(counts, 1.0)[:, :, None]
    land_query = sum_query / divisor
    land_key = sum_key / divisor
    query_heads = queries.reshape(items, span, heads, head_size)
    key_heads = key_rows.reshape(items, span, heads, head_size)
    value_heads = values.reshape(items, span, heads, head_size)
    land_q = land_query.reshape(items, MARKS, heads, head_size)
    land_k = land_key.reshape(items, MARKS, heads, head_size)
    kernel_one = jax.nn.softmax(
        jnp.einsum("ijhe,ithe->ihjt", land_k, query_heads, precision=highest), axis=2
    )
    kernel_two = jax.nn.softmax(
        jnp.einsum("ijhe,ikhe->ihjk", land_q, land_k, precision=highest), axis=-1
    )
    key_mask = usable[:, None, None, :]
    scores_three = jnp.einsum("ijhe,ithe->ihjt", land_q, key_heads, precision=highest)
    masked = jnp.where(key_mask > 0, scores_three, -1e30)
    local_top = jnp.max(masked, axis=-1)
    local_weights = jnp.exp(masked - local_top[..., None]) * key_mask
    local_total = jnp.sum(local_weights, axis=-1)
    local_weighted = jnp.einsum("ihjt,ithe->ihje", local_weights, value_heads, precision=highest)
    largest, totals, weighted = merged(
        (local_top, local_total, local_weighted), "seq", softmax_merge
    )
    context = weighted / totals[..., None]
    kernel_three = jnp.exp(masked - largest[..., None]) * key_mask / totals[..., None]
    inverse, newton_back = jax.vjp(newton, kernel_two)
    mixed_context = jnp.einsum("ihjk,ihke->ihje", inverse, context, precision=highest)
    nystrom = jnp.einsum("ihjt,ihje->ithe", kernel_one, mixed_context, precision=highest)
    masked_values = value_heads * usable[:, :, None, None]
    padded = padded_2(masked_values, (("seq", 1),), margin)
    conv_out = jnp.zeros_like(masked_values)
    for tap_index in range(taps):
        conv_out = (
            conv_out
            + conv_weight[:, tap_index][None, None, :, None]
            * padded[:, tap_index : tap_index + span]
        )
    attn_input = (nystrom + conv_out).reshape(items, span, width)
    attention = jnp.einsum("itd,de->ite", attn_input, w_out, precision=highest) + b_out
    scaled_one, root_one = normalize(tokens + attention)
    hidden_one = scaled_one * gain_one + shift_one
    pre_up = jnp.einsum("itd,df->itf", hidden_one, w_up, precision=highest) + b_up
    act_up, gelu_back = jax.vjp(gelu_exact, pre_up)
    down_out = jnp.einsum("itf,fd->itd", act_up, w_down, precision=highest) + b_down
    scaled_two, root_two = normalize(hidden_one + down_out)
    output = scaled_two * gain_two + shift_two
    grad_gain_two = row_sums(cotangent * scaled_two)
    grad_shift_two = row_sums(cotangent)
    grad_res_two = norm_back(cotangent * gain_two, scaled_two, root_two)
    grad_b_down = row_sums(grad_res_two)
    grad_w_down = jnp.einsum("itf,itd->fd", act_up, grad_res_two, precision=highest)
    grad_act = jnp.einsum("itd,fd->itf", grad_res_two, w_down, precision=highest)
    (grad_pre_up,) = gelu_back(grad_act)
    grad_b_up = row_sums(grad_pre_up)
    grad_w_up = jnp.einsum("itd,itf->df", hidden_one, grad_pre_up, precision=highest)
    grad_hidden = grad_res_two + jnp.einsum("itf,df->itd", grad_pre_up, w_up, precision=highest)
    grad_gain_one = row_sums(grad_hidden * scaled_one)
    grad_shift_one = row_sums(grad_hidden)
    grad_res_one = norm_back(grad_hidden * gain_one, scaled_one, root_one)
    grad_b_out = row_sums(grad_res_one)
    grad_w_out = jnp.einsum("itd,ite->de", attn_input, grad_res_one, precision=highest)
    grad_pre = jnp.einsum("ite,de->itd", grad_res_one, w_out, precision=highest)
    grad_pre = grad_pre.reshape(items, span, heads, head_size)
    conv_rows = []
    for tap_index in range(taps):
        conv_rows.append(
            jnp.sum(grad_pre * padded[:, tap_index : tap_index + span], axis=(0, 1, 3))
        )
    grad_conv = jnp.stack(conv_rows, axis=1)
    grad_padded = padded_2(grad_pre, (("seq", 1),), margin)
    grad_masked = jnp.zeros_like(grad_pre)
    for tap_index in range(taps):
        lower = 2 * margin - tap_index
        grad_masked = (
            grad_masked
            + conv_weight[:, tap_index][None, None, :, None] * grad_padded[:, lower : lower + span]
        )
    grad_values = grad_masked * usable[:, :, None, None]
    grad_kernel_one = jnp.einsum("ithe,ihje->ihjt", grad_pre, mixed_context, precision=highest)
    part_mixed = jnp.einsum("ihjt,ithe->ihje", kernel_one, grad_pre, precision=highest)
    grad_scores_one = kernel_one * (
        grad_kernel_one - jnp.sum(kernel_one * grad_kernel_one, axis=2, keepdims=True)
    )
    grad_query_heads = jnp.einsum("ihjt,ijhe->ithe", grad_scores_one, land_k, precision=highest)
    part_land_key = jnp.einsum("ihjt,ithe->ijhe", grad_scores_one, query_heads, precision=highest)
    grad_mixed, part_land_key = lax.psum((part_mixed, part_land_key), "seq")
    grad_inverse = jnp.einsum("ihje,ihke->ihjk", grad_mixed, context, precision=highest)
    grad_context = jnp.einsum("ihjk,ihje->ihke", inverse, grad_mixed, precision=highest)
    (grad_kernel_two,) = newton_back(grad_inverse)
    grad_scores_two = kernel_two * (
        grad_kernel_two - jnp.sum(kernel_two * grad_kernel_two, axis=-1, keepdims=True)
    )
    grad_land_query = jnp.einsum("ihjk,ikhe->ijhe", grad_scores_two, land_k, precision=highest)
    grad_land_key = part_land_key + jnp.einsum(
        "ihjk,ijhe->ikhe", grad_scores_two, land_q, precision=highest
    )
    grad_values = grad_values + jnp.einsum(
        "ihjt,ihje->ithe", kernel_three, grad_context, precision=highest
    )
    grad_kernel_three = jnp.einsum("ihje,ithe->ihjt", grad_context, value_heads, precision=highest)
    row_dot = jnp.sum(grad_context * context, axis=-1)
    grad_scores_three = kernel_three * (grad_kernel_three - row_dot[..., None])
    grad_key_heads = jnp.einsum("ihjt,ijhe->ithe", grad_scores_three, land_q, precision=highest)
    part_land_query = jnp.einsum("ihjt,ithe->ijhe", grad_scores_three, key_heads, precision=highest)
    part_land_query = lax.psum(part_land_query, "seq")
    grad_land_query = grad_land_query + part_land_query
    spread_query = grad_land_query.reshape(items, MARKS, width) / divisor
    spread_key = grad_land_key.reshape(items, MARKS, width) / divisor
    grad_queries = (
        grad_query_heads.reshape(items, span, width)
        + jnp.einsum("itm,ime->ite", member, spread_query, precision=highest)
    ) * factor
    grad_keys = (
        grad_key_heads.reshape(items, span, width)
        + jnp.einsum("itm,ime->ite", member, spread_key, precision=highest)
    ) * factor
    grad_vals = grad_values.reshape(items, span, width)
    grad_w_query = jnp.einsum("itd,ite->de", tokens, grad_queries, precision=highest)
    grad_b_query = row_sums(grad_queries)
    grad_w_key = jnp.einsum("itd,ite->de", tokens, grad_keys, precision=highest)
    grad_w_value = jnp.einsum("itd,ite->de", tokens, grad_vals, precision=highest)
    grad_b_value = row_sums(grad_vals)
    grad_tokens = (
        grad_res_one
        + jnp.einsum("ite,de->itd", grad_queries, w_query, precision=highest)
        + jnp.einsum("ite,de->itd", grad_keys, w_key, precision=highest)
        + jnp.einsum("ite,de->itd", grad_vals, w_value, precision=highest)
    )
    grad_w_query, grad_w_key, grad_w_value, grad_w_out, grad_w_up, grad_w_down = (
        lax.psum_scatter(grad_w_query, "seq", scatter_dimension=1, tiled=True),
        lax.psum_scatter(grad_w_key, "seq", scatter_dimension=1, tiled=True),
        lax.psum_scatter(grad_w_value, "seq", scatter_dimension=1, tiled=True),
        lax.psum_scatter(grad_w_out, "seq", scatter_dimension=1, tiled=True),
        lax.psum_scatter(grad_w_up, "seq", scatter_dimension=1, tiled=True),
        lax.psum_scatter(grad_w_down, "seq", scatter_dimension=1, tiled=True),
    )
    grad_w_query, grad_w_key, grad_w_value, grad_w_out, grad_w_up, grad_w_down = (
        lax.psum_scatter(grad_w_query, "dp", scatter_dimension=0, tiled=True),
        lax.psum_scatter(grad_w_key, "dp", scatter_dimension=0, tiled=True),
        lax.psum_scatter(grad_w_value, "dp", scatter_dimension=0, tiled=True),
        lax.psum_scatter(grad_w_out, "dp", scatter_dimension=0, tiled=True),
        lax.psum_scatter(grad_w_up, "dp", scatter_dimension=0, tiled=True),
        lax.psum_scatter(grad_w_down, "dp", scatter_dimension=0, tiled=True),
    )
    (
        grad_b_query,
        grad_b_value,
        grad_conv,
        grad_b_out,
        grad_gain_one,
        grad_shift_one,
        grad_b_up,
        grad_b_down,
        grad_gain_two,
        grad_shift_two,
    ) = lax.psum(
        (
            grad_b_query,
            grad_b_value,
            grad_conv,
            grad_b_out,
            grad_gain_one,
            grad_shift_one,
            grad_b_up,
            grad_b_down,
            grad_gain_two,
            grad_shift_two,
        ),
        ("dp", "seq"),
    )
    return (
        output,
        grad_tokens,
        grad_w_query,
        grad_b_query,
        grad_w_key,
        grad_w_value,
        grad_b_value,
        grad_conv,
        grad_w_out,
        grad_b_out,
        grad_gain_one,
        grad_shift_one,
        grad_w_up,
        grad_b_up,
        grad_w_down,
        grad_b_down,
        grad_gain_two,
        grad_shift_two,
    )


def solution(mesh):
    in_specs = (
        P("dp", "seq", None),
        P("dp"),
        P("dp", "seq"),
        P(),
        P(),
        P(),
        P(),
        P(),
        P(),
        P(),
        P(),
        P(),
        P(),
        P(),
        P(),
        P(),
        P(),
        P(),
        P(),
        P("dp", "seq", None),
    )
    out_specs = (
        P("dp", "seq", None),
        P("dp", "seq", None),
        P("dp", "seq"),
        P(),
        P("dp", "seq"),
        P("dp", "seq"),
        P(),
        P(),
        P("dp", "seq"),
        P(),
        P(),
        P(),
        P("dp", "seq"),
        P(),
        P("dp", "seq"),
        P(),
        P(),
        P(),
    )
    return jax.shard_map(
        on_device, mesh=mesh, in_specs=in_specs, out_specs=out_specs, check_vma=False
    )
```

profile of v0, /device:TPU:0, one launch (start us, length us, event | category | flops | bytes accessed | tf_op | source)
XLA Modules:
  0.0 1415.2 jit_solution(7666298331711490860)
XLA Ops:
  7.3 11.6 fusion.196
  35.9 10.8 fusion.191
  46.8 21.8 %add_multiply_fusion.2 = f32[4,256,768]{2,1,0:T(8,128)S(1)} fusion(f32[4,256,768]{2,1,0:T(8,128)S(1)} %copy-done.6, f32[768,768]{1,0:T(8,128)S(1)} %copy-done.105, f32[768]{0:T(1024)S(1)} %copy-done.162), kind=kOutput, calls=%fused_computation.346 | convolution fusion | flops 7249330176 | bytes 8653824 | tf_op jit(solution)/shard_map/itd,de->ite/dot_general | solution.py:127
  83.4 20.1 %psum.113 = f32[4,64]{1,0:T(4,128)S(1)} all-reduce(f32[4,64]{1,0:T(4,128)S(1)} %select_reduce_fusion.1), channel_id=1, replica_groups=mesh['dp'=4,'seq'=8] {'seq'}, use_global_device_ids=true, to_apply=%region_2.3 | all-reduce | flops 256 | bytes 2048 | tf_op jit(solution)/shard_map/psum | solution.py:132
  110.1 32.8 %all-reduce.11.cloned.1.call-done = (f32[4,64,768]{2,1,0:T(8,128)}, f32[4,64,768]{2,1,0:T(8,128)}) async-done(((f32[4,64,768]{2,1,0:T(8,128)}, f32[4,64,768]{2,1,0:T(8,128)}), (f32[4,64,768]{2,1,0:T(8,128)}, f32[4,64,768]{2,1,0:T(8,128)})) %all-reduce.11.cloned.1.call-update) | async-done | bytes 1572880 | tf_op jit(solution)/shard_map/psum | solution.py:132
  148.1 5.9 select_reduce_fusion
  164.6 15.1 %all-gather.1 = f32[32,12,64]{2,1,0:T(8,128)S(1)} all-gather(f32[4,12,64]{2,1,0:T(8,128)S(1)} %fusion.150), channel_id=3, replica_groups=mesh['dp'=4,'seq'=8] {'seq'}, dimensions={0}, use_global_device_ids=true | all-gather | bytes 110592 | tf_op jit(solution)/shard_map/all_gather | solution.py:15
  179.7 17.6 %all-gather = f32[32,12,64]{2,1,0:T(8,128)S(1)} all-gather(f32[4,12,64]{2,1,0:T(8,128)S(1)} %get-tuple-element.393), channel_id=2, replica_groups=mesh['dp'=4,'seq'=8] {'seq'}, dimensions={0}, use_global_device_ids=true | all-gather | bytes 110592 | tf_op jit(solution)/shard_map/all_gather | solution.py:15
  282.2 23.0 %while.19 = (s32[]{:T(128)}, f32[4,12,64]{2,1,0:T(8,128)S(1)}, f32[4,12,64]{2,1,0:T(8,128)S(1)}, f32[4,12,64,64]{3,2,1,0:T(8,128)}, f32[8,4,12,64]{3,2,1,0:T(8,1...) while((s32[]{:T(128)}, f32[4,12,64]{2,1,0:T(8,128)S(1)}, ...), condition=%wide.region_10.11_spmd, body=%wide.region_9.10_spmd.sunk | while | flops 608261 | bytes 2482319 | solution.py:21
  308.3 5.9 fusion.288
  314.3 51.4 %bitcast_add_fusion = f32[4,256,12,64]{1,3,2,0:T(8,128)} fusion(f32[4,256,12,64]{1,3,2,0:T(8,128)S(1)} %copy-done.3, f32[4,12,64,64]{3,2,1,0:T(8,128)} %fusion.288, f32[4,16,12,64]{1,3,2,0:T(8,128)S(1)} %copy-done.52, f32[4,16,12,64]{1,3,2,0:T(8,128)} %copy.284, f32[12]{0:T(128)} %get-tuple-element.344, f32[12]{0:T(128)} %get-tuple-element.345, ...), kind=kOutput, calls=%fused_computation.291 | convolution fusion | flops 681050112 | bytes 10618416 | tf_op jit(solution)/shard_map/ihjt,ihje->ithe/dot_general | solution.py:161
  365.7 10.5 fusion.304
  377.1 39.4 %fusion.148 = (u8[256,3072]{1,0:T(8,128)(4,1)S(1)}, u8[256,3072]{1,0:T(8,128)(4,1)S(1)}, f32[4,256,3072]{2,1,0:T(8,128)}) fusion(f32[3072]{0:T(1024)S(1)} %copy-done.137, f32[768,3072]{1,0:T(8,128)} %param.35, f32[768]{0:T(1024)S(1)} %copy-done.124, f32[768]{0:T(1024)S(1)} %copy-done.122, f32[4,256]{1,0:T(4,128)S(1)} %add_rsqrt_fusion.1, ...), kind=kOutput, calls=%fused_computation.348 | convolution fusion | flops 29036642304 | bytes 26765312 | tf_op jit(solution)/shard_map/itd,df->itf/dot_general | solution.py:175
  416.6 30.2 %fusion.5 = f32[4,256,3072]{2,1,0:T(8,128)} fusion(f32[4,256,3072]{2,1,0:T(8,128)} %get-tuple-element.399, f32[3072]{0:T(1024)S(1)} %copy-done.137, u8[256,3072]{1,0:T(8,128)(4,1)S(1)} %get-tuple-element.272, u8[256,3072]{1,0:T(8,128)(4,1)S(1)} %get-tuple-element.271), kind=kLoop, calls=%fused_computation.71 | loop fusion | flops 213909504 | bytes 26750976 | tf_op jit(solution)/shard_map/jvp()/erfc | solution.py:70
  446.8 39.2 %fusion.305 = (f32[4,256]{1,0:T(4,128)S(1)}, f32[4,256,768]{2,1,0:T(8,128)S(1)}) fusion(f32[768]{0:T(1024)S(1)} %copy-done.163, f32[3072,768]{1,0:T(8,128)} %param.37, f32[4,256,3072]{2,1,0:T(8,128)} %fusion.5, f32[4,256,3072]{2,1,0:T(8,128)} %get-tuple-element.399, f32[3072]{0:T(1024)S(1)} %copy-done.137, f32[768]{0:T(1024)S(1)} %copy-done.124, ...), kind=kOutput, calls=%fused_computation.593 | convolution fusion | flops 29005971456 | bytes 40928256 | tf_op jit(solution)/shard_map/itf,fd->itd/dot_general | solution.py:177
  493.1 42.0 %fusion.308 = (f32[3072]{0:T(1024)}, f32[4,256,3072]{2,1,0:T(8,128)}) fusion(f32[4,256,3072]{2,1,0:T(8,128)} %fusion.5, f32[4,256,768]{2,1,0:T(8,128)S(1)} %get-tuple-element.379, f32[3072,768]{1,0:T(8,128)} %param.37, f32[4,256,3072]{2,1,0:T(8,128)} %get-tuple-element.399, f32[3072]{0:T(1024)S(1)} %copy-done.137), kind=kOutput, calls=%fused_computation.596 | convolution fusion | flops 29038211072 | bytes 50356224 | tf_op jit(solution)/shard_map/itd,fd->itf/dot_general | solution.py:185
  535.1 39.6 %multiply_reduce_fusion.1 = (f32[768]{0:T(1024)}, f32[4,256]{1,0:T(4,128)S(1)}, f32[4,256]{1,0:T(4,128)S(1)}, f32[768]{0:T(1024)}, f32[4,256,768]{2,1,0:T(8,128)S(1)}) fusion(f32[4,256]{1,0:T(4,128)S(1)} %add_rsqrt_fusion.1, f32[4,256,768]{2,1,0:T(8,128)S(1)} %get-tuple-element.398, f32[4,256]{1,0:T(4,128)S(1)} %broadcast_multiply_fusion.6, ...), kind=kOutput, calls=%fused_computation.293 | convolution fusion | flops 28998889472 | bytes 31482880 | tf_op jit(solution)/shard_map/itf,df->itd/dot_general | solution.py:189
  576.6 10.2 multiply_reduce_fusion.18
  589.4 7.3 fusion.290
  596.7 7.3 multiply_reduce_fusion.35
  604.5 8.3 convolution_bitcast_fusion.6
  612.8 56.9 %all-reduce.7.cloned.1.call-done = f32[4,12,64,64]{3,2,1,0:T(8,128)} async-done(((f32[4,12,64,64]{3,2,1,0:T(8,128)}), f32[4,12,64,64]{3,2,1,0:T(8,128)}) %all-reduce.7.cloned.1.call-update) | async-done | bytes 786448 | tf_op jit(solution)/shard_map/psum | solution.py:219
  669.7 5.2 multiply_reduce_fusion.42
  696.4 11.6 convolution_bitcast_fusion.2
  713.5 7.0 fusion.328
  839.5 52.8 %fusion.307 = (f32[12,64]{1,0:T(8,128)S(1)}, f32[4,256,12,64]{1,3,2,0:T(8,128)}) fusion(f32[4,12,64,64]{2,3,1,0:T(8,128)S(1)} %copy-done.108, f32[4,12,64,256]{3,2,1,0:T(8,128)} %copy-done.30, f32[4,12,64]{2,1,0:T(8,128)S(1)} %get-tuple-element.197, f32[4,12,64]{2,1,0:T(8,128)S(1)} %get-tuple-element.198, f32[4,256]{1,0:T(4,128)S(1)} %copy-done.115, ...), kind=kOutput, calls=%fused_computation.595 | convolution fusion | flops 685767936 | bytes 11485920 | tf_op jit(solution)/shard_map/ihjt,ihje->ithe/dot_general | solution.py:230
  892.3 10.6 convolution_bitcast_fusion.3
  929.5 5.9 bitcast_add_fusion.1
  938.2 5.4 add_multiply_fusion
  945.2 9.9 convolution_bitcast_fusion.4
  955.2 8.2 fusion.239
  967.1 5.8 bitcast_add_fusion.2
  982.5 10.3 convolution_bitcast_fusion.5
  992.8 37.3 %convolution_bitcast_fusion = f32[3072,768]{0,1:T(8,128)} fusion(f32[4,256,768]{2,1,0:T(8,128)} %copy-done.103, f32[4,256,3072]{2,1,0:T(8,128)} %fusion.5, f32[4,256,3072]{2,1,0:T(8,128)} %get-tuple-element.399, f32[3072]{0:T(1024)S(1)} %copy-done.138), kind=kOutput, calls=%fused_computation.159 | convolution fusion | flops 29000466432 | bytes 37761024 | tf_op jit(solution)/shard_map/itf,itd->fd/dot_general | solution.py:184
  1032.1 35.4 %convolution_bitcast_fusion.1 = f32[768,3072]{1,0:T(8,128)} fusion(f32[4,256,3072]{2,1,0:T(8,128)} %get-tuple-element.418, f32[768]{0:T(1024)S(1)} %copy-done.125, f32[768]{0:T(1024)S(1)} %copy-done.123, f32[4,256,768]{2,1,0:T(8,128)S(1)} %copy-done.23, f32[4,256]{1,0:T(4,128)S(1)} %copy-done.119, f32[4,256]{1,0:T(4,128)S(1)} %copy-done.117), kind=kOutput, calls=%fused_computation.160 | convolution fusion | flops 28994174976 | bytes 25180160 | tf_op jit(solution)/shard_map/itd,itf->df/dot_general | solution.py:188
  1075.9 13.4 multiply_reduce_fusion.3
  1089.5 45.2 %reduce-scatter.33.cloned.1.call-done = f32[3072,96]{0,1:T(8,128)} async-done(((f32[3072,768]{0,1:T(8,128)}), f32[3072,96]{0,1:T(8,128)}) %reduce-scatter.33.cloned.1.call-update) | async-done | bytes 1179664 | tf_op jit(solution)/shard_map/reduce_scatter | solution.py:268
  1134.8 16.3 %multiply_reduce_fusion.2 = (f32[12]{0:T(128)S(1)}, f32[12]{0:T(128)S(1)}, f32[12]{0:T(128)S(1)}, f32[12]{0:T(128)S(1)}, f32[12]{0:T(128)S(1)}, /*index=5*/f32[1...) fusion(f32[4,256,12,64]{1,3,2,0:T(8,128)} %bitcast.353, f32[4,16,12,64]{1,3,2,0:T(8,128)} %copy.284, ...), kind=kLoop, calls=%fused_computation.294 | loop fusion | flops 21233556 | bytes 6488496 | tf_op jit(solution)/shard_map/reduce_sum | solution.py:200
  1151.3 12.1 multiply_reduce_fusion.28
  1163.5 71.2 %reduce-scatter.29.cloned.1.call-done = f32[768,384]{1,0:T(8,128)} async-done(((f32[768,3072]{1,0:T(8,128)}), f32[768,384]{1,0:T(8,128)}) %reduce-scatter.29.cloned.1.call-update) | async-done | bytes 1179664 | tf_op jit(solution)/shard_map/reduce_scatter | solution.py:267
  1234.9 14.9 %multiply_reduce_fusion.19 = (f32[12]{0:T(128)S(1)}, f32[12]{0:T(128)S(1)}, f32[12]{0:T(128)S(1)}, f32[12]{0:T(128)S(1)}, f32[12]{0:T(128)S(1)}, /*index=5*/f32[...) fusion(f32[4,256,12,64]{1,3,2,0:T(8,128)} %bitcast.355, f32[4,256,12,64]{1,3,2,0:T(8,128)S(1)} %copy-done.4, ...), kind=kLoop, calls=%fused_computation.311 | loop fusion | flops 21233556 | bytes 6488496 | tf_op jit(solution)/shard_map/reduce_sum | solution.py:200
  1252.5 39.5 %all-reduce = (f32[768]{0:T(1024)}, f32[768]{0:T(1024)}, f32[12,33]{1,0:T(8,128)}, f32[768]{0:T(1024)}, f32[768]{0:T(1024)}, /*index=5*/f32[768]{0:T(1024)}, f32...) all-reduce(f32[768]{0:T(1024)S(1)} %get-tuple-element.411, ...), channel_id=1, replica_groups=mesh['dp'=4,'seq'=8] {'dp','seq'}, use_global_device_ids=true, to_apply=%region_31.32 | all-reduce | flops 9612 | bytes 76896 | tf_op jit(solution)/shard_map/psum | solution.py:289
  1292.0 10.8 fusion.159
  1302.8 8.3 fusion.163
  1311.1 17.4 %add_add_fusion = f32[4,256,768]{2,1,0:T(8,128)} fusion(f32[4,256,768]{2,1,0:T(8,128)S(1)} %fusion.159, f32[4,256,768]{2,1,0:T(8,128)S(1)} %copy-done.25, f32[4,256,768]{2,1,0:T(8,128)S(1)} %fusion.163, f32[4,256,768]{1,2,0:T(8,128)S(1)} %bitcast.375, f32[768,768]{1,0:T(8,128)S(1)} %copy-done.104), kind=kOutput, calls=%fused_computation.327 | convolution fusion | flops 7250116608 | bytes 18087936 | tf_op jit(solution)/shard_map/ite,de->itd/dot_general | solution.py:260
  1328.5 15.8 %reduce-scatter.37.cloned.1.call-done = f32[192,96]{1,0:T(8,128)} async-done(((f32[768,96]{1,0:T(8,128)}), f32[192,96]{1,0:T(8,128)}) %reduce-scatter.37.cloned.1.call-update) | async-done | bytes 73744
  1344.4 31.9 %reduce-scatter.35.cloned.1.call-done = f32[768,96]{0,1:T(8,128)} async-done(((f32[3072,96]{0,1:T(8,128)}), f32[768,96]{0,1:T(8,128)}) %reduce-scatter.35.cloned.1.call-update) | async-done | bytes 294928 | tf_op jit(solution)/shard_map/reduce_scatter | solution.py:276
  1376.3 31.9 %reduce-scatter.31.cloned.1.call-done = f32[192,384]{1,0:T(8,128)} async-done(((f32[768,384]{1,0:T(8,128)}), f32[192,384]{1,0:T(8,128)}) %reduce-scatter.31.cloned.1.call-update) | async-done | bytes 294928 | tf_op jit(solution)/shard_map/reduce_scatter | solution.py:275
  (570 shorter events, 380.2 us)
Async XLA Ops:
  7.2 358.5 %copy-start = (f32[768,768]{1,0:T(8,128)S(1)}, f32[768,768]{1,0:T(8,128)}, u32[]{:S(2)}) copy-start(f32[768,768]{1,0:T(8,128)} %param.31) | copy-start | bytes 7077892
  7.2 135.7 %all-reduce.11.cloned.1.call-start = ((), (), s32[]{:S(2)}) async-start(), calls=%async_computation.27 | async-start | bytes 3145728 | tf_op jit(solution)/shard_map/psum | solution.py:132
  22.5 137.9 %copy-start.114 = (f32[4,256]{1,0:T(4,128)}, f32[4,256]{1,0:T(4,128)S(1)}, u32[]{:S(2)}) copy-start(f32[4,256]{1,0:T(4,128)S(1)} %get-tuple-element.383) | copy-start | bytes 12292
  22.5 137.9 %copy-start.134 = (pred[4,256]{1,0:T(4,128)(4,1)}, pred[4,256]{1,0:T(4,128)(4,1)S(1)}, u32[]{:S(2)}) copy-start(pred[4,256]{1,0:T(4,128)(4,1)S(1)} %get-tuple-element.382) | copy-start | bytes 3076
  29.3 79.1 %collective-permute-start = (f32[4,16,12,64]{3,1,2,0:T(8,128)S(1)}, f32[4,16,12,64]{3,1,2,0:T(8,128)S(1)}, u32[]{:S(2)}, u32[]{:S(2)}) collective-permute-start(f32[4,16,12,64]{3,1,2,0:T(8,128)S(1)} %copy.281), channel_id=1, source_target_pairs={{0,1},{1,2},{2,3},{3,4},{4,5},{5,6},{6,7},{8,9},{9,10},{10,11},{11... | collective-permute-start | bytes 589832 | tf_op jit(solution)/shard_map/ppermute | solution.py:32
  34.3 71.4 %collective-permute-start.1 = (f32[4,16,12,64]{3,1,2,0:T(8,128)}, f32[4,16,12,64]{3,1,2,0:T(8,128)}, u32[]{:S(2)}, u32[]{:S(2)}) collective-permute-start(f32[4,16,12,64]{3,1,2,0:T(8,128)} %copy.283), channel_id=1, source_target_pairs={{1,0},{2,1},{3,2},{4,3},{5,4},{6,5},{7,6},{9,8},{10,9},{11,10},{12... | collective-permute-start | bytes 589832 | tf_op jit(solution)/shard_map/ppermute | solution.py:34
  46.8 26.4 %copy-start.33 = (f32[4,256,768]{2,1,0:T(8,128)}, f32[4,256,768]{2,1,0:T(8,128)S(1)}, u32[]{:S(2)}) copy-start(f32[4,256,768]{2,1,0:T(8,128)S(1)} %fusion.191) | copy-start | bytes 9437188
  76.1 203.3 %all-gather.5.cloned.1.call-start = ((), (), s32[]{:S(2)}) async-start(), calls=%async_computation.21 | async-start | bytes 14155776 | tf_op jit(solution)/shard_map/all_gather | solution.py:15
  79.8 23.8 %copy-start.86 = (f32[12,33]{1,0:T(8,128)S(1)}, f32[12,33]{1,0:T(8,128)}, u32[]{:S(2)}) copy-start(f32[12,33]{1,0:T(8,128)} %param.30) | copy-start | bytes 4756
  104.6 209.6 %copy-start.148 = (f32[12]{0:T(128)}, f32[12]{0:T(128)S(1)}, u32[]{:S(2)}) copy-start(f32[12]{0:T(128)S(1)} %get-tuple-element.332) | copy-start | bytes 148
  104.6 209.6 %copy-start.150 = (f32[12]{0:T(128)}, f32[12]{0:T(128)S(1)}, u32[]{:S(2)}) copy-start(f32[12]{0:T(128)S(1)} %get-tuple-element.333) | copy-start | bytes 148
  104.6 209.6 %copy-start.152 = (f32[12]{0:T(128)}, f32[12]{0:T(128)S(1)}, u32[]{:S(2)}) copy-start(f32[12]{0:T(128)S(1)} %get-tuple-element.334) | copy-start | bytes 148
  104.6 209.6 %copy-start.154 = (f32[12]{0:T(128)}, f32[12]{0:T(128)S(1)}, u32[]{:S(2)}) copy-start(f32[12]{0:T(128)S(1)} %get-tuple-element.335) | copy-start | bytes 148
  104.6 209.6 %copy-start.156 = (f32[12]{0:T(128)}, f32[12]{0:T(128)S(1)}, u32[]{:S(2)}) copy-start(f32[12]{0:T(128)S(1)} %get-tuple-element.336) | copy-start | bytes 148
  104.6 209.6 %copy-start.158 = (f32[12]{0:T(128)}, f32[12]{0:T(128)S(1)}, u32[]{:S(2)}) copy-start(f32[12]{0:T(128)S(1)} %get-tuple-element.337) | copy-start | bytes 148
  104.6 209.6 %copy-start.160 = (f32[12]{0:T(128)}, f32[12]{0:T(128)S(1)}, u32[]{:S(2)}) copy-start(f32[12]{0:T(128)S(1)} %get-tuple-element.338) | copy-start | bytes 148
  104.6 154.8 %copy-start.101 = (f32[64,64]{1,0:T(8,128)}, f32[64,64]{1,0:T(8,128)S(1)}, u32[]{:S(2)}) copy-start(f32[64,64]{1,0:T(8,128)S(1)} %get-tuple-element.421) | copy-start | bytes 49156
  105.7 39.6 %copy-start.126 = (f32[4,64]{1,0:T(4,128)}, f32[4,64]{1,0:T(4,128)S(1)}, u32[]{:S(2)}) copy-start(f32[4,64]{1,0:T(4,128)S(1)} %broadcast_maximum_fusion) | copy-start | bytes 3076
  160.4 509.3 %all-reduce.7.cloned.1.call-start = ((), (), s32[]{:S(2)}) async-start(), calls=%async_computation.12 | async-start | bytes 3145728 | tf_op jit(solution)/shard_map/psum | solution.py:219
  204.7 52.0 %copy-start.48 = (f32[4,12,64,64]{2,3,1,0:T(8,128)}, f32[4,12,64,64]{2,3,1,0:T(8,128)S(1)}, u32[]{:S(2)}) copy-start(f32[4,12,64,64]{2,3,1,0:T(8,128)S(1)} %get-tuple-element.392) | copy-start | bytes 2359300
  204.7 52.0 %copy-start.112 = (f32[4,12,64]{2,1,0:T(8,128)}, f32[4,12,64]{2,1,0:T(8,128)S(1)}, u32[]{:S(2)}) copy-start(f32[4,12,64]{2,1,0:T(8,128)S(1)} %get-tuple-element.391) | copy-start | bytes 36868
  314.3 51.5 %copy-start.141 = (f32[768]{0:T(1024)S(1)}, f32[768]{0:T(1024)}, u32[]{:S(2)}) copy-start(f32[768]{0:T(1024)} %param.32) | copy-start | bytes 9220
  376.3 198.4 %copy-start.22 = (f32[4,256,768]{2,1,0:T(8,128)}, f32[4,256,768]{2,1,0:T(8,128)S(1)}, u32[]{:S(2)}) copy-start(f32[4,256,768]{2,1,0:T(8,128)S(1)} %get-tuple-element.398) | copy-start | bytes 9437188
  376.4 198.4 %copy-start.116 = (f32[4,256]{1,0:T(4,128)}, f32[4,256]{1,0:T(4,128)S(1)}, u32[]{:S(2)}) copy-start(f32[4,256]{1,0:T(4,128)S(1)} %broadcast_multiply_fusion.6) | copy-start | bytes 12292
  377.1 197.6 %copy-start.118 = (f32[4,256]{1,0:T(4,128)}, f32[4,256]{1,0:T(4,128)S(1)}, u32[]{:S(2)}) copy-start(f32[4,256]{1,0:T(4,128)S(1)} %add_rsqrt_fusion.1) | copy-start | bytes 12292
  416.5 30.2 %copy-start.163 = (f32[768]{0:T(1024)S(1)}, f32[768]{0:T(1024)}, u32[]{:S(2)}) copy-start(f32[768]{0:T(1024)} %param.38) | copy-start | bytes 9220
  493.0 42.0 %copy-start.103 = (f32[4,256,768]{2,1,0:T(8,128)}, f32[4,256,768]{2,1,0:T(8,128)S(1)}, u32[]{:S(2)}) copy-start(f32[4,256,768]{2,1,0:T(8,128)S(1)} %get-tuple-element.379) | copy-start | bytes 9437188
  589.4 250.0 %copy-start.5 = (f32[4,256,768]{1,2,0:T(8,128)}, f32[4,256,768]{1,2,0:T(8,128)S(1)}, u32[]{:S(2)}) copy-start(f32[4,256,768]{1,2,0:T(8,128)S(1)} %copy.286) | copy-start | bytes 9437188
  604.0 325.5 %all-reduce.9.cloned.1.call-start = ((), (), s32[]{:S(2)}) async-start(), calls=%async_computation.26 | async-start | bytes 6291456 | tf_op jit(solution)/shard_map/psum | solution.py:219
  612.8 62.1 %copy-start.135 = (pred[4,256]{1,0:T(4,128)(4,1)S(1)}, pred[4,256]{1,0:T(4,128)(4,1)}, u32[]{:S(2)}) copy-start(pred[4,256]{1,0:T(4,128)(4,1)} %copy-done.134) | copy-start | bytes 3076
  685.5 382.0 %reduce-scatter.27.cloned.1.call-start = ((), (), s32[]{:S(2)}) async-start(), calls=%async_computation.16 | async-start | bytes 2654208 | tf_op jit(solution)/shard_map/reduce_scatter | solution.py:266
  693.1 17.8 %collective-permute-start.3 = (f32[4,16,12,64]{3,1,2,0:T(8,128)}, f32[4,16,12,64]{3,1,2,0:T(8,128)}, u32[]{:S(2)}, u32[]{:S(2)}) collective-permute-start(f32[4,16,12,64]{3,1,2,0:T(8,128)} %copy.320), channel_id=1, source_target_pairs={{0,1},{1,2},{2,3},{3,4},{4,5},{5,6},{6,7},{8,9},{9,10},{10,11},{11... | collective-permute-start | bytes 589832 | tf_op jit(solution)/shard_map/ppermute | solution.py:32
  695.1 13.1 collective-permute-start.2
  708.0 361.7 %reduce-scatter.25.cloned.1.call-start = ((), (), s32[]{:S(2)}) async-start(), calls=%async_computation.15 | async-start | bytes 2654208 | tf_op jit(solution)/shard_map/reduce_scatter | solution.py:265
  839.5 52.8 %copy-start.7 = (f32[4,256,768]{2,1,0:T(8,128)S(1)}, f32[4,256,768]{2,1,0:T(8,128)}, u32[]{:S(2)}) copy-start(f32[4,256,768]{2,1,0:T(8,128)} %param.22) | copy-start | bytes 9437188
  902.9 168.8 %reduce-scatter.23.cloned.1.call-start = ((), (), s32[]{:S(2)}) async-start(), calls=%async_computation.14 | async-start | bytes 2654208 | tf_op jit(solution)/shard_map/reduce_scatter | solution.py:264
  955.2 118.8 %reduce-scatter.21.cloned.1.call-start = ((), (), s32[]{:S(2)}) async-start(), calls=%async_computation.13 | async-start | bytes 2654208 | tf_op jit(solution)/shard_map/reduce_scatter | solution.py:263
  992.8 141.9 %reduce-scatter.33.cloned.1.call-start = ((), (), s32[]{:S(2)}) async-start(), calls=%async_computation.19 | async-start | bytes 10616832 | tf_op jit(solution)/shard_map/reduce_scatter | solution.py:268
  1030.2 204.5 %reduce-scatter.29.cloned.1.call-start = ((), (), s32[]{:S(2)}) async-start(), calls=%async_computation.17 | async-start | bytes 10616832 | tf_op jit(solution)/shard_map/reduce_scatter | solution.py:267
  1067.5 261.0 %reduce-scatter.43.cloned.1.call-start = ((), (), s32[]{:S(2)}) async-start(), calls=%async_computation.25 | async-start | bytes 491520
  1069.6 258.9 %reduce-scatter.41.cloned.1.call-start = ((), (), s32[]{:S(2)}) async-start(), calls=%async_computation.24 | async-start | bytes 491520
  1071.6 256.9 %reduce-scatter.39.cloned.1.call-start = ((), (), s32[]{:S(2)}) async-start(), calls=%async_computation.23 | async-start | bytes 491520
  1073.6 270.8 %reduce-scatter.37.cloned.1.call-start = ((), (), s32[]{:S(2)}) async-start(), calls=%async_computation.22 | async-start | bytes 491520
  1075.9 300.4 %reduce-scatter.35.cloned.1.call-start = ((), (), s32[]{:S(2)}) async-start(), calls=%async_computation.20 | async-start | bytes 1474560 | tf_op jit(solution)/shard_map/reduce_scatter | solution.py:276
  1134.7 273.5 %reduce-scatter.31.cloned.1.call-start = ((), (), s32[]{:S(2)}) async-start(), calls=%async_computation.18 | async-start | bytes 1474560 | tf_op jit(solution)/shard_map/reduce_scatter | solution.py:275
  1234.8 17.6 %copy-start.129 = (f32[768]{0:T(1024)S(1)}, f32[768]{0:T(1024)}, u32[]{:S(2)}) copy-start(f32[768]{0:T(1024)} %get-tuple-element.378) | copy-start | bytes 9220
  1234.8 17.6 %copy-start.131 = (f32[768]{0:T(1024)S(1)}, f32[768]{0:T(1024)}, u32[]{:S(2)}) copy-start(f32[768]{0:T(1024)} %get-tuple-element.380) | copy-start | bytes 9220
  1311.1 97.1 %copy-start.1 = (f32[768,768]{1,0:T(8,128)S(1)}, f32[768,768]{1,0:T(8,128)}, u32[]{:S(2)}) copy-start(f32[768,768]{1,0:T(8,128)} %param.31) | copy-start | bytes 7077892
  (136 other events, 614.2 us)
Sparse Core Ops, SparseCore 0:
  76.2 66.5 all-reduce.10
  160.5 118.9 all-gather.4
  604.1 65.4 all-reduce.6
  685.6 80.4 all-reduce.8
  768.3 36.1 reduce-scatter.26
  903.0 40.6 reduce-scatter.24
  955.3 40.6 reduce-scatter.22
  998.3 35.3 reduce-scatter.20
  1036.0 98.6 reduce-scatter.32
  1136.9 97.8 reduce-scatter.28
  1238.1 22.8 reduce-scatter.42
  1264.3 24.3 reduce-scatter.40
  1292.1 24.5 reduce-scatter.38
  1319.9 24.4 reduce-scatter.36
  1347.7 28.5 reduce-scatter.34
  1379.6 28.5 reduce-scatter.30
where the time goes:
time: 1420 us
  matrix products  775 us (55%)
  waiting for transfers between devices  287 us (20%)
  other arithmetic  136 us (10%)
  local copies, waits for them, and re-layouts  99.2 us (7%)
  blocking collectives  92.4 us (7%)
  between operations  17 us (1%)
    dot_general x36, matrix products, newton(): jnp.einsum('...ij,...jk->...ik', product, nested, precision=highest)  93.4 us
    reduce_scatter x1, waiting for transfers between devices, on_device(): lax.psum_scatter(grad_w_up, 'seq', scatter_dimension=1, tiled=True)  71.2 us
    psum x2, waiting for transfers between devices, on_device(): grad_mixed, part_land_key = lax.psum((part_mixed, part_land_key), 'seq')  56.9 us
    reduce_sum x5, other arithmetic, on_device(): jnp.sum(grad_pre * padded[:, tap_index:tap_index + span], axis=(0, 1, 3))  56.7 us
    dot_general x1, matrix products, on_device(): jnp.einsum('ihjt,ihje->ithe', kernel_three, grad_context, precision=highest)  52.8 us
    dot_general x1, matrix products, on_device(): jnp.einsum('ihjt,ihje->ithe', kernel_one, mixed_context, precision=highest)  51.4 us
    dot_general x18, matrix products, newton(): jnp.einsum('...ij,...jk->...ik', approx, nested, precision=highest)  48 us
    dot_general x18, matrix products, newton(): jnp.einsum('...ij,...jk->...ik', kernel, approx, precision=highest)  46.9 us
  transfers between devices with their start and end apart: 20, of which 8 were waited for; matrix products, arithmetic and copies ran while one was open for 43% of the time, Pallas kernels for 0%

commit v1 on v0

v1 whole, which is shorter than its diff:
```python
import functools

import jax
import jax.numpy as jnp
from jax import lax
from jax.experimental import pallas as pl
from jax.experimental.pallas import tpu as pltpu
from jax.sharding import PartitionSpec as P

MARKS = 64
NEWTON = 6
PAIR = 128
HIGH = lax.Precision.HIGH
epsilon = 1e-05
f32 = jnp.float32
bf16 = jnp.bfloat16
VM = pltpu.VMEM
LIMIT = 66 * 1024 * 1024


def split(x):
    hi = x.astype(bf16)
    return hi, (x - hi.astype(f32)).astype(bf16)


def dg(a, b, ca, cb):
    return lax.dot_general(a, b, (((ca,), (cb,)), ((), ())), preferred_element_type=f32)


def dots(a, b, ca, cb):
    return dg(a[0], b[0], ca, cb) + dg(a[0], b[1], ca, cb) + dg(a[1], b[0], ca, cb)


def dot3(a, b, ca=1, cb=0):
    return dots(split(a), split(b), ca, cb)


def lane_low(shape):
    return lax.broadcasted_iota(jnp.int32, shape, len(shape) - 1) < PAIR // 2


def spread(compact):
    low = lane_low(compact.shape)
    zero = jnp.zeros_like(compact)
    return jnp.concatenate([jnp.where(low, compact, zero), jnp.where(low, zero, compact)], axis=0)


def compacted(block):
    half = block.shape[0] // 2
    return jnp.where(lane_low((half, block.shape[1])), block[:half], block[half:])


def row_of(column):
    return jnp.transpose(jnp.broadcast_to(column, (PAIR, PAIR)))[0:1, :]


def column_of(row):
    return jnp.transpose(jnp.broadcast_to(row, (PAIR, PAIR)))


def diagonal_mask():
    rows = lax.broadcasted_iota(jnp.int32, (PAIR, PAIR), 0) < PAIR // 2
    return rows == lane_low((PAIR, PAIR))


def block_sum(x):
    halves = x.reshape(2, x.shape[0] // 2, x.shape[1])
    total = jnp.sum(halves, axis=1, keepdims=True)
    return jnp.broadcast_to(total, halves.shape).reshape(x.shape)


def block_max(x):
    halves = x.reshape(2, x.shape[0] // 2, x.shape[1])
    total = jnp.max(halves, axis=1, keepdims=True)
    return jnp.broadcast_to(total, halves.shape).reshape(x.shape)


def params(**more):
    return pltpu.CompilerParams(vmem_limit_bytes=LIMIT, **more)


def whole(shape):
    return pl.BlockSpec(shape, lambda *_: (0,) * len(shape))


def per_item(shape):
    return pl.BlockSpec((1,) + shape, lambda i, *_: (i,) + (0,) * len(shape))


def land_item(ref, item, me, into):
    rows = ref.shape[1]
    count = MARKS // rows
    for part in range(count):
        slot = jnp.bitwise_xor(item * count + part, me)
        into[part * rows : (part + 1) * rows, :] = ref[slot]


def scores_kernel(n, per, pairs, me_ref, q_ref, k_ref, v_ref, lq_ref, lk_ref, use_ref, *rest):
    k1_ref, w3_ref, top_ref = rest[:3]
    outs = rest[3 : 3 + n]
    lq_s, lk_s, chunk = rest[3 + n :]
    item = pl.program_id(0)
    me = me_ref[0]
    stats = per * MARKS

    @pl.when(item == 0)
    def _():
        chunk[...] = jnp.zeros_like(chunk)

    land_item(lq_ref, item, me, lq_s)
    land_item(lk_ref, item, me, lk_s)
    use = use_ref[0]
    for p in range(pairs):
        lanes = slice(p * PAIR, (p + 1) * PAIR)
        q = q_ref[0, :, lanes]
        s1 = dot3(spread(lk_s[:, lanes]), q, 1, 1)
        e1 = jnp.exp(s1 - block_max(s1))
        k1_ref[0, lanes, :] = e1 / block_sum(e1)
        s3 = dot3(spread(lq_s[:, lanes]), k_ref[0, :, lanes], 1, 1)
        masked = jnp.where(use > 0, s3, -1e30)
        top = jnp.max(masked, axis=1, keepdims=True)
        w3 = jnp.exp(masked - top) * use
        w3_ref[0, lanes, :] = w3
        total = jnp.sum(w3, axis=1, keepdims=True)
        weighted = compacted(dot3(w3, v_ref[0, :, lanes]))
        top_row = row_of(top)
        top_ref[0, p : p + 1, :] = top_row
        g = item * pairs + p
        owner, place = g // per, g % per
        chunk[owner, pl.ds(pl.multiple_of(place * MARKS, MARKS), MARKS), :] = weighted
        chunk[owner, pl.ds(stats + 2 * place, 1), :] = top_row
        chunk[owner, pl.ds(stats + 2 * place + 1, 1), :] = row_of(total)

    @pl.when(item == pl.num_programs(0) - 1)
    def _():
        for k in range(n):
            outs[k][...] = chunk[jnp.bitwise_xor(me, k)]


def scores_call(me, q, k, v, lq, lk, use_row, n, per, pairs, chunk_rows):
    items, span, width = q.shape
    out_shape = [
        jax.ShapeDtypeStruct((items, width, span), f32),
        jax.ShapeDtypeStruct((items, width, span), f32),
        jax.ShapeDtypeStruct((items, 8, PAIR), f32),
    ] + [jax.ShapeDtypeStruct((chunk_rows, PAIR), f32)] * n
    return pl.pallas_call(
        functools.partial(scores_kernel, n, per, pairs),
        out_shape=out_shape,
        grid_spec=pltpu.PrefetchScalarGridSpec(
            num_scalar_prefetch=1,
            grid=(items,),
            in_specs=[per_item((span, width))] * 3
            + [whole(lq.shape), whole(lk.shape), per_item((1, span))],
            out_specs=[per_item((width, span))] * 2
            + [per_item((8, PAIR))]
            + [whole((chunk_rows, PAIR))] * n,
            scratch_shapes=[
                VM((MARKS, width), f32),
                VM((MARKS, width), f32),
                VM((n, chunk_rows, PAIR), f32),
            ],
        ),
        compiler_params=params(),
        name="scores",
    )(me, q, k, v, lq, lk, use_row)


def owned_land(per, pairs, items, me, ref, into):
    rows = ref.shape[1]
    count = MARKS // rows
    for place in range(per):
        g = jnp.minimum(me * per + place, items * pairs - 1)
        item, p = g // pairs, g % pairs
        lanes = pl.ds(pl.multiple_of(p * PAIR, PAIR), PAIR)
        for part in range(count):
            slot = jnp.bitwise_xor(item * count + part, me)
            into[place, part * rows : (part + 1) * rows, :] = ref[slot, :, lanes]


def newton_step(a, z, eye):
    pr = dot3(a, z)
    n1 = 7.0 * eye - pr
    n2 = 15.0 * eye - dot3(pr, n1)
    n3 = 13.0 * eye - dot3(pr, n2)
    return pr, n1, n2, n3


def unit():
    rows = lax.broadcasted_iota(jnp.int32, (PAIR, PAIR), 0)
    return (rows == lax.broadcasted_iota(jnp.int32, (PAIR, PAIR), 1)).astype(f32)


def head_total(x):
    return block_sum(jnp.sum(x, axis=1, keepdims=True))


def newton_kernel(per, pairs, items, me_ref, lq_ref, lk_ref, a_ref, z_ref, lqo_ref, lko_ref):
    me = me_ref[0]
    owned_land(per, pairs, items, me, lq_ref, lqo_ref)
    owned_land(per, pairs, items, me, lk_ref, lko_ref)
    diagonal = diagonal_mask()
    eye = unit()
    for place in range(per):
        s2 = dot3(spread(lqo_ref[place]), spread(lko_ref[place]), 1, 1)
        s2 = jnp.where(diagonal, s2, -1e30)
        e2 = jnp.exp(s2 - jnp.max(s2, axis=1, keepdims=True))
        e2 = jnp.where(diagonal, e2, 0.0)
        a = e2 / jnp.sum(e2, axis=1, keepdims=True)
        a_ref[place] = a
        z_ref[0, place] = jnp.transpose(a) / head_total(a * a)

    def lap(step, _):
        for place in range(per):
            z = z_ref[step, place]
            _, _, _, n3 = newton_step(a_ref[place], z, eye)
            z_ref[step + 1, place] = 0.25 * dot3(z, n3)
        return 0

    lax.fori_loop(0, NEWTON, lap, 0)


def newton_call(me, lq, lk, per, pairs, items):
    small = jax.ShapeDtypeStruct((per, MARKS, PAIR), f32)
    square = jax.ShapeDtypeStruct((per, PAIR, PAIR), f32)
    steps = jax.ShapeDtypeStruct((NEWTON + 1, per, PAIR, PAIR), f32)
    return pl.pallas_call(
        functools.partial(newton_kernel, per, pairs, items),
        out_shape=[square, steps, small, small],
        in_specs=[
            pl.BlockSpec(memory_space=pltpu.SMEM),
            pl.BlockSpec(memory_space=VM),
            pl.BlockSpec(memory_space=VM),
        ],
        out_specs=[pl.BlockSpec(memory_space=VM)] * 4,
        compiler_params=params(),
        name="newton",
    )(me, lq, lk)


def context_kernel(n, per, *refs):
    chunks = refs[:n]
    z_ref, ctx_ref, out_ref = refs[n:]
    stats = per * MARKS
    out_ref[...] = jnp.zeros_like(out_ref)
    for place in range(per):
        tops = [c[stats + 2 * place : stats + 2 * place + 1, :] for c in chunks]
        largest = functools.reduce(jnp.maximum, tops)
        total = jnp.zeros_like(largest)
        weighted = jnp.zeros((MARKS, PAIR), f32)
        for k in range(n):
            scale = jnp.exp(tops[k] - largest)
            total = total + scale * chunks[k][stats + 2 * place + 1 : stats + 2 * place + 2, :]
            scales = compacted(column_of(scale))
            weighted = weighted + scales * chunks[k][place * MARKS : (place + 1) * MARKS, :]
        context = weighted / compacted(column_of(total))
        ctx_ref[place] = context
        mixed = dot3(z_ref[NEWTON, place], spread(context))
        out_ref[place * MARKS : (place + 1) * MARKS, :] = compacted(mixed)
        out_ref[stats + 2 * place : stats + 2 * place + 1, :] = largest
        out_ref[stats + 2 * place + 1 : stats + 2 * place + 2, :] = total


def context_call(chunks, z, per):
    rows = chunks[0].shape[0]
    n = len(chunks)
    return pl.pallas_call(
        functools.partial(context_kernel, n, per),
        out_shape=[
            jax.ShapeDtypeStruct((per, MARKS, PAIR), f32),
            jax.ShapeDtypeStruct((rows, PAIR), f32),
        ],
        in_specs=[pl.BlockSpec(memory_space=VM)] * (n + 1),
        out_specs=[pl.BlockSpec(memory_space=VM)] * 2,
        compiler_params=params(),
        name="context",
    )(*chunks, z)


def toeplitz(taps_row, rows):
    wide = jnp.broadcast_to(taps_row, (rows, 2 * PAIR))
    return pltpu.roll(wide, 0, 1, stride=1, stride_axis=0)


def keep_taps(taps_ref, into, heads):
    for h in range(heads):
        hi, lo = split(toeplitz(taps_ref[h : h + 1, :], PAIR))
        into[0, h] = hi
        into[1, h] = lo


def keep_window(win, left, middle, right, margin, span):
    for rows, part in (
        (slice(0, margin), left),
        (slice(margin, margin + span), middle),
        (slice(margin + span, 2 * margin + span), right),
    ):
        hi, lo = split(part)
        win[0, rows, :] = hi
        win[1, rows, :] = lo


def convolve(taps, win, p, block, window):
    lanes = slice(p * PAIR, (p + 1) * PAIR)
    rows = slice(block * PAIR, block * PAIR + window)
    v = (win[0, rows, lanes], win[1, rows, lanes])
    halves = []
    for h in (2 * p, 2 * p + 1):
        t = (taps[0, h, :, :window], taps[1, h, :, :window])
        halves.append(dots(t, v, 1, 0))
    return jnp.where(lane_low((PAIR, PAIR)), halves[0], halves[1])


def slot_of(g, per, me):
    return jnp.bitwise_xor(g // per, me), g % per


def mix_kernel(n, per, pairs, margin, me_ref, *refs):
    blocks = refs[:n]
    k1_ref, v_ref, use_ref, left_ref, right_ref, taps_ref, out_ref, held, taps, win = refs[n:]
    item = pl.program_id(0)
    me = me_ref[0]
    span = v_ref.shape[1]
    window = PAIR + 2 * margin

    @pl.when(item == 0)
    def _():
        for k in range(n):
            held[k] = blocks[k][...]
        keep_taps(taps_ref, taps, 2 * pairs)

    keep_window(win, left_ref[0], v_ref[0] * use_ref[0], right_ref[0], margin, span)
    for p in range(pairs):
        lanes = slice(p * PAIR, (p + 1) * PAIR)
        slot, place = slot_of(item * pairs + p, per, me)
        mixed = held[slot, pl.ds(pl.multiple_of(place * MARKS, MARKS), MARKS), :]
        nystrom = dot3(k1_ref[0, lanes, :], spread(mixed), 0, 0)
        for block in range(span // PAIR):
            rows = slice(block * PAIR, (block + 1) * PAIR)
            out_ref[0, rows, lanes] = nystrom[rows] + convolve(taps, win, p, block, window)


def mix_call(me, blocks, k1, v, use_col, left, right, taps, per, pairs, margin):
    items, span, width = v.shape
    n = len(blocks)
    rows = blocks[0].shape[0]
    return pl.pallas_call(
        functools.partial(mix_kernel, n, per, pairs, margin),
        out_shape=jax.ShapeDtypeStruct((items, span, width), f32),
        grid_spec=pltpu.PrefetchScalarGridSpec(
            num_scalar_prefetch=1,
            grid=(items,),
            in_specs=[whole((rows, PAIR))] * n
            + [per_item((width, span)), per_item((span, width)), per_item((span, 1))]
            + [per_item((margin, width))] * 2
            + [whole(taps.shape)],
            out_specs=per_item((span, width)),
            scratch_shapes=[
                VM((n, rows, PAIR), f32),
                VM((2, 2 * pairs, PAIR, 2 * PAIR), bf16),
                VM((2, span + 2 * margin, width), bf16),
            ],
        ),
        compiler_params=params(),
        name="mix",
    )(me, *blocks, k1, v, use_col, left, right, taps)


def erf(x):
    x = jnp.clip(x, -3.832506856900711, 3.832506856900711)
    s = x * x
    a = 0.00022905065861350646
    for c in (0.0034082910107109506, 0.050955695062380861, 0.18520832239976145, 1.128379143519084):
        a = a * s + c
    b = -1.1791602954361697e-7
    for c in (
        0.000023547966471313185,
        0.0010179625278914885,
        0.014070470171167667,
        0.11098505178285362,
        0.49746925110067538,
        1.0,
    ):
        b = b * s + c
    return x * a / b


def normalize(x):
    center = x - jnp.mean(x, axis=-1, keepdims=True)
    inv_root = lax.rsqrt(jnp.mean(center * center, axis=-1, keepdims=True) + epsilon)
    return center * inv_root, inv_root


def norm_back(grad, scaled, inv_root):
    first = jnp.mean(grad, axis=-1, keepdims=True)
    second = jnp.mean(grad * scaled, axis=-1, keepdims=True)
    return inv_root * (grad - first - scaled * second)


def rows_kernel(
    ff_tile,
    x_ref,
    tok_ref,
    cot_ref,
    wo_h,
    wo_l,
    wu_h,
    wu_l,
    wd_h,
    wd_l,
    vec_ref,
    bup_ref,
    out_ref,
    act_ref,
    u_ref,
    r2_ref,
    h1_ref,
    r1_ref,
    og_ref,
    sums_ref,
    bsum_ref,
    slope,
):
    @pl.when(pl.program_id(0) == 0)
    def _():
        sums_ref[...] = jnp.zeros_like(sums_ref)
        bsum_ref[...] = jnp.zeros_like(bsum_ref)

    b_out, gain_one, shift_one = vec_ref[0:1, :], vec_ref[1:2, :], vec_ref[2:3, :]
    b_down, gain_two, shift_two = vec_ref[3:4, :], vec_ref[4:5, :], vec_ref[5:6, :]
    wo = (wo_h[...], wo_l[...])
    attention = dots(split(x_ref[...]), wo, 1, 0) + b_out
    scaled_one, root_one = normalize(tok_ref[...] + attention)
    hidden = scaled_one * gain_one + shift_one
    h1_ref[...] = hidden
    hs = split(hidden)
    ff = wu_h.shape[1]
    tiles = [slice(c, c + ff_tile) for c in range(0, ff, ff_tile)]
    down = b_down
    for c in tiles:
        pre = dots(hs, (wu_h[:, c], wu_l[:, c]), 1, 0) + bup_ref[:, c]
        phi = 0.5 + 0.5 * erf(pre * 0.7071067811865476)
        slope[:, c] = phi + pre * (0.3989422804014327 * jnp.exp(-0.5 * pre * pre))
        act = pre * phi
        act_ref[:, c] = act
        down = down + dots(split(act), (wd_h[c, :], wd_l[c, :]), 1, 0)
    scaled_two, root_two = normalize(hidden + down)
    out_ref[...] = scaled_two * gain_two + shift_two
    cot = cot_ref[...]
    r2 = norm_back(cot * gain_two, scaled_two, root_two)
    r2_ref[...] = r2
    rs = split(r2)
    grad_hidden = r2
    for c in tiles:
        u = dots(rs, (wd_h[c, :], wd_l[c, :]), 1, 1) * slope[:, c]
        u_ref[:, c] = u
        bsum_ref[:, c] += jnp.sum(u, axis=0, keepdims=True)
        grad_hidden = grad_hidden + dots(split(u), (wu_h[:, c], wu_l[:, c]), 1, 1)
    r1 = norm_back(grad_hidden * gain_one, scaled_one, root_one)
    r1_ref[...] = r1
    og_ref[...] = dots(split(r1), wo, 1, 1)
    for row, value in enumerate(
        (cot * scaled_two, cot, r2, grad_hidden * scaled_one, grad_hidden, r1)
    ):
        sums_ref[row : row + 1, :] += jnp.sum(value, axis=0, keepdims=True)


def rows_call(x, tokens, cotangent, wo, wu, wd, vectors, b_up):
    rows, width = x.shape
    ff = wu[0].shape[1]
    tile = 256
    ff_tile = 768
    wide = pl.BlockSpec((tile, width), lambda i: (i, 0))
    hidden = pl.BlockSpec((tile, ff), lambda i: (i, 0))

    def fixed(a):
        return pl.BlockSpec(a.shape, lambda i: (0, 0), pipeline_mode=pl.Buffered(1))

    narrow = jax.ShapeDtypeStruct((rows, width), f32)
    broad = jax.ShapeDtypeStruct((rows, ff), f32)
    return pl.pallas_call(
        functools.partial(rows_kernel, ff_tile),
        out_shape=[
            narrow,
            broad,
            broad,
            narrow,
            narrow,
            narrow,
            narrow,
            jax.ShapeDtypeStruct((8, width), f32),
            jax.ShapeDtypeStruct((1, ff), f32),
        ],
        grid=(rows // tile,),
        in_specs=[wide] * 3
        + [fixed(a) for a in (*wo, *wu, *wd)]
        + [fixed(vectors), fixed(b_up)],
        out_specs=[wide, hidden, hidden, wide, wide, wide, wide]
        + [pl.BlockSpec((8, width), lambda i: (0, 0)), pl.BlockSpec((1, ff), lambda i: (0, 0))],
        scratch_shapes=[VM((tile, ff), f32)],
        compiler_params=params(),
        name="rows",
    )(x, tokens, cotangent, *wo, *wu, *wd, vectors, b_up)


def one_back_kernel(n, per, pairs, me_ref, *refs):
    blocks = refs[:n]
    k1_ref, og_ref, q_ref, lk_ref = refs[n : n + 4]
    gq_ref = refs[n + 4]
    outs = refs[n + 5 : 2 * n + 5]
    held, lk_s, chunk = refs[2 * n + 5 :]
    item = pl.program_id(0)
    me = me_ref[0]

    @pl.when(item == 0)
    def _():
        chunk[...] = jnp.zeros_like(chunk)
        for k in range(n):
            held[k] = blocks[k][...]

    land_item(lk_ref, item, me, lk_s)
    for p in range(pairs):
        lanes = slice(p * PAIR, (p + 1) * PAIR)
        g = item * pairs + p
        slot, place = slot_of(g, per, me)
        mixed = spread(held[slot, pl.ds(pl.multiple_of(place * MARKS, MARKS), MARKS), :])
        k1 = k1_ref[0, lanes, :]
        og = split(og_ref[0, :, lanes])
        part_mixed = compacted(dots(split(k1), og, 1, 0))
        grad = dots(split(mixed), og, 1, 1)
        scores = k1 * (grad - block_sum(k1 * grad))
        ss = split(scores)
        gq_ref[0, :, lanes] = dots(ss, split(spread(lk_s[:, lanes])), 0, 0)
        part_key = compacted(dots(ss, split(q_ref[0, :, lanes]), 1, 0))
        owner = g // per
        chunk[owner, pl.ds(pl.multiple_of(place * 2 * MARKS, 2 * MARKS), MARKS), :] = part_mixed
        chunk[owner, pl.ds(pl.multiple_of(place * 2 * MARKS + MARKS, MARKS), MARKS), :] = part_key

    @pl.when(item == pl.num_programs(0) - 1)
    def _():
        for k in range(n):
            outs[k][...] = chunk[jnp.bitwise_xor(me, k)]


def one_back_call(me, blocks, k1, og, q, lk, per, pairs):
    items, span, width = q.shape
    n = len(blocks)
    rows = blocks[0].shape[0]
    out_rows = 2 * per * MARKS
    return pl.pallas_call(
        functools.partial(one_back_kernel, n, per, pairs),
        out_shape=[jax.ShapeDtypeStruct((items, span, width), f32)]
        + [jax.ShapeDtypeStruct((out_rows, PAIR), f32)] * n,
        grid_spec=pltpu.PrefetchScalarGridSpec(
            num_scalar_prefetch=1,
            grid=(items,),
            in_specs=[whole((rows, PAIR))] * n
            + [per_item((width, span)), per_item((span, width)), per_item((span, width))]
            + [whole(lk.shape)],
            out_specs=[per_item((span, width))] + [whole((out_rows, PAIR))] * n,
            scratch_shapes=[
                VM((n, rows, PAIR), f32),
                VM((MARKS, width), f32),
                VM((n, out_rows, PAIR), f32),
            ],
        ),
        compiler_params=params(),
        name="one_back",
    )(me, *blocks, k1, og, q, lk)


def conv_back_kernel(pairs, margin, og_ref, gl_ref, gr_ref, v_ref, vl_ref, vr_ref, use_ref, taps_ref, *refs):
    gv_ref, gtaps_ref, taps, gwin, vwin, acc = refs
    item = pl.program_id(0)
    span = v_ref.shape[1]
    window = PAIR + 2 * margin

    @pl.when(item == 0)
    def _():
        keep_taps(taps_ref, taps, 2 * pairs)
        acc[...] = jnp.zeros_like(acc)

    use = use_ref[0]
    keep_window(gwin, gl_ref[0], og_ref[0], gr_ref[0], margin, span)
    keep_window(vwin, vl_ref[0], v_ref[0] * use, vr_ref[0], margin, span)
    for p in range(pairs):
        lanes = slice(p * PAIR, (p + 1) * PAIR)
        for block in range(span // PAIR):
            rows = slice(block * PAIR, (block + 1) * PAIR)
            gv_ref[0, rows, lanes] = convolve(taps, gwin, p, block, window) * use[rows]
            inner = slice(margin + block * PAIR, margin + (block + 1) * PAIR)
            outer = slice(block * PAIR, block * PAIR + window)
            v = (vwin[0, outer, lanes], vwin[1, outer, lanes])
            low = lane_low((PAIR, PAIR))
            hi, lo = gwin[0, inner, lanes], gwin[1, inner, lanes]
            zero = jnp.zeros_like(hi)
            acc[2 * p] += dots((jnp.where(low, hi, zero), jnp.where(low, lo, zero)), v, 1, 1)
            acc[2 * p + 1] += dots((jnp.where(low, zero, hi), jnp.where(low, zero, lo)), v, 1, 1)

    @pl.when(item == pl.num_programs(0) - 1)
    def _():
        rows = lax.broadcasted_iota(jnp.int32, (PAIR, PAIR), 0)
        flip = (rows + lax.broadcasted_iota(jnp.int32, (PAIR, PAIR), 1) == PAIR - 1).astype(bf16)
        for h in range(2 * pairs):
            c = acc[h]
            c = jnp.concatenate([c, jnp.zeros((PAIR, 2 * PAIR - window), f32)], axis=1)
            hi = c.astype(bf16)
            rest = c - hi.astype(f32)
            mid = rest.astype(bf16)
            low = (rest - mid.astype(f32)).astype(bf16)
            c = dg(flip, hi, 1, 0) + dg(flip, mid, 1, 0) + dg(flip, low, 1, 0)
            c = pltpu.roll(c, 0, 1, stride=1, stride_axis=0)
            gtaps_ref[h : h + 1, :] = jnp.sum(c, axis=0, keepdims=True)


def conv_back_call(og, gleft, gright, v, vleft, vright, use_col, taps, pairs, margin):
    items, span, width = v.shape
    window = PAIR + 2 * margin
    wide, edge = per_item((span, width)), per_item((margin, width))
    rows = -(-2 * pairs // 8) * 8
    return pl.pallas_call(
        functools.partial(conv_back_kernel, pairs, margin),
        out_shape=[
            jax.ShapeDtypeStruct((items, span, width), f32),
            jax.ShapeDtypeStruct((rows, 2 * PAIR), f32),
        ],
        grid=(items,),
        in_specs=[wide, edge, edge, wide, edge, edge, per_item((span, 1)), whole(taps.shape)],
        out_specs=[wide, whole((rows, 2 * PAIR))],
        scratch_shapes=[
            VM((2, 2 * pairs, PAIR, 2 * PAIR), bf16),
            VM((2, span + 2 * margin, width), bf16),
            VM((2, span + 2 * margin, width), bf16),
            VM((2 * pairs, PAIR, window), f32),
        ],
        compiler_params=params(),
        name="conv_back",
    )(og, gleft, gright, v, vleft, vright, use_col, taps)


def context_back_kernel(n, per, *refs):
    chunks = refs[:n]
    z_ref, ctx_ref, out_ref, gm_ref, key_ref = refs[n:]
    stats = per * MARKS
    out_ref[...] = jnp.zeros_like(out_ref)
    for place in range(per):
        rows = slice(place * 2 * MARKS, place * 2 * MARKS + MARKS)
        more = slice(place * 2 * MARKS + MARKS, (place + 1) * 2 * MARKS)
        mixed = sum(c[rows, :] for c in chunks)
        gm_ref[place] = mixed
        key_ref[place] = sum(c[more, :] for c in chunks)
        grad = dot3(jnp.transpose(z_ref[NEWTON, place]), spread(mixed))
        out_ref[place * MARKS : (place + 1) * MARKS, :] = compacted(grad)
        dot = jnp.sum(grad * spread(ctx_ref[place]), axis=1, keepdims=True)
        out_ref[stats + place : stats + place + 1, :] = row_of(dot)


def context_back_call(chunks, z, ctx, per, rows):
    n = len(chunks)
    small = jax.ShapeDtypeStruct((per, MARKS, PAIR), f32)
    return pl.pallas_call(
        functools.partial(context_back_kernel, n, per),
        out_shape=[jax.ShapeDtypeStruct((rows, PAIR), f32), small, small],
        in_specs=[pl.BlockSpec(memory_space=VM)] * (n + 2),
        out_specs=[pl.BlockSpec(memory_space=VM)] * 3,
        compiler_params=params(),
        name="context_back",
    )(*chunks, z, ctx)


def newton_back_kernel(per, gm_ref, key_ref, ctx_ref, a_ref, z_ref, lq_ref, lk_ref, gq_ref, gk_ref, gz, ga):
    diagonal = diagonal_mask()
    eye = unit()
    for place in range(per):
        start = dot3(spread(gm_ref[place]), spread(ctx_ref[place]), 1, 1)
        gz[place] = jnp.where(diagonal, start, 0.0)
        ga[place] = jnp.zeros((PAIR, PAIR), f32)

    def lap(back, _):
        step = NEWTON - 1 - back
        for place in range(per):
            a, z, g = a_ref[place], z_ref[step, place], 0.25 * gz[place]
            pr, n1, n2, n3 = newton_step(a, z, eye)
            back_three = dot3(jnp.transpose(z), g)
            turned = jnp.transpose(pr)
            back_two = -dot3(turned, back_three)
            back_one = -dot3(turned, back_two)
            grad = -dot3(back_three, n2, 1, 1) - dot3(back_two, n1, 1, 1) - back_one
            ga[place] += dot3(grad, z, 1, 1)
            gz[place] = dot3(g, n3, 1, 1) + dot3(jnp.transpose(a), grad)
        return 0

    lax.fori_loop(0, NEWTON, lap, 0)
    for place in range(per):
        a, g = a_ref[place], jnp.transpose(gz[place])
        norm = head_total(a * a)
        slope = -head_total(g * a) / (norm * norm)
        grad = ga[place] + g / norm + 2.0 * slope * a
        scores = a * (grad - jnp.sum(a * grad, axis=1, keepdims=True))
        gq_ref[place] = compacted(dot3(scores, spread(lk_ref[place])))
        gk_ref[place] = key_ref[place] + compacted(
            dot3(jnp.transpose(scores), spread(lq_ref[place]))
        )


def newton_back_call(gm, key, ctx, a, z, lq, lk):
    per = gm.shape[0]
    small = jax.ShapeDtypeStruct(gm.shape, f32)
    return pl.pallas_call(
        functools.partial(newton_back_kernel, per),
        out_shape=[small, small],
        in_specs=[pl.BlockSpec(memory_space=VM)] * 7,
        out_specs=[pl.BlockSpec(memory_space=VM)] * 2,
        scratch_shapes=[VM((per, PAIR, PAIR), f32)] * 2,
        compiler_params=params(),
        name="newton_back",
    )(gm, key, ctx, a, z, lq, lk)


def three_back_kernel(n, per, pairs, me_ref, *refs):
    grads, blocks = refs[:n], refs[n : 2 * n]
    w3_ref, top_ref, v_ref, k_ref, gvc_ref, lq_ref = refs[2 * n : 2 * n + 6]
    gv_ref, gk_ref = refs[2 * n + 6 : 2 * n + 8]
    outs = refs[2 * n + 8 : 3 * n + 8]
    held, stat, lq_s, chunk = refs[3 * n + 8 :]
    item = pl.program_id(0)
    me = me_ref[0]
    stats = per * MARKS

    @pl.when(item == 0)
    def _():
        chunk[...] = jnp.zeros_like(chunk)
        for k in range(n):
            held[k] = grads[k][...]
            stat[k] = blocks[k][stats:, :]

    land_item(lq_ref, item, me, lq_s)
    for p in range(pairs):
        lanes = slice(p * PAIR, (p + 1) * PAIR)
        g = item * pairs + p
        slot, place = slot_of(g, per, me)
        grad = split(spread(held[slot, pl.ds(pl.multiple_of(place * MARKS, MARKS), MARKS), :]))
        row_dot = column_of(held[slot, pl.ds(stats + place, 1), :])
        largest = stat[slot, pl.ds(2 * place, 1), :]
        total = stat[slot, pl.ds(2 * place + 1, 1), :]
        scale = column_of(jnp.exp(top_ref[0, p : p + 1, :] - largest) / total)
        k3 = w3_ref[0, lanes, :] * scale[:, 0:1]
        gk3 = dots(grad, split(v_ref[0, :, lanes]), 1, 1)
        scores = split(k3 * (gk3 - row_dot[:, 0:1]))
        gv_ref[0, :, lanes] = gvc_ref[0, :, lanes] + dots(split(k3), grad, 0, 0)
        gk_ref[0, :, lanes] = dots(scores, split(spread(lq_s[:, lanes])), 0, 0)
        part = compacted(dots(scores, split(k_ref[0, :, lanes]), 1, 0))
        chunk[g // per, pl.ds(pl.multiple_of(place * MARKS, MARKS), MARKS), :] = part

    @pl.when(item == pl.num_programs(0) - 1)
    def _():
        for k in range(n):
            outs[k][...] = chunk[jnp.bitwise_xor(me, k)]


def three_back_call(me, grads, blocks, w3, top, v, k, gv_conv, lq, per, pairs):
    items, span, width = v.shape
    n = len(blocks)
    rows = blocks[0].shape[0]
    stats = per * MARKS
    wide = per_item((span, width))
    shape = jax.ShapeDtypeStruct((items, span, width), f32)
    return pl.pallas_call(
        functools.partial(three_back_kernel, n, per, pairs),
        out_shape=[shape, shape] + [jax.ShapeDtypeStruct((stats, PAIR), f32)] * n,
        grid_spec=pltpu.PrefetchScalarGridSpec(
            num_scalar_prefetch=1,
            grid=(items,),
            in_specs=[whole((rows, PAIR))] * (2 * n)
            + [per_item((width, span)), per_item((8, PAIR)), wide, wide, wide, whole(lq.shape)],
            out_specs=[wide, wide] + [whole((stats, PAIR))] * n,
            scratch_shapes=[
                VM((n, rows, PAIR), f32),
                VM((n, rows - stats, PAIR), f32),
                VM((MARKS, width), f32),
                VM((n, stats, PAIR), f32),
            ],
        ),
        compiler_params=params(),
        name="three_back",
    )(me, *grads, *blocks, w3, top, v, k, gv_conv, lq)


def land_back_kernel(n, per, pairs, factor, me_ref, *refs):
    blocks = refs[:n]
    gq_ref, gk_ref, gv_ref, mem_ref, inv_ref = refs[n : n + 5]
    oq_ref, ok_ref, sums_ref, held, inv_s = refs[n + 5 :]
    item = pl.program_id(0)
    me = me_ref[0]
    half = per * MARKS

    @pl.when(item == 0)
    def _():
        sums_ref[...] = jnp.zeros_like(sums_ref)
        for k in range(n):
            held[k] = blocks[k][...]

    land_item(inv_ref, item, me, inv_s)
    member = mem_ref[0].astype(bf16)
    inv = inv_s[...]
    for p in range(pairs):
        lanes = slice(p * PAIR, (p + 1) * PAIR)
        slot, place = slot_of(item * pairs + p, per, me)
        for ref, out, base in ((gq_ref, oq_ref, 0), (gk_ref, ok_ref, half)):
            grad = held[slot, pl.ds(pl.multiple_of(base + place * MARKS, MARKS), MARKS), :]
            hi, lo = split(grad * inv)
            landed = dg(member, hi, 0, 0) + dg(member, lo, 0, 0)
            out[0, :, lanes] = (ref[0, :, lanes] + landed) * factor
        sums_ref[0:1, lanes] += jnp.sum(oq_ref[0, :, lanes], axis=0, keepdims=True)
        sums_ref[1:2, lanes] += jnp.sum(gv_ref[0, :, lanes], axis=0, keepdims=True)


def land_back_call(me, blocks, gq, gk, gv, member_t, inv, per, pairs, factor):
    items, span, width = gq.shape
    n = len(blocks)
    rows = blocks[0].shape[0]
    wide = per_item((span, width))
    shape = jax.ShapeDtypeStruct((items, span, width), f32)
    return pl.pallas_call(
        functools.partial(land_back_kernel, n, per, pairs, factor),
        out_shape=[shape, shape, jax.ShapeDtypeStruct((8, width), f32)],
        grid_spec=pltpu.PrefetchScalarGridSpec(
            num_scalar_prefetch=1,
            grid=(items,),
            in_specs=[whole((rows, PAIR))] * n
            + [wide, wide, wide, per_item((MARKS, span)), whole(inv.shape)],
            out_specs=[wide, wide, whole((8, width))],
            scratch_shapes=[VM((n, rows, PAIR), f32), VM((MARKS, PAIR), f32)],
        ),
        compiler_params=params(),
        name="land_back",
    )(me, *blocks, gq, gk, gv, member_t, inv)


def swap(x, axis, offset):
    count = lax.axis_size(axis)
    return lax.ppermute(x, axis, [(i, i ^ offset) for i in range(count)])


def exchange(chunks):
    return [chunks[0]] + [swap(chunks[k], "seq", k) for k in range(1, len(chunks))]


def gathered(x):
    count = lax.axis_size("seq")
    slots = [None] * count
    for k in range(0, count, 2):
        slots[k] = swap(x, "seq", k) if k else x
    for k in range(0, count, 2):
        slots[k + 1] = swap(slots[k], "seq", 1)
    return slots


def edges(x, margin):
    count = lax.axis_size("seq")
    left = lax.ppermute(x[:, -margin:], "seq", [(i, i + 1) for i in range(count - 1)])
    right = lax.ppermute(x[:, :margin], "seq", [(i + 1, i) for i in range(count - 1)])
    return left, right


def bit_of(axis, bit):
    return lax.axis_index(axis) // bit % 2


def halve_rows(x, bit):
    blocks, rows, columns = x.shape
    y = x.reshape(blocks // 2, 2, rows, columns)
    mine = bit_of("seq", bit)
    keep = lax.dynamic_index_in_dim(y, mine, 1, False)
    send = lax.dynamic_index_in_dim(y, 1 - mine, 1, False)
    return keep + swap(send, "seq", bit)


def halve_columns(x, bits, bit):
    mine = bit_of("dp", bit)
    columns = x.shape[2]
    groups = 2 ** bits.index(bit)
    size = columns // (2 * groups)

    def pick(which):
        parts = [
            lax.dynamic_slice_in_dim(x, 2 * g * size + which * size, size, 2)
            for g in range(groups)
        ]
        return parts[0] if groups == 1 else jnp.concatenate(parts, axis=2)

    return pick(mine) + swap(pick(1 - mine), "dp", bit)


def powers(axis):
    count = lax.axis_size(axis)
    return [2**i for i in range(count.bit_length() - 1)]


def scatter_sum(x, order):
    seq_bits, dp_bits = powers("seq"), powers("dp")[::-1]
    count = lax.axis_size("seq")
    x = x.reshape(count, x.shape[0] // count, x.shape[1])
    x = halve_rows(x, seq_bits.pop(0))
    for axis in order:
        if axis == "z" and seq_bits:
            x = halve_rows(x, seq_bits.pop(0))
        elif axis in "xy" and dp_bits:
            half = len(powers("dp")) // 2
            low = [b for b in dp_bits if b < 2**half]
            high = [b for b in dp_bits if b >= 2**half]
            chosen = (low if axis == "x" else high) or dp_bits
            x = halve_columns(x, dp_bits, chosen[0])
            dp_bits.remove(chosen[0])
    while seq_bits:
        x = halve_rows(x, seq_bits.pop(0))
    while dp_bits:
        x = halve_columns(x, dp_bits, dp_bits[0])
        dp_bits.pop(0)
    return x[0]


def sum_everywhere(x):
    for axis in ("seq", "dp"):
        for bit in powers(axis):
            x = x + swap(x, axis, bit)
    return x


def rounded_pair(w):
    hi = lax.reduce_precision(w, 8, 7)
    return hi.astype(bf16), (w - hi).astype(bf16)


def product(a, b, ca, cb):
    return lax.dot_general(a, b, (((ca,), (cb,)), ((), ())), precision=HIGH)


def on_device(
    tokens,
    lengths,
    keep,
    w_query,
    b_query,
    w_key,
    w_value,
    b_value,
    conv_weight,
    w_out,
    b_out,
    gain_one,
    shift_one,
    w_up,
    b_up,
    w_down,
    b_down,
    gain_two,
    shift_two,
    cotangent,
):
    items, span, width = tokens.shape
    heads, taps = conv_weight.shape
    head_size = width // heads
    margin = taps // 2
    factor = head_size ** (-0.25)
    pairs = heads // 2
    n = lax.axis_size("seq")
    per = -(-items * pairs // n)
    chunk_rows = per * MARKS + 8
    me_index = lax.axis_index("seq")
    me = me_index.astype(jnp.int32).reshape(1)
    position = me_index * span + jnp.arange(span, dtype=jnp.int32)
    inside = position[None, :] < lengths[:, None]
    usable = (inside & (keep > 0)).astype(f32)
    use_row, use_col = usable[:, None, :], usable[:, :, None]
    segment = jnp.where(inside, position[None, :] * MARKS // lengths[:, None], MARKS)
    marks = jnp.arange(MARKS, dtype=jnp.int32)
    member_t = (segment[:, None, :] == marks[None, :, None]).astype(f32) * use_row

    sums = jnp.einsum("imt,itd->imd", member_t, tokens, precision=HIGH)
    counts = jnp.broadcast_to(jnp.sum(member_t, axis=2, keepdims=True), (items, MARKS, PAIR))
    sums = jnp.concatenate([sums, counts], axis=2).reshape(n, items * MARKS // n, width + PAIR)
    parts = [lax.dynamic_index_in_dim(sums, me_index ^ k, 0, False) for k in range(n)]
    land = jnp.stack(gathered(sum(exchange(parts))))
    divisor = jnp.maximum(land[:, :, width:], 1.0)
    inverse_divisor = 1.0 / divisor
    filled = land[:, :, width : width + 1] / divisor[:, :, :1]
    land_tokens = (land[:, :, :width] / divisor[:, :, :1]).reshape(items * MARKS, width)
    land_q = product(land_tokens, w_query, 1, 0).reshape(n, -1, width)
    land_q = (land_q + filled * b_query) * factor
    land_k = product(land_tokens, w_key, 1, 0).reshape(n, -1, width) * factor

    rows = tokens.reshape(items * span, width)
    values = (product(rows, w_value, 1, 0) + b_value).reshape(items, span, width)
    queries = ((product(rows, w_query, 1, 0) + b_query) * factor).reshape(items, span, width)
    key_rows = (product(rows, w_key, 1, 0) * factor).reshape(items, span, width)
    vleft, vright = edges(values * use_col, margin)
    taps_forward = jnp.pad(conv_weight, ((0, 4), (0, 2 * PAIR - taps)))
    taps_backward = jnp.pad(conv_weight[:, ::-1], ((0, 4), (0, 2 * PAIR - taps)))

    k1, w3, top, *chunks = scores_call(
        me, queries, key_rows, values, land_q, land_k, use_row, n, per, pairs, chunk_rows
    )
    chunks = exchange(chunks)
    kernel_two, z, owned_q, owned_k = newton_call(me, land_q, land_k, per, pairs, items)
    context, mixed = context_call(chunks, z, per)
    mixed = gathered(mixed)
    attn_input = mix_call(
        me, mixed, k1, values, use_col, vleft, vright, taps_forward, per, pairs, margin
    )

    vectors = jnp.stack(
        [b_out, gain_one, shift_one, b_down, gain_two, shift_two, b_out, b_out]
    )
    x = attn_input.reshape(items * span, width)
    output, act, u, r2, hidden, r1, og, row_sums, up_sums = rows_call(
        x,
        rows,
        cotangent.reshape(items * span, width),
        rounded_pair(w_out),
        rounded_pair(w_up),
        rounded_pair(w_down),
        vectors,
        b_up[None, :],
    )
    og = og.reshape(items, span, width)
    gleft, gright = edges(og, margin)
    grad_queries, *chunks = one_back_call(me, mixed, k1, og, queries, land_k, per, pairs)
    chunks = exchange(chunks)

    grad_w_down = scatter_sum(product(r2, act, 0, 0), "yxzz")
    grad_w_up = scatter_sum(product(u, hidden, 0, 0), "xzyz")
    grad_w_out = scatter_sum(product(r1, x, 0, 0), "zyxz")
    gv_conv, grad_taps = conv_back_call(
        og, gleft, gright, values, vleft, vright, use_col, taps_backward, pairs, margin
    )

    grad_context, grad_mixed, part_key = context_back_call(chunks, z, context, per, chunk_rows)
    grad_context = gathered(grad_context)
    own_q, own_k = newton_back_call(
        grad_mixed, part_key, context, kernel_two, z, owned_q, owned_k
    )
    grad_values, grad_keys, *chunks = three_back_call(
        me, grad_context, mixed, w3, top, values, key_rows, gv_conv, land_q, per, pairs
    )
    own_q = own_q.reshape(per * MARKS, PAIR) + sum(exchange(chunks))
    land_grads = gathered(jnp.concatenate([own_q, own_k.reshape(per * MARKS, PAIR)]))
    grad_queries, grad_keys, late_sums = land_back_call(
        me, land_grads, grad_queries, grad_keys, grad_values, member_t, inverse_divisor,
        per, pairs, factor,
    )
    grad_queries = grad_queries.reshape(items * span, width)
    grad_keys = grad_keys.reshape(items * span, width)
    grad_values = grad_values.reshape(items * span, width)
    grad_w_value = scatter_sum(product(grad_values, rows, 0, 0), "zyxz")
    grad_w_query = scatter_sum(product(grad_queries, rows, 0, 0), "yxzz")
    grad_w_key = scatter_sum(product(grad_keys, rows, 0, 0), "xzyz")
    grad_tokens = (
        r1
        + product(grad_values, w_value, 1, 1)
        + product(grad_queries, w_query, 1, 1)
        + product(grad_keys, w_key, 1, 1)
    )

    early = sum_everywhere(
        jnp.concatenate([row_sums.reshape(-1), up_sums.reshape(-1), grad_taps.reshape(-1)]).reshape(
            -1, PAIR
        )
    ).reshape(-1)
    late = sum_everywhere(late_sums)
    row_sums = early[: 8 * width].reshape(8, width)
    ff = w_up.shape[1]
    up_sums = early[8 * width : 8 * width + ff]
    grad_taps = early[8 * width + ff :].reshape(-1, 2 * PAIR)
    grad_conv = grad_taps[:heads, PAIR - 1 : PAIR - 1 + taps]
    return (
        output.reshape(tokens.shape),
        grad_tokens.reshape(tokens.shape),
        grad_w_query.T,
        late[0],
        grad_w_key.T,
        grad_w_value.T,
        late[1],
        grad_conv,
        grad_w_out.T,
        row_sums[5],
        row_sums[3],
        row_sums[4],
        grad_w_up.T,
        up_sums,
        grad_w_down.T,
        row_sums[2],
        row_sums[0],
        row_sums[1],
    )


def solution(mesh):
    rows = P("dp", "seq", None)
    block = P("dp", "seq")
    in_specs = (rows, P("dp"), block) + (P(),) * 16 + (rows,)
    out_specs = (
        rows, rows, block, P(), block, block, P(), P(), block,
        P(), P(), P(), block, P(), block, P(), P(), P(),
    )
    return jax.shard_map(
        on_device, mesh=mesh, in_specs=in_specs, out_specs=out_specs, check_vma=False
    )
```

time: 1420 us -> 754 us (0.53)
  matrix products: 775 us -> 113 us
  Pallas kernels: 0 us -> 229 us
  waiting for transfers between devices: 287 us -> 148 us
  starting transfers between devices: 8.72 us -> 120 us
  blocking collectives: 92.4 us -> 0 us
  other arithmetic: 136 us -> 66.7 us
  local copies, waits for them, and re-layouts: 99.2 us -> 64.2 us
  between operations: 17 us -> 2.66 us
    dot_general x112 -> x15, matrix products: 775 us -> 113 us  [the longest x14 110 us: product(): return lax.dot_general(a, b, (((ca,), (cb,)), ((), ())), precision=HIGH)]
    pallas_call x0 -> x11, Pallas kernels: none -> 229 us  [the longest x1 110 us: rows_call(): pl.pallas_call(functools.partial(rows_kernel, ff_tile), out_shape=[narrow...]
    reduce_scatter x8 -> x0, waiting for transfers between devices: 180 us -> none  [the longest x1 71.2 us: on_device(): lax.psum_scatter(grad_w_up, 'seq', scatter_dimension=1, tiled=True)]
    ppermute x4 -> x100, waiting for transfers between devices: 0.01 us -> 148 us  [the longest x96 148 us: swap(): return lax.ppermute(x, axis, [(i, i ^ offset) for i in range(count)])]
    ppermute x4 -> x100, starting transfers between devices: 7.26 us -> 120 us  [the longest x96 112 us: swap(): return lax.ppermute(x, axis, [(i, i ^ offset) for i in range(count)])]
    psum x3 -> x0, waiting for transfers between devices: 89.7 us -> none  [the longest x2 56.9 us: on_device(): grad_mixed, part_land_key = lax.psum((part_mixed, part_land_key), 'seq')]
    reduce_sum x13 -> x0, other arithmetic: 67.5 us -> none  [the longest x5 56.7 us: on_device(): jnp.sum(grad_pre * padded[:, tap_index:tap_index + span], axis=(0, 1, 3))]
    psum x2 -> x0, blocking collectives: 59.6 us -> none  [the longest x1 39.5 us: on_device(): lax.psum((grad_b_query, grad_b_value, grad_conv, grad_b_out, grad_gain_on...]
  transfers between devices with their start and end apart: 20 -> 100, of which waited for: 8 -> 24; matrix products, arithmetic and copies ran while one was open for 43% -> 29% of each run, Pallas kernels for 0% -> 13%
where the time goes in v1:
time: 754 us; the launch traced here: 744 us
  Pallas kernels  229 us (30%)
  waiting for transfers between devices  148 us (20%)
  starting transfers between devices  120 us (16%)
  matrix products  113 us (15%)
  other arithmetic  66.7 us (9%)
  local copies, waits for them, and re-layouts  64.2 us (9%)
    ppermute x96, waiting for transfers between devices, swap(): return lax.ppermute(x, axis, [(i, i ^ offset) for i in range(count)])  148 us
    ppermute x96, starting transfers between devices, swap(): return lax.ppermute(x, axis, [(i, i ^ offset) for i in range(count)])  112 us
    pallas_call x1, Pallas kernels, rows_call(): pl.pallas_call(functools.partial(rows_kernel, ff_tile), out_shape=[narrow...  110 us
    dot_general x14, matrix products, product(): return lax.dot_general(a, b, (((ca,), (cb,)), ((), ())), precision=HIGH)  110 us
    convert_element_type x3, other arithmetic, rounded_pair(): return (hi.astype(bf16), (w - hi).astype(bf16))  21.6 us
    pallas_call x1, Pallas kernels, newton_back_call(): pl.pallas_call(functools.partial(newton_back_kernel, per), out_shape=[sma...  21.1 us
    pallas_call x1, Pallas kernels, conv_back_call(): pl.pallas_call(functools.partial(conv_back_kernel, pairs, margin), out_sh...  17.9 us
    squeeze x18, local copies, waits for them, and re-layouts, halve_rows(): send = lax.dynamic_index_in_dim(y, 1 - mine, 1, False)  15.6 us
  transfers between devices with their start and end apart: 100, of which 24 were waited for; matrix products, arithmetic and copies ran while one was open for 29% of the time, Pallas kernels for 13%

profile of v1, /device:TPU:0, one launch (start us, length us, event | category | flops | bytes accessed | tf_op | source)
XLA Modules:
  0.0 744.1 jit_solution(7760087276811450881)
XLA Ops:
  13.7 8.7 %fusion.1 = (bf16[3072,768]{1,0:T(8,128)(2,1)}, bf16[3072,768]{1,0:T(8,128)(2,1)}) fusion(f32[3072,768]{1,0:T(8,128)} %param.35), kind=kLoop, calls=%fused_computation.5 | loop fusion | flops 9437184 | bytes 18874368 | tf_op jit(solution)/shard_map/convert_element_type | solution.py:932
  22.4 9.5 %fusion = (bf16[768,3072]{1,0:T(8,128)(2,1)}, bf16[768,3072]{1,0:T(8,128)(2,1)}) fusion(f32[768,3072]{1,0:T(8,128)} %param.33), kind=kLoop, calls=%fused_computation.4 | loop fusion | flops 9437184 | bytes 18874368 | tf_op jit(solution)/shard_map/convert_element_type | solution.py:932
  31.9 5.7 convolution_add_fusion
  37.6 3.5 collective-permute-start.5
  41.8 6.0 add_multiply_fusion
  49.8 3.5 collective-permute-start.8
  53.3 7.3 convolution_multiply_fusion
  63.8 8.2 %collective-permute-done.10 = f32[32,896]{1,0:T(8,128)S(1)} collective-permute-done((f32[32,896]{1,0:T(8,128)S(1)}, f32[32,896]{1,0:T(8,128)S(1)}, u32[]{:S(2)}, u32[]{:S(2)}) %collective-permute-start.10) | collective-permute-done | bytes 114720 | tf_op jit(solution)/shard_map/ppermute | solution.py:842
  78.9 14.5 %scores.1 = (f32[4,768,256]{2,1,0:T(8,128)}, f32[4,768,256]{2,1,0:T(8,128)}, f32[4,8,128]{2,1,0:T(8,128)}, f32[200,128]{1,0:T(8,128)}, f32[200,128]{1,0:T(8,128)...) custom-call(s32[1]{0:T(128)} %bitcast.me_ref, ...), custom_call_target="tpu_custom_call" | custom-call | tf_op jit(solution)/shard_map/scores/pallas_call | solution.py:147
  105.8 12.3 %newton.1 = (f32[3,128,128]{2,1,0:T(8,128)}, f32[7,3,128,128]{3,2,1,0:T(8,128)}, f32[3,64,128]{2,1,0:T(8,128)}, f32[3,64,128]{2,1,0:T(8,128)}) custom-call(s32[1]{0:T(128)} %bitcast.me_ref, f32[8,32,768]{2,1,0:T(8,128)} %fusion.10.lq_ref.refs_21_, f32[8,32,768]{2,1,0:T(8,128)} %fusion.13.lk_ref.refs_11_), custom_call_target="tpu_custom_call" | custom-call | tf_op jit(solution)/shard_map/newton/pallas_call | solution.py:227
  130.2 3.5 fusion.2
  134.3 4.3 collective-permute-done.24.refs_4_.refs_12_
  143.8 10.7 %mix.1 = f32[4,256,768]{2,1,0:T(8,128)} custom-call(s32[1]{0:T(128)} %bitcast.me_ref, f32[200,128]{1,0:T(8,128)} %get-tuple-element.82.refs_0_.refs_8_, f32[200,128]{1,0:T(8,128)} %copy-done.32, f32[200,128]{1,0:T(8,128)} %copy-done.29, f32[200,128]{1,0:T(8,128)} %copy-done.33, f32[200,128]{1,0:T(8,128)} %copy-done.30, f32[200,128]{1,0:T(8,128)} %copy-done.34, ...), custom_call_target="tpu_custom_call" | custom-call | tf_op jit(solution)/shard_map/mix/pallas_call | solution.py:347
  154.5 109.9 %rows.1 = (f32[1024,768]{1,0:T(8,128)}, f32[1024,3072]{1,0:T(8,128)}, f32[1024,3072]{1,0:T(8,128)}, f32[1024,768]{1,0:T(8,128)}, f32[1024,768]{1,0:T(8,128)}, /*...) custom-call(f32[1024,768]{1,0:T(8,128)} %bitcast.236, f32[1024,768]{1,0:T(8,128)} %bitcast.224, ...), custom_call_target="tpu_custom_call" | custom-call | tf_op jit(solution)/shard_map/rows/pallas_call | solution.py:481
  264.5 3.5 copy.65
  273.8 13.1 %one_back.1 = (f32[4,256,768]{2,1,0:T(8,128)}, f32[384,128]{1,0:T(8,128)}, f32[384,128]{1,0:T(8,128)}, f32[384,128]{1,0:T(8,128)}, f32[384,128]{1,0:T(8,128)}, /...) custom-call(s32[1]{0:T(128)} %bitcast.me_ref, ...), custom_call_target="tpu_custom_call" | custom-call | tf_op jit(solution)/shard_map/one_back/pallas_call | solution.py:550
  290.0 20.8 %fusion.45 = f32[768,3072]{1,0:T(8,128)} fusion(f32[1024,768]{1,0:T(8,128)} %get-tuple-element.126, f32[1024,3072]{1,0:T(8,128)} %get-tuple-element.127), kind=kOutput, calls=%fused_computation.157 | convolution fusion | flops 14495514624 | bytes 25165824 | tf_op jit(solution)/shard_map/dot_general | solution.py:936
  310.8 22.0 %fusion.44 = f32[3072,768]{1,0:T(8,128)} fusion(f32[1024,3072]{1,0:T(8,128)} %get-tuple-element.124, f32[1024,768]{1,0:T(8,128)S(1)} %copy-done.70), kind=kOutput, calls=%fused_computation.156 | convolution fusion | flops 14495514624 | bytes 25165824 | tf_op jit(solution)/shard_map/dot_general | solution.py:936
  332.8 5.5 fusion.43
  341.5 17.9 %conv_back.1 = (f32[4,256,768]{2,1,0:T(8,128)}, f32[16,256]{1,0:T(8,128)}) custom-call(f32[4,256,768]{2,1,0:T(8,128)} %bitcast.246, f32[4,16,768]{2,1,0:T(8,128)} %collective-permute-done.44.gl_ref, f32[4,16,768]{2,1,0:T(8,128)} %collective-permute-done.45.gr_ref, f32[4,256,768]{2,1,0:T(8,128)} %bitcast.234, ...), custom_call_target="tpu_custom_call" | custom-call | tf_op jit(solution)/shard_map/conv_back/pallas_call | solution.py:621
  366.2 5.0 dynamic-slice_bitcast_fusion
  378.3 8.4 %collective-permute-start.38 = (f32[200,128]{1,0:T(8,128)}, f32[200,128]{1,0:T(8,128)}, u32[]{:S(2)}, u32[]{:S(2)}) collective-permute-start(f32[200,128]{1,0:T(8,128)} %get-tuple-element.96.refs_0_), channel_id=1, source_target_pairs={{0,2},{1,3},{2,0},{3,1},{4,6},{5,7},{6,4},{7,5},{8,10},{9,11},{10,... | collective-permute-start | bytes 307208 | tf_op jit(solution)/shard_map/ppermute | solution.py:842
  391.1 4.9 dynamic-slice_bitcast_fusion.1
  403.3 21.1 %newton_back.1 = (f32[3,64,128]{2,1,0:T(8,128)}, f32[3,64,128]{2,1,0:T(8,128)}) custom-call(f32[3,64,128]{2,1,0:T(8,128)} %get-tuple-element.101.gm_ref, f32[3,64,128]{2,1,0:T(8,128)} %get-tuple-element.102.key_ref, f32[3,64,128]{2,1,0:T(8,128)} %get-tuple-element.95.refs_9_.ctx_ref, f32[3,128,128]{2,1,0:T(8,128)} %get-tuple-element.103.a_ref, ...), custom_call_target="tpu_custom_call" | custom-call | tf_op jit(solution)/shard_map/newton_back/pallas_call | solution.py:709
  427.4 14.8 %three_back.1 = (f32[4,256,768]{2,1,0:T(8,128)}, f32[4,256,768]{2,1,0:T(8,128)}, f32[192,128]{1,0:T(8,128)}, f32[192,128]{1,0:T(8,128)}, f32[192,128]{1,0:T(8,12...) custom-call(s32[1]{0:T(128)} %bitcast.me_ref, ...), custom_call_target="tpu_custom_call" | custom-call | tf_op jit(solution)/shard_map/three_back/pallas_call | solution.py:768
  442.2 4.1 copy.64
  449.0 6.1 fusion.42
  457.6 5.7 fusion.38
  470.8 5.0 collective-permute-done.50
  475.9 4.8 collective-permute-start.54
  483.7 5.5 collective-permute-done.54.refs_2_
  489.2 8.6 %collective-permute-done.56.refs_4_ = f32[384,128]{1,0:T(8,128)S(1)} collective-permute-done((f32[384,128]{1,0:T(8,128)S(1)}, f32[384,128]{1,0:T(8,128)S(1)}, u32[]{:S(2)}, u32[]{:S(2)}) %collective-permute-start.56) | collective-permute-done | bytes 196640 | tf_op jit(solution)/shard_map/ppermute | solution.py:842
  500.4 8.5 %land_back.1 = (f32[4,256,768]{2,1,0:T(8,128)}, f32[4,256,768]{2,1,0:T(8,128)}, f32[8,768]{1,0:T(8,128)}) custom-call(s32[1]{0:T(128)} %bitcast.me_ref, f32[384,128]{1,0:T(8,128)} %copy-done.39, f32[384,128]{1,0:T(8,128)} %copy-done.47, f32[384,128]{1,0:T(8,128)} %copy-done.44, f32[384,128]{1,0:T(8,128)} %copy-done.48, f32[384,128]{1,0:T(8,128)} %copy-done.45, ...), custom_call_target="tpu_custom_call" | custom-call | tf_op jit(solution)/shard_map/land_back/pallas_call | solution.py:824
  509.4 6.8 fusion.39
  516.3 8.1 %add_add_fusion = f32[1024,768]{1,0:T(8,128)} fusion(f32[1024,768]{1,0:T(8,128)S(1)} %fusion.39, f32[1024,768]{1,0:T(8,128)S(1)} %copy-done.10, f32[1024,768]{1,0:T(8,128)S(1)} %copy-done.11, f32[1024,768]{1,0:T(8,128)} %bitcast.256, f32[768,768]{1,0:T(8,128)S(1)} %copy-done.6), kind=kOutput, calls=%fused_computation.12 | convolution fusion | flops 3626237952 | bytes 18087936 | tf_op jit(solution)/shard_map/dot_general | solution.py:936
  524.3 3.7 copy.63
  528.0 3.2 collective-permute-start.66
  531.3 7.3 fusion.41
  538.6 3.7 copy.62
  546.9 4.1 fusion.40
  551.7 3.2 collective-permute-done.68
  555.5 3.2 collective-permute-done.69
  562.7 7.4 collective-permute-done.87
  576.6 8.5 %collective-permute-done.76 = f32[2,96,768]{2,1,0:T(8,128)S(1)} collective-permute-done((f32[2,96,768]{2,1,0:T(8,128)S(1)}, f32[2,96,768]{2,1,0:T(8,128)S(1)}, u32[]{:S(2)}, u32[]{:S(2)}) %collective-permute-start.76) | collective-permute-done | bytes 589856 | tf_op jit(solution)/shard_map/ppermute | solution.py:842
  595.6 4.5 bitcast_add_fusion.1
  624.0 38.7 %collective-permute-done.62 = f32[4,96,192]{2,1,0:T(8,128)} collective-permute-done((f32[4,96,192]{2,1,0:T(8,128)}, f32[4,96,192]{2,1,0:T(8,128)}, u32[]{:S(2)}, u32[]{:S(2)}) %collective-permute-start.62) | collective-permute-done | bytes 294944 | tf_op jit(solution)/shard_map/ppermute | solution.py:842
  675.0 21.8 %collective-permute-done.63 = f32[2,96,192]{2,1,0:T(8,128)S(1)} collective-permute-done((f32[2,96,192]{2,1,0:T(8,128)S(1)}, f32[2,96,192]{2,1,0:T(8,128)S(1)}, u32[]{:S(2)}, u32[]{:S(2)}) %collective-permute-start.63) | collective-permute-done | bytes 147488 | tf_op jit(solution)/shard_map/ppermute | solution.py:842
  724.9 14.9 %collective-permute-done.94 = f32[1,384,192]{2,1,0:T(8,128)S(1)} collective-permute-done((f32[1,384,192]{2,1,0:T(8,128)S(1)}, f32[1,384,192]{2,1,0:T(8,128)S(1)}, u32[]{:S(2)}, u32[]{:S(2)}) %collective-permute-start.94) | collective-permute-done | bytes 294944 | tf_op jit(solution)/shard_map/ppermute | solution.py:842
  (474 shorter events, 209.3 us)
Async XLA Ops:
  7.8 29.8 %collective-permute-start = (f32[32,896]{1,0:T(8,128)S(1)}, f32[32,896]{1,0:T(8,128)S(1)}, u32[]{:S(2)}, u32[]{:S(2)}) collective-permute-start(f32[32,896]{1,0:T(8,128)S(1)} %get-tuple-element.190), channel_id=1, source_target_pairs={{0,1},{1,0},{2,3},{3,2},{4,5},{5,4},{6,7},{7,6},{8,9},{9,8},{10,11... | collective-permute-start | bytes 344072 | tf_op jit(solution)/shard_map/ppermute | solution.py:842
  8.3 32.9 %collective-permute-start.1 = (f32[32,896]{1,0:T(8,128)S(1)}, f32[32,896]{1,0:T(8,128)S(1)}, u32[]{:S(2)}, u32[]{:S(2)}) collective-permute-start(f32[32,896]{1,0:T(8,128)S(1)} %get-tuple-element.196), channel_id=1, source_target_pairs={{0,2},{1,3},{2,0},{3,1},{4,6},{5,7},{6,4},{7,5},{8,10},{9,11},{10,... | collective-permute-start | bytes 344072 | tf_op jit(solution)/shard_map/ppermute | solution.py:842
  10.8 37.0 %collective-permute-start.2 = (f32[32,896]{1,0:T(8,128)}, f32[32,896]{1,0:T(8,128)}, u32[]{:S(2)}, u32[]{:S(2)}) collective-permute-start(f32[32,896]{1,0:T(8,128)} %get-tuple-element.195), channel_id=1, source_target_pairs={{0,3},{1,2},{2,1},{3,0},{4,7},{5,6},{6,5},{7,4},{8,11},{9,10},{10,... | collective-permute-start | bytes 344072 | tf_op jit(solution)/shard_map/ppermute | solution.py:842
  11.0 36.8 %collective-permute-start.3 = (f32[32,896]{1,0:T(8,128)}, f32[32,896]{1,0:T(8,128)}, u32[]{:S(2)}, u32[]{:S(2)}) collective-permute-start(f32[32,896]{1,0:T(8,128)} %get-tuple-element.194), channel_id=1, source_target_pairs={{0,4},{1,5},{2,6},{3,7},{4,0},{5,1},{6,2},{7,3},{8,12},{9,13},{10,... | collective-permute-start | bytes 344072 | tf_op jit(solution)/shard_map/ppermute | solution.py:842
  13.7 34.1 %collective-permute-start.4 = (f32[32,896]{1,0:T(8,128)}, f32[32,896]{1,0:T(8,128)}, u32[]{:S(2)}, u32[]{:S(2)}) collective-permute-start(f32[32,896]{1,0:T(8,128)} %get-tuple-element.193), channel_id=1, source_target_pairs={{0,5},{1,4},{2,7},{3,6},{4,1},{5,0},{6,3},{7,2},{8,13},{9,12},{10,... | collective-permute-start | bytes 344072 | tf_op jit(solution)/shard_map/ppermute | solution.py:842
  98.6 19.4 %collective-permute-start.16 = (f32[200,128]{1,0:T(8,128)}, f32[200,128]{1,0:T(8,128)}, u32[]{:S(2)}, u32[]{:S(2)}) collective-permute-start(f32[200,128]{1,0:T(8,128)} %get-tuple-element.76), channel_id=1, source_target_pairs={{0,3},{1,2},{2,1},{3,0},{4,7},{5,6},{6,5},{7,4},{8,11},{9,10},{10,... | collective-permute-start | bytes 307208 | tf_op jit(solution)/shard_map/ppermute | solution.py:842
  98.7 22.5 %collective-permute-start.17 = (f32[200,128]{1,0:T(8,128)}, f32[200,128]{1,0:T(8,128)}, u32[]{:S(2)}, u32[]{:S(2)}) collective-permute-start(f32[200,128]{1,0:T(8,128)} %get-tuple-element.77), channel_id=1, source_target_pairs={{0,4},{1,5},{2,6},{3,7},{4,0},{5,1},{6,2},{7,3},{8,12},{9,13},{10,... | collective-permute-start | bytes 307208 | tf_op jit(solution)/shard_map/ppermute | solution.py:842
  101.5 21.0 %collective-permute-start.18 = (f32[200,128]{1,0:T(8,128)}, f32[200,128]{1,0:T(8,128)}, u32[]{:S(2)}, u32[]{:S(2)}) collective-permute-start(f32[200,128]{1,0:T(8,128)} %get-tuple-element.78), channel_id=1, source_target_pairs={{0,5},{1,4},{2,7},{3,6},{4,1},{5,0},{6,3},{7,2},{8,13},{9,12},{10,... | collective-permute-start | bytes 307208 | tf_op jit(solution)/shard_map/ppermute | solution.py:842
  101.6 20.9 %collective-permute-start.19 = (f32[200,128]{1,0:T(8,128)}, f32[200,128]{1,0:T(8,128)}, u32[]{:S(2)}, u32[]{:S(2)}) collective-permute-start(f32[200,128]{1,0:T(8,128)} %get-tuple-element.79), channel_id=1, source_target_pairs={{0,6},{1,7},{2,4},{3,5},{4,2},{5,3},{6,0},{7,1},{8,14},{9,15},{10,... | collective-permute-start | bytes 307208 | tf_op jit(solution)/shard_map/ppermute | solution.py:842
  103.7 18.8 %collective-permute-start.20 = (f32[200,128]{1,0:T(8,128)}, f32[200,128]{1,0:T(8,128)}, u32[]{:S(2)}, u32[]{:S(2)}) collective-permute-start(f32[200,128]{1,0:T(8,128)} %get-tuple-element.80), channel_id=1, source_target_pairs={{0,7},{1,6},{2,5},{3,4},{4,3},{5,2},{6,1},{7,0},{8,15},{9,14},{10,... | collective-permute-start | bytes 307208 | tf_op jit(solution)/shard_map/ppermute | solution.py:842
  121.2 21.2 %collective-permute-start.29 = (f32[4,16,768]{2,1,0:T(8,128)}, f32[4,16,768]{2,1,0:T(8,128)}, u32[]{:S(2)}, u32[]{:S(2)}) collective-permute-start(f32[4,16,768]{2,1,0:T(8,128)} %get-tuple-element.180), channel_id=1, source_target_pairs={{1,0},{2,1},{3,2},{4,3},{5,4},{6,5},{7,6},{9,8},{10,9},{11,10},{12... | collective-permute-start | bytes 589832 | tf_op jit(solution)/shard_map/ppermute | solution.py:862
  269.8 69.0 %collective-permute-start.44 = (f32[4,16,768]{2,1,0:T(8,128)}, f32[4,16,768]{2,1,0:T(8,128)}, u32[]{:S(2)}, u32[]{:S(2)}) collective-permute-start(f32[4,16,768]{2,1,0:T(8,128)} %get-tuple-element.179), channel_id=1, source_target_pairs={{0,1},{1,2},{2,3},{3,4},{4,5},{5,6},{6,7},{8,9},{9,10},{10,11},{11... | collective-permute-start | bytes 589832 | tf_op jit(solution)/shard_map/ppermute | solution.py:861
  272.5 69.0 %collective-permute-start.45 = (f32[4,16,768]{2,1,0:T(8,128)}, f32[4,16,768]{2,1,0:T(8,128)}, u32[]{:S(2)}, u32[]{:S(2)}) collective-permute-start(f32[4,16,768]{2,1,0:T(8,128)} %get-tuple-element.178), channel_id=1, source_target_pairs={{1,0},{2,1},{3,2},{4,3},{5,4},{6,5},{7,6},{9,8},{10,9},{11,10},{12... | collective-permute-start | bytes 589832 | tf_op jit(solution)/shard_map/ppermute | solution.py:862
  286.9 75.3 %collective-permute-start.30 = (f32[384,128]{1,0:T(8,128)}, f32[384,128]{1,0:T(8,128)}, u32[]{:S(2)}, u32[]{:S(2)}) collective-permute-start(f32[384,128]{1,0:T(8,128)} %get-tuple-element.88), channel_id=1, source_target_pairs={{0,1},{1,0},{2,3},{3,2},{4,5},{5,4},{6,7},{7,6},{8,9},{9,8},{10,11... | collective-permute-start | bytes 589832 | tf_op jit(solution)/shard_map/ppermute | solution.py:842
  288.2 76.4 %collective-permute-start.31 = (f32[384,128]{1,0:T(8,128)}, f32[384,128]{1,0:T(8,128)}, u32[]{:S(2)}, u32[]{:S(2)}) collective-permute-start(f32[384,128]{1,0:T(8,128)} %get-tuple-element.89), channel_id=1, source_target_pairs={{0,2},{1,3},{2,0},{3,1},{4,6},{5,7},{6,4},{7,5},{8,10},{9,11},{10,... | collective-permute-start | bytes 589832 | tf_op jit(solution)/shard_map/ppermute | solution.py:842
  289.9 75.8 %collective-permute-start.32 = (f32[384,128]{1,0:T(8,128)}, f32[384,128]{1,0:T(8,128)}, u32[]{:S(2)}, u32[]{:S(2)}) collective-permute-start(f32[384,128]{1,0:T(8,128)} %get-tuple-element.90), channel_id=1, source_target_pairs={{0,3},{1,2},{2,1},{3,0},{4,7},{5,6},{6,5},{7,4},{8,11},{9,10},{10,... | collective-permute-start | bytes 589832 | tf_op jit(solution)/shard_map/ppermute | solution.py:842
  338.9 32.3 %collective-permute-start.33 = (f32[384,128]{1,0:T(8,128)}, f32[384,128]{1,0:T(8,128)}, u32[]{:S(2)}, u32[]{:S(2)}) collective-permute-start(f32[384,128]{1,0:T(8,128)} %get-tuple-element.91), channel_id=1, source_target_pairs={{0,4},{1,5},{2,6},{3,7},{4,0},{5,1},{6,2},{7,3},{8,12},{9,13},{10,... | collective-permute-start | bytes 589832 | tf_op jit(solution)/shard_map/ppermute | solution.py:842
  341.5 29.7 %collective-permute-start.34 = (f32[384,128]{1,0:T(8,128)}, f32[384,128]{1,0:T(8,128)}, u32[]{:S(2)}, u32[]{:S(2)}) collective-permute-start(f32[384,128]{1,0:T(8,128)} %get-tuple-element.92), channel_id=1, source_target_pairs={{0,5},{1,4},{2,7},{3,6},{4,1},{5,0},{6,3},{7,2},{8,13},{9,12},{10,... | collective-permute-start | bytes 589832 | tf_op jit(solution)/shard_map/ppermute | solution.py:842
  365.7 23.4 %collective-permute-start.80 = (f32[104,128]{1,0:T(8,128)}, f32[104,128]{1,0:T(8,128)}, u32[]{:S(2)}, u32[]{:S(2)}) collective-permute-start(f32[104,128]{1,0:T(8,128)} %maximum_bitcast_fusion), channel_id=1, source_target_pairs={{0,1},{1,0},{2,3},{3,2},{4,5},{5,4},{6,7},{7,6},{8,9},{9,8},{10,11... | collective-permute-start | bytes 159752 | tf_op jit(solution)/shard_map/ppermute | solution.py:842
  378.3 17.7 %collective-permute-start.38 = (f32[200,128]{1,0:T(8,128)}, f32[200,128]{1,0:T(8,128)}, u32[]{:S(2)}, u32[]{:S(2)}) collective-permute-start(f32[200,128]{1,0:T(8,128)} %get-tuple-element.96.refs_0_), channel_id=1, source_target_pairs={{0,2},{1,3},{2,0},{3,1},{4,6},{5,7},{6,4},{7,5},{8,10},{9,11},{10,... | collective-permute-start | bytes 307208 | tf_op jit(solution)/shard_map/ppermute | solution.py:842
  396.0 31.4 %collective-permute-start.37 = (f32[200,128]{1,0:T(8,128)}, f32[200,128]{1,0:T(8,128)}, u32[]{:S(2)}, u32[]{:S(2)}) collective-permute-start(f32[200,128]{1,0:T(8,128)} %get-tuple-element.96.refs_0_), channel_id=1, source_target_pairs={{0,1},{1,0},{2,3},{3,2},{4,5},{5,4},{6,7},{7,6},{8,9},{9,8},{10,11... | collective-permute-start | bytes 307208 | tf_op jit(solution)/shard_map/ppermute | solution.py:842
  396.0 31.4 %collective-permute-start.39 = (f32[200,128]{1,0:T(8,128)}, f32[200,128]{1,0:T(8,128)}, u32[]{:S(2)}, u32[]{:S(2)}) collective-permute-start(f32[200,128]{1,0:T(8,128)} %collective-permute-done.38.refs_2_), channel_id=1, source_target_pairs={{0,1},{1,0},{2,3},{3,2},{4,5},{5,4},{6,7},{7,6},{8,9},{9,8},{10,11... | collective-permute-start | bytes 307208 | tf_op jit(solution)/shard_map/ppermute | solution.py:842
  398.0 29.4 %collective-permute-start.41 = (f32[200,128]{1,0:T(8,128)}, f32[200,128]{1,0:T(8,128)}, u32[]{:S(2)}, u32[]{:S(2)}) collective-permute-start(f32[200,128]{1,0:T(8,128)} %collective-permute-done.40.refs_4_), channel_id=1, source_target_pairs={{0,1},{1,0},{2,3},{3,2},{4,5},{5,4},{6,7},{7,6},{8,9},{9,8},{10,11... | collective-permute-start | bytes 307208 | tf_op jit(solution)/shard_map/ppermute | solution.py:842
  398.0 29.4 %collective-permute-start.43 = (f32[200,128]{1,0:T(8,128)}, f32[200,128]{1,0:T(8,128)}, u32[]{:S(2)}, u32[]{:S(2)}) collective-permute-start(f32[200,128]{1,0:T(8,128)} %collective-permute-done.42.refs_6_), channel_id=1, source_target_pairs={{0,1},{1,0},{2,3},{3,2},{4,5},{5,4},{6,7},{7,6},{8,9},{9,8},{10,11... | collective-permute-start | bytes 307208 | tf_op jit(solution)/shard_map/ppermute | solution.py:842
  400.0 24.4 %collective-permute-start.82 = (f32[104,128]{1,0:T(8,128)}, f32[104,128]{1,0:T(8,128)}, u32[]{:S(2)}, u32[]{:S(2)}) collective-permute-start(f32[104,128]{1,0:T(8,128)} %fusion.71), channel_id=1, source_target_pairs={{0,4},{1,5},{2,6},{3,7},{4,0},{5,1},{6,2},{7,3},{8,12},{9,13},{10,... | collective-permute-start | bytes 159752 | tf_op jit(solution)/shard_map/ppermute | solution.py:842
  425.9 29.2 %collective-permute-start.83 = (f32[104,128]{1,0:T(8,128)}, f32[104,128]{1,0:T(8,128)}, u32[]{:S(2)}, u32[]{:S(2)}) collective-permute-start(f32[104,128]{1,0:T(8,128)} %add.490), channel_id=1, source_target_pairs={{0,8},{8,0},{16,24},{24,16},{1,9},{9,1},{17,25},{25,17},{2,10},{10... | collective-permute-start | bytes 159752 | tf_op jit(solution)/shard_map/ppermute | solution.py:842
  446.3 18.7 %collective-permute-start.46 = (f32[192,128]{1,0:T(8,128)}, f32[192,128]{1,0:T(8,128)S(1)}, u32[]{:S(2)}, u32[]{:S(2)}) collective-permute-start(f32[192,128]{1,0:T(8,128)} %get-tuple-element.108), channel_id=1, source_target_pairs={{0,1},{1,0},{2,3},{3,2},{4,5},{5,4},{6,7},{7,6},{8,9},{9,8},{10,11... | collective-permute-start | bytes 294920 | tf_op jit(solution)/shard_map/ppermute | solution.py:842
  446.4 20.1 %collective-permute-start.47 = (f32[192,128]{1,0:T(8,128)}, f32[192,128]{1,0:T(8,128)S(1)}, u32[]{:S(2)}, u32[]{:S(2)}) collective-permute-start(f32[192,128]{1,0:T(8,128)} %get-tuple-element.109), channel_id=1, source_target_pairs={{0,2},{1,3},{2,0},{3,1},{4,6},{5,7},{6,4},{7,5},{8,10},{9,11},{10,... | collective-permute-start | bytes 294920 | tf_op jit(solution)/shard_map/ppermute | solution.py:842
  446.9 23.8 %collective-permute-start.48 = (f32[192,128]{1,0:T(8,128)}, f32[192,128]{1,0:T(8,128)S(1)}, u32[]{:S(2)}, u32[]{:S(2)}) collective-permute-start(f32[192,128]{1,0:T(8,128)} %get-tuple-element.110), channel_id=1, source_target_pairs={{0,3},{1,2},{2,1},{3,0},{4,7},{5,6},{6,5},{7,4},{8,11},{9,10},{10,... | collective-permute-start | bytes 294920 | tf_op jit(solution)/shard_map/ppermute | solution.py:842
  448.2 22.6 %collective-permute-start.49 = (f32[192,128]{1,0:T(8,128)}, f32[192,128]{1,0:T(8,128)S(1)}, u32[]{:S(2)}, u32[]{:S(2)}) collective-permute-start(f32[192,128]{1,0:T(8,128)} %get-tuple-element.111), channel_id=1, source_target_pairs={{0,4},{1,5},{2,6},{3,7},{4,0},{5,1},{6,2},{7,3},{8,12},{9,13},{10,... | collective-permute-start | bytes 294920 | tf_op jit(solution)/shard_map/ppermute | solution.py:842
  470.7 134.6 %collective-permute-start.95 = (f32[4,96,3072]{2,1,0:T(8,128)}, f32[4,96,3072]{2,1,0:T(8,128)}, u32[]{:S(2)}, u32[]{:S(2)}) collective-permute-start(f32[4,96,3072]{2,1,0:T(8,128)} %dynamic-slice_bitcast_fusion), channel_id=1, source_target_pairs={{0,1},{1,0},{2,3},{3,2},{4,5},{5,4},{6,7},{7,6},{8,9},{9,8},{10,11... | collective-permute-start | bytes 14155784 | tf_op jit(solution)/shard_map/ppermute | solution.py:842
  498.9 96.7 %collective-permute-start.90 = (f32[4,384,768]{2,1,0:T(8,128)}, f32[4,384,768]{2,1,0:T(8,128)}, u32[]{:S(2)}, u32[]{:S(2)}) collective-permute-start(f32[4,384,768]{2,1,0:T(8,128)} %dynamic-slice_bitcast_fusion.1), channel_id=1, source_target_pairs={{0,1},{1,0},{2,3},{3,2},{4,5},{5,4},{6,7},{7,6},{8,9},{9,8},{10,11... | collective-permute-start | bytes 14155784 | tf_op jit(solution)/shard_map/ppermute | solution.py:842
  499.1 44.0 %collective-permute-start.85 = (f32[4,96,768]{2,1,0:T(8,128)}, f32[4,96,768]{2,1,0:T(8,128)}, u32[]{:S(2)}, u32[]{:S(2)}) collective-permute-start(f32[4,96,768]{2,1,0:T(8,128)} %dynamic-slice_bitcast_fusion.3), channel_id=1, source_target_pairs={{0,1},{1,0},{2,3},{3,2},{4,5},{5,4},{6,7},{7,6},{8,9},{9,8},{10,11... | collective-permute-start | bytes 3538952 | tf_op jit(solution)/shard_map/ppermute | solution.py:842
  499.6 61.1 %collective-permute-start.75 = (f32[4,96,768]{2,1,0:T(8,128)}, f32[4,96,768]{2,1,0:T(8,128)}, u32[]{:S(2)}, u32[]{:S(2)}) collective-permute-start(f32[4,96,768]{2,1,0:T(8,128)} %dynamic-slice_bitcast_fusion.4), channel_id=1, source_target_pairs={{0,1},{1,0},{2,3},{3,2},{4,5},{5,4},{6,7},{7,6},{8,9},{9,8},{10,11... | collective-permute-start | bytes 3538952 | tf_op jit(solution)/shard_map/ppermute | solution.py:842
  508.9 19.1 %collective-permute-start.65 = (f32[8,768]{1,0:T(8,128)}, f32[8,768]{1,0:T(8,128)S(1)}, u32[]{:S(2)}, u32[]{:S(2)}) collective-permute-start(f32[8,768]{1,0:T(8,128)} %get-tuple-element.120), channel_id=1, source_target_pairs={{0,1},{1,0},{2,3},{3,2},{4,5},{5,4},{6,7},{7,6},{8,9},{9,8},{10,11... | collective-permute-start | bytes 73736 | tf_op jit(solution)/shard_map/ppermute | solution.py:842
  574.9 36.7 %collective-permute-start.71 = (f32[4,96,384]{2,1,0:T(8,128)}, f32[4,96,384]{2,1,0:T(8,128)}, u32[]{:S(2)}, u32[]{:S(2)}) collective-permute-start(f32[4,96,384]{2,1,0:T(8,128)} %pad_maximum_fusion.2), channel_id=1, source_target_pairs={{0,8},{8,0},{16,24},{24,16},{1,9},{9,1},{17,25},{25,17},{2,10},{10... | collective-permute-start | bytes 1769480 | tf_op jit(solution)/shard_map/ppermute | solution.py:842
  591.5 22.7 %collective-permute-start.61 = (f32[4,96,384]{2,1,0:T(8,128)}, f32[4,96,384]{2,1,0:T(8,128)}, u32[]{:S(2)}, u32[]{:S(2)}) collective-permute-start(f32[4,96,384]{2,1,0:T(8,128)} %constant_dynamic-slice_fusion.23), channel_id=1, source_target_pairs={{0,16},{8,24},{16,0},{24,8},{1,17},{9,25},{17,1},{25,9},{2,18},{10... | collective-permute-start | bytes 1769480 | tf_op jit(solution)/shard_map/ppermute | solution.py:842
  603.9 60.4 %collective-permute-start.91 = (f32[4,384,384]{2,1,0:T(8,128)}, f32[4,384,384]{2,1,0:T(8,128)}, u32[]{:S(2)}, u32[]{:S(2)}) collective-permute-start(f32[4,384,384]{2,1,0:T(8,128)} %pad_maximum_fusion), channel_id=1, source_target_pairs={{0,8},{8,0},{16,24},{24,16},{1,9},{9,1},{17,25},{25,17},{2,10},{10... | collective-permute-start | bytes 7077896 | tf_op jit(solution)/shard_map/ppermute | solution.py:842
  610.1 57.1 %collective-permute-start.96 = (f32[4,96,1536]{2,1,0:T(8,128)}, f32[4,96,1536]{2,1,0:T(8,128)}, u32[]{:S(2)}, u32[]{:S(2)}) collective-permute-start(f32[4,96,1536]{2,1,0:T(8,128)} %constant_dynamic-slice_fusion.2), channel_id=1, source_target_pairs={{0,16},{8,24},{16,0},{24,8},{1,17},{9,25},{17,1},{25,9},{2,18},{10... | collective-permute-start | bytes 7077896 | tf_op jit(solution)/shard_map/ppermute | solution.py:842
  617.2 45.5 %collective-permute-start.62 = (f32[4,96,192]{2,1,0:T(8,128)}, f32[4,96,192]{2,1,0:T(8,128)}, u32[]{:S(2)}, u32[]{:S(2)}) collective-permute-start(f32[4,96,192]{2,1,0:T(8,128)} %constant_dynamic-slice_fusion.22), channel_id=1, source_target_pairs={{0,8},{8,0},{16,24},{24,16},{1,9},{9,1},{17,25},{25,17},{2,10},{10... | collective-permute-start | bytes 884744 | tf_op jit(solution)/shard_map/ppermute | solution.py:842
  621.7 51.6 %collective-permute-start.73 = (f32[2,96,192]{2,1,0:T(8,128)S(1)}, f32[2,96,192]{2,1,0:T(8,128)S(1)}, u32[]{:S(2)}, u32[]{:S(2)}) collective-permute-start(f32[2,96,192]{2,1,0:T(8,128)S(1)} %constant_dynamic-slice_fusion.16), channel_id=1, source_target_pairs={{0,16},{8,24},{16,0},{24,8},{1,17},{9,25},{17,1},{25,9},{2,18},{10... | collective-permute-start | bytes 442376 | tf_op jit(solution)/shard_map/ppermute | solution.py:842
  666.5 31.1 %collective-permute-start.92 = (f32[2,384,384]{2,1,0:T(8,128)S(1)}, f32[2,384,384]{2,1,0:T(8,128)S(1)}, u32[]{:S(2)}, u32[]{:S(2)}) collective-permute-start(f32[2,384,384]{2,1,0:T(8,128)S(1)} %dynamic-slice_bitcast_fusion.2), channel_id=1, source_target_pairs={{0,2},{1,3},{2,0},{3,1},{4,6},{5,7},{6,4},{7,5},{8,10},{9,11},{10,... | collective-permute-start | bytes 3538952 | tf_op jit(solution)/shard_map/ppermute | solution.py:842
  670.4 31.6 %collective-permute-start.97 = (f32[4,96,768]{2,1,0:T(8,128)}, f32[4,96,768]{2,1,0:T(8,128)}, u32[]{:S(2)}, u32[]{:S(2)}) collective-permute-start(f32[4,96,768]{2,1,0:T(8,128)} %constant_dynamic-slice_fusion.1), channel_id=1, source_target_pairs={{0,8},{8,0},{16,24},{24,16},{1,9},{9,1},{17,25},{25,17},{2,10},{10... | collective-permute-start | bytes 3538952 | tf_op jit(solution)/shard_map/ppermute | solution.py:842
  671.8 25.0 %collective-permute-start.63 = (f32[2,96,192]{2,1,0:T(8,128)S(1)}, f32[2,96,192]{2,1,0:T(8,128)S(1)}, u32[]{:S(2)}, u32[]{:S(2)}) collective-permute-start(f32[2,96,192]{2,1,0:T(8,128)S(1)} %dynamic-slice_bitcast_fusion.11), channel_id=1, source_target_pairs={{0,2},{1,3},{2,0},{3,1},{4,6},{5,7},{6,4},{7,5},{8,10},{9,11},{10,... | collective-permute-start | bytes 442376 | tf_op jit(solution)/shard_map/ppermute | solution.py:842
  674.2 33.4 %collective-permute-start.74 = (f32[1,96,192]{2,1,0:T(8,128)}, f32[1,96,192]{2,1,0:T(8,128)}, u32[]{:S(2)}, u32[]{:S(2)}) collective-permute-start(f32[1,96,192]{2,1,0:T(8,128)} %constant_dynamic-slice_fusion.15), channel_id=1, source_target_pairs={{0,4},{1,5},{2,6},{3,7},{4,0},{5,1},{6,2},{7,3},{8,12},{9,13},{10,... | collective-permute-start | bytes 221192 | tf_op jit(solution)/shard_map/ppermute | solution.py:842
  697.6 24.8 %collective-permute-start.64 = (f32[1,96,192]{2,1,0:T(8,128)}, f32[1,96,192]{2,1,0:T(8,128)}, u32[]{:S(2)}, u32[]{:S(2)}) collective-permute-start(f32[1,96,192]{2,1,0:T(8,128)} %constant_dynamic-slice_fusion.21), channel_id=1, source_target_pairs={{0,4},{1,5},{2,6},{3,7},{4,0},{5,1},{6,2},{7,3},{8,12},{9,13},{10,... | collective-permute-start | bytes 221192 | tf_op jit(solution)/shard_map/ppermute | solution.py:842
  715.6 24.2 %collective-permute-start.94 = (f32[1,384,192]{2,1,0:T(8,128)S(1)}, f32[1,384,192]{2,1,0:T(8,128)S(1)}, u32[]{:S(2)}, u32[]{:S(2)}) collective-permute-start(f32[1,384,192]{2,1,0:T(8,128)S(1)} %constant_dynamic-slice_fusion.3), channel_id=1, source_target_pairs={{0,4},{1,5},{2,6},{3,7},{4,0},{5,1},{6,2},{7,3},{8,12},{9,13},{10,... | collective-permute-start | bytes 884744 | tf_op jit(solution)/shard_map/ppermute | solution.py:842
  721.0 21.9 %collective-permute-start.99 = (f32[1,96,768]{2,1,0:T(8,128)S(1)}, f32[1,96,768]{2,1,0:T(8,128)S(1)}, u32[]{:S(2)}, u32[]{:S(2)}) collective-permute-start(f32[1,96,768]{2,1,0:T(8,128)S(1)} %constant_dynamic-slice_fusion), channel_id=1, source_target_pairs={{0,4},{1,5},{2,6},{3,7},{4,0},{5,1},{6,2},{7,3},{8,12},{9,13},{10,... | collective-permute-start | bytes 884744 | tf_op jit(solution)/shard_map/ppermute | solution.py:842
  (133 other events, 1249.1 us)

commit v2 on v1

v2 whole, which is shorter than its diff:
```python
import functools

import jax
import jax.numpy as jnp
from jax import lax
from jax.experimental import pallas as pl
from jax.experimental.pallas import tpu as pltpu
from jax.sharding import PartitionSpec as P

MARKS = 64
NEWTON = 6
PAIR = 128
HIGH = lax.Precision.HIGH
epsilon = 1e-05
f32 = jnp.float32
bf16 = jnp.bfloat16
VM = pltpu.VMEM
LIMIT = 66 * 1024 * 1024


def split(x):
    hi = x.astype(bf16)
    return hi, (x - hi.astype(f32)).astype(bf16)


def dg(a, b, ca, cb):
    return lax.dot_general(a, b, (((ca,), (cb,)), ((), ())), preferred_element_type=f32)


def dots(a, b, ca, cb):
    return dg(a[0], b[0], ca, cb) + dg(a[0], b[1], ca, cb) + dg(a[1], b[0], ca, cb)


def dot3(a, b, ca=1, cb=0):
    return dots(split(a), split(b), ca, cb)


def lane_low(shape):
    return lax.broadcasted_iota(jnp.int32, shape, len(shape) - 1) < PAIR // 2


def spread(compact):
    low = lane_low(compact.shape)
    zero = jnp.zeros_like(compact)
    return jnp.concatenate([jnp.where(low, compact, zero), jnp.where(low, zero, compact)], axis=0)


def compacted(block):
    half = block.shape[0] // 2
    return jnp.where(lane_low((half, block.shape[1])), block[:half], block[half:])


def row_of(column):
    return jnp.transpose(jnp.broadcast_to(column, (PAIR, PAIR)))[0:1, :]


def column_of(row):
    return jnp.transpose(jnp.broadcast_to(row, (PAIR, PAIR)))


def diagonal_mask():
    rows = lax.broadcasted_iota(jnp.int32, (PAIR, PAIR), 0) < PAIR // 2
    return rows == lane_low((PAIR, PAIR))


def block_sum(x):
    halves = x.reshape(2, x.shape[0] // 2, x.shape[1])
    total = jnp.sum(halves, axis=1, keepdims=True)
    return jnp.broadcast_to(total, halves.shape).reshape(x.shape)


def block_max(x):
    halves = x.reshape(2, x.shape[0] // 2, x.shape[1])
    total = jnp.max(halves, axis=1, keepdims=True)
    return jnp.broadcast_to(total, halves.shape).reshape(x.shape)


def params(**more):
    return pltpu.CompilerParams(vmem_limit_bytes=LIMIT, **more)


def whole(shape):
    return pl.BlockSpec(shape, lambda *_: (0,) * len(shape))


def per_item(shape):
    return pl.BlockSpec((1,) + shape, lambda i, *_: (i,) + (0,) * len(shape))


class Seat:
    def __init__(self, n):
        self.n, self.nz = n, n // 2
        self.me = lax.axis_index("seq")
        self.core = lax.rem(self.me, 2)
        self.z = self.me // 2
        self.owner = self.core * self.nz + self.z
        self.partner = self.me + 1 - 2 * self.core
        self.extra = lax.rem(self.me + 2 * self.core - 1 + n, n)

    def ahead(self, j):
        return lax.rem(self.z + j, self.nz)

    def behind(self, j):
        return lax.rem(self.z - j + self.nz, self.nz)

    def at(self, z):
        return 2 * z + self.core

    def hello(self, edges):
        others = [self.partner] + [self.at(self.ahead(j)) for j in range(1, self.nz)]
        if edges:
            others.append(self.extra)
        barrier = pltpu.get_barrier_semaphore()
        for other in others:
            pl.semaphore_signal(barrier, inc=1, device_id={"seq": other}, device_id_type=MESH)
        pl.semaphore_wait(barrier, len(others))


MESH = pl.DeviceIdType.MESH


def remote(src, dst, send, recv, device):
    return pltpu.make_async_remote_copy(
        src_ref=src, dst_ref=dst, send_sem=send, recv_sem=recv,
        device_id={"seq": device}, device_id_type=MESH,
    )


class Reduce:
    def __init__(self, seat, chunks, first, acc, second, send, recv):
        self.seat, self.chunks, self.first, self.acc, self.second = seat, chunks, first, acc, second
        self.send, self.recv = send, recv
        self.across = remote(chunks.at[1 - seat.core], first, send.at[0], recv.at[0], seat.partner)
        self.along = [
            remote(
                acc.at[seat.ahead(j)], second.at[j - 1], send.at[j], recv.at[j],
                seat.at(seat.ahead(j)),
            )
            for j in range(1, seat.nz)
        ]

    def start(self):
        self.across.start()

    def middle(self, merge):
        self.across.wait()
        for z in range(self.seat.nz):
            self.acc[z] = merge([self.chunks.at[self.seat.core, z], self.first.at[z]])
        for copy in self.along:
            copy.start()

    def finish(self, merge):
        for copy in self.along:
            copy.wait()
        refs = [self.acc.at[self.seat.z]] + [self.second.at[j] for j in range(self.seat.nz - 1)]
        return merge(refs)

    @staticmethod
    def scratch(n, shape):
        nz = n // 2
        return [
            VM((nz,) + shape, f32),
            VM((nz,) + shape, f32),
            VM((nz - 1,) + shape, f32),
            pltpu.SemaphoreType.DMA((nz,)),
            pltpu.SemaphoreType.DMA((nz,)),
        ]


class Gather:
    def __init__(self, seat, out, send, recv):
        own = out.at[seat.core, seat.z]
        self.along = [
            remote(own, own, send.at[j], recv.at[j], seat.at(seat.ahead(j)))
            for j in range(1, seat.nz)
        ]
        self.across = [remote(own, own, send.at[0], recv.at[0], seat.partner)]
        for j in range(1, seat.nz):
            block = out.at[seat.core, seat.behind(j)]
            k = seat.nz + j
            self.across.append(remote(block, block, send.at[k], recv.at[k], seat.partner))

    def start(self):
        for copy in self.along:
            copy.start()
        self.across[0].start()

    def forward(self):
        for copy, onward in zip(self.along, self.across[1:]):
            copy.wait_recv()
            onward.start()

    def finish(self):
        for copy in self.along:
            copy.wait_send()
        for copy in self.across:
            copy.wait()

    @staticmethod
    def scratch(n):
        return [pltpu.SemaphoreType.DMA((n,)), pltpu.SemaphoreType.DMA((n,))]


class Edges:
    def __init__(self, seat, sides, halos, send, recv):
        self.seat, self.halos = seat, halos
        core = seat.core
        self.copies = [
            remote(sides.at[1 - core], halos.at[core], send.at[0], recv.at[0], seat.partner),
            remote(sides.at[core], halos.at[1 - core], send.at[1], recv.at[1], seat.extra),
        ]

    def start(self):
        for copy in self.copies:
            copy.start()

    def finish(self, out):
        for copy in self.copies:
            copy.wait()
        seat = self.seat
        inner = (jnp.where(seat.me > 0, 1.0, 0.0), jnp.where(seat.me < seat.n - 1, 1.0, 0.0))
        for side in range(2):
            out[side] = self.halos[side] * inner[side]

    @staticmethod
    def scratch(shape):
        return [VM(shape, f32), pltpu.SemaphoreType.DMA((2,)), pltpu.SemaphoreType.DMA((2,))]


def add_all(refs):
    return functools.reduce(lambda x, y: x + y, [r[...] for r in refs])


def project_kernel(n, items, factor, tok_ref, mem_ref, wq_ref, wk_ref, wv_ref, vec_ref,
                   q_ref, k_ref, v_ref, lq_ref, lk_ref, inv_ref,
                   sums, land, halves, *scratch):
    seat = Seat(n)
    rows = items * MARKS // n
    width = tok_ref.shape[2]
    reduce = Reduce(seat, sums, *scratch[:5])
    gather = Gather(seat, land, *scratch[5:])
    seat.hello(False)
    for item in range(items):
        member = mem_ref[item].astype(bf16)
        hi, lo = split(tok_ref[item])
        total = dg(member, hi, 1, 0) + dg(member, lo, 1, 0)
        count = jnp.sum(mem_ref[item], axis=1, keepdims=True)
        for part in range(MARKS // rows):
            c = item * (MARKS // rows) + part
            piece = slice(part * rows, (part + 1) * rows)
            sums[c // seat.nz, c % seat.nz, :, :width] = total[piece]
            sums[c // seat.nz, c % seat.nz, :, width:] = jnp.broadcast_to(
                count[piece], (rows, PAIR)
            )
    reduce.start()
    b_query, b_value = vec_ref[0:1, :], vec_ref[1:2, :]
    for place, w_ref in enumerate((wq_ref, wk_ref, wv_ref)):
        hi, lo = split(w_ref[...])
        halves[2 * place], halves[2 * place + 1] = hi, lo

    def project(place, out_ref, bias, scale):
        def lap(item, _):
            x = split(tok_ref[item])
            y = dots(x, (halves[2 * place], halves[2 * place + 1]), 1, 0)
            y = y if bias is None else y + bias
            out_ref[item] = y if scale is None else y * scale
            return 0

        lax.fori_loop(0, items, lap, 0)

    project(0, q_ref, b_query, factor)
    reduce.middle(add_all)
    project(1, k_ref, None, factor)
    land[seat.core, seat.z] = reduce.finish(add_all)
    gather.start()
    project(2, v_ref, b_value, None)
    gather.forward()
    gather.finish()
    whole_land = land[...].reshape(items * MARKS, width + PAIR)
    divisor = jnp.maximum(whole_land[:, width:], 1.0)
    inv_ref[...] = (1.0 / divisor).reshape(items, MARKS, PAIR)
    filled = whole_land[:, width : width + 1] / divisor[:, 0:1]
    x = split(whole_land[:, :width] / divisor[:, 0:1])
    lq = (dots(x, (halves[0], halves[1]), 1, 0) + filled * b_query) * factor
    lk = dots(x, (halves[2], halves[3]), 1, 0) * factor
    lq_ref[...] = lq.reshape(items, MARKS, width)
    lk_ref[...] = lk.reshape(items, MARKS, width)


def project_call(tokens, member_t, w_query, w_key, w_value, vectors, n, factor):
    items, span, width = tokens.shape
    rows = items * MARKS // n
    big = jax.ShapeDtypeStruct((items, span, width), f32)
    small = jax.ShapeDtypeStruct((items, MARKS, width), f32)
    return pl.pallas_call(
        functools.partial(project_kernel, n, items, factor),
        out_shape=[big, big, big, small, small, jax.ShapeDtypeStruct((items, MARKS, PAIR), f32)],
        in_specs=[pl.BlockSpec(memory_space=VM)] * 6,
        out_specs=[pl.BlockSpec(memory_space=VM)] * 6,
        scratch_shapes=[
            VM((2, n // 2, rows, width + PAIR), f32),
            VM((2, n // 2, rows, width + PAIR), f32),
            VM((6, width, width), bf16),
        ]
        + Reduce.scratch(n, (rows, width + PAIR))
        + Gather.scratch(n),
        compiler_params=params(collective_id=0, has_side_effects=True),
        name="project",
    )(tokens, member_t, w_query, w_key, w_value, vectors)


def scores_kernel(per, pairs, q_ref, k_ref, v_ref, lq_ref, lk_ref, use_ref, k1_ref, w3_ref, top_ref, chunk):
    item = pl.program_id(0)
    stats = per * MARKS

    @pl.when(item == 0)
    def _():
        chunk[...] = jnp.zeros_like(chunk)

    use = use_ref[0]
    for p in range(pairs):
        lanes = slice(p * PAIR, (p + 1) * PAIR)
        q = q_ref[0, :, lanes]
        s1 = dot3(spread(lk_ref[0, :, lanes]), q, 1, 1)
        e1 = jnp.exp(s1 - block_max(s1))
        k1_ref[0, lanes, :] = e1 / block_sum(e1)
        s3 = dot3(spread(lq_ref[0, :, lanes]), k_ref[0, :, lanes], 1, 1)
        masked = jnp.where(use > 0, s3, -1e30)
        top = jnp.max(masked, axis=1, keepdims=True)
        w3 = jnp.exp(masked - top) * use
        w3_ref[0, lanes, :] = w3
        total = jnp.sum(w3, axis=1, keepdims=True)
        weighted = compacted(dot3(w3, v_ref[0, :, lanes]))
        top_row = row_of(top)
        top_ref[0, p : p + 1, :] = top_row
        g = item * pairs + p
        owner, place = g // per, g % per
        chunk[owner, pl.ds(pl.multiple_of(place * MARKS, MARKS), MARKS), :] = weighted
        chunk[owner, pl.ds(stats + 2 * place, 1), :] = top_row
        chunk[owner, pl.ds(stats + 2 * place + 1, 1), :] = row_of(total)


def scores_call(q, k, v, lq, lk, use_row, n, per, pairs, chunk_rows):
    items, span, width = q.shape
    return pl.pallas_call(
        functools.partial(scores_kernel, per, pairs),
        out_shape=[
            jax.ShapeDtypeStruct((items, width, span), f32),
            jax.ShapeDtypeStruct((items, width, span), f32),
            jax.ShapeDtypeStruct((items, 8, PAIR), f32),
            jax.ShapeDtypeStruct((n, chunk_rows, PAIR), f32),
        ],
        grid=(items,),
        in_specs=[per_item((span, width))] * 3
        + [per_item((MARKS, width))] * 2
        + [per_item((1, span))],
        out_specs=[per_item((width, span))] * 2
        + [per_item((8, PAIR)), whole((n, chunk_rows, PAIR))],
        compiler_params=params(),
        name="scores",
    )(q, k, v, lq, lk, use_row)


def owned_land(seat, per, pairs, ref, into):
    for place in range(per):
        g = lax.rem(seat.owner * per + place, ref.shape[0] * pairs)
        item, p = g // pairs, lax.rem(g, pairs)
        into[place] = ref[item, :, pl.ds(pl.multiple_of(p * PAIR, PAIR), PAIR)]


def newton_step(a, z, eye):
    pr = dot3(a, z)
    n1 = 7.0 * eye - pr
    n2 = 15.0 * eye - dot3(pr, n1)
    n3 = 13.0 * eye - dot3(pr, n2)
    return pr, n1, n2, n3


def unit():
    rows = lax.broadcasted_iota(jnp.int32, (PAIR, PAIR), 0)
    return (rows == lax.broadcasted_iota(jnp.int32, (PAIR, PAIR), 1)).astype(f32)


def head_total(x):
    return block_sum(jnp.sum(x, axis=1, keepdims=True))


def merged(per, refs):
    stats = per * MARKS
    weights, rest = [], []
    for place in range(per):
        tops = [r[stats + 2 * place : stats + 2 * place + 1, :] for r in refs]
        largest = functools.reduce(jnp.maximum, tops)
        total = jnp.zeros_like(largest)
        weighted = jnp.zeros((MARKS, PAIR), f32)
        for r, top in zip(refs, tops):
            scale = jnp.exp(top - largest)
            total = total + scale * r[stats + 2 * place + 1 : stats + 2 * place + 2, :]
            scales = compacted(column_of(scale))
            weighted = weighted + scales * r[place * MARKS : (place + 1) * MARKS, :]
        weights.append(weighted)
        rest += [largest, total]
    filler = jnp.zeros((refs[0].shape[0] - stats - 2 * per, PAIR), f32)
    return jnp.concatenate(weights + rest + [filler], axis=0)


def exchange_kernel(n, per, pairs, chunk_ref, lq_ref, lk_ref, side_ref,
                    a_ref, z_ref, lqo_ref, lko_ref, ctx_ref, out_ref, halo_ref, mine, *scratch):
    seat = Seat(n)
    merge = functools.partial(merged, per)
    reduce = Reduce(seat, chunk_ref, *scratch[:5])
    gather = Gather(seat, out_ref, *scratch[5:7])
    edges = Edges(seat, side_ref, *scratch[7:])
    seat.hello(True)
    reduce.start()
    edges.start()
    owned_land(seat, per, pairs, lq_ref, lqo_ref)
    owned_land(seat, per, pairs, lk_ref, lko_ref)
    diagonal = diagonal_mask()
    eye = unit()
    for place in range(per):
        s2 = dot3(spread(lqo_ref[place]), spread(lko_ref[place]), 1, 1)
        s2 = jnp.where(diagonal, s2, -1e30)
        e2 = jnp.exp(s2 - jnp.max(s2, axis=1, keepdims=True))
        e2 = jnp.where(diagonal, e2, 0.0)
        a = e2 / jnp.sum(e2, axis=1, keepdims=True)
        a_ref[place] = a
        z_ref[0, place] = jnp.transpose(a) / head_total(a * a)
    reduce.middle(merge)

    def lap(step, _):
        for place in range(per):
            z = z_ref[step, place]
            _, _, _, n3 = newton_step(a_ref[place], z, eye)
            z_ref[step + 1, place] = 0.25 * dot3(z, n3)
        return 0

    lax.fori_loop(0, NEWTON, lap, 0)
    mine[...] = reduce.finish(merge)
    stats = per * MARKS
    block = out_ref.at[seat.core, seat.z]
    block[stats:, :] = mine[stats:, :]
    for place in range(per):
        rows = slice(place * MARKS, (place + 1) * MARKS)
        total = mine[stats + 2 * place + 1 : stats + 2 * place + 2, :]
        context = mine[rows, :] / compacted(column_of(total))
        ctx_ref[place] = context
        block[rows, :] = compacted(dot3(z_ref[NEWTON, place], spread(context)))
    gather.start()
    edges.finish(halo_ref)
    gather.forward()
    gather.finish()


def exchange_call(chunks, lq, lk, sides, n, per, pairs):
    rows = chunks.shape[1]
    small = jax.ShapeDtypeStruct((per, MARKS, PAIR), f32)
    blocks = (2, n // 2, rows, PAIR)
    out = pl.pallas_call(
        functools.partial(exchange_kernel, n, per, pairs),
        out_shape=[
            jax.ShapeDtypeStruct((per, PAIR, PAIR), f32),
            jax.ShapeDtypeStruct((NEWTON + 1, per, PAIR, PAIR), f32),
            small,
            small,
            small,
            jax.ShapeDtypeStruct(blocks, f32),
            jax.ShapeDtypeStruct(sides.shape, f32),
        ],
        in_specs=[pl.BlockSpec(memory_space=VM)] * 4,
        out_specs=[pl.BlockSpec(memory_space=VM)] * 7,
        scratch_shapes=[VM((rows, PAIR), f32)]
        + Reduce.scratch(n, (rows, PAIR))
        + Gather.scratch(n)
        + Edges.scratch(sides.shape),
        compiler_params=params(collective_id=1, has_side_effects=True),
        name="exchange",
    )(chunks.reshape(blocks), lq, lk, sides)
    return list(out[:5]) + [out[5].reshape(n, rows, PAIR), out[6]]


def toeplitz(taps_row, rows):
    wide = jnp.broadcast_to(taps_row, (rows, 2 * PAIR))
    return pltpu.roll(wide, 0, 1, stride=1, stride_axis=0)


def keep_taps(taps_ref, into, heads):
    for h in range(heads):
        hi, lo = split(toeplitz(taps_ref[h : h + 1, :], PAIR))
        into[0, h] = hi
        into[1, h] = lo


def keep_window(win, left, middle, right, margin, span):
    for rows, part in (
        (slice(0, margin), left),
        (slice(margin, margin + span), middle),
        (slice(margin + span, 2 * margin + span), right),
    ):
        hi, lo = split(part)
        win[0, rows, :] = hi
        win[1, rows, :] = lo


def convolve(taps, win, p, block, window):
    lanes = slice(p * PAIR, (p + 1) * PAIR)
    rows = slice(block * PAIR, block * PAIR + window)
    v = (win[0, rows, lanes], win[1, rows, lanes])
    halves = []
    for h in (2 * p, 2 * p + 1):
        t = (taps[0, h, :, :window], taps[1, h, :, :window])
        halves.append(dots(t, v, 1, 0))
    return jnp.where(lane_low((PAIR, PAIR)), halves[0], halves[1])


def owned_by(g, per):
    return g // per, g % per


def mix_kernel(per, pairs, margin, held, k1_ref, v_ref, use_ref, left_ref, right_ref, taps_ref, out_ref, taps, win):
    item = pl.program_id(0)
    span = v_ref.shape[1]
    window = PAIR + 2 * margin

    @pl.when(item == 0)
    def _():
        keep_taps(taps_ref, taps, 2 * pairs)

    keep_window(win, left_ref[0, 0], v_ref[0] * use_ref[0], right_ref[0, 0], margin, span)
    for p in range(pairs):
        lanes = slice(p * PAIR, (p + 1) * PAIR)
        slot, place = owned_by(item * pairs + p, per)
        mixed = held[slot, pl.ds(pl.multiple_of(place * MARKS, MARKS), MARKS), :]
        nystrom = dot3(k1_ref[0, lanes, :], spread(mixed), 0, 0)
        for block in range(span // PAIR):
            rows = slice(block * PAIR, (block + 1) * PAIR)
            out_ref[0, rows, lanes] = nystrom[rows] + convolve(taps, win, p, block, window)


def halo_specs(margin, width):
    return [
        pl.BlockSpec((1, 1, margin, width), lambda i, side=side: (side, i, 0, 0))
        for side in range(2)
    ]


def mix_call(blocks, k1, v, use_col, halos, taps, per, pairs, margin):
    items, span, width = v.shape
    return pl.pallas_call(
        functools.partial(mix_kernel, per, pairs, margin),
        out_shape=jax.ShapeDtypeStruct((items, span, width), f32),
        grid=(items,),
        in_specs=[whole(blocks.shape)]
        + [per_item((width, span)), per_item((span, width)), per_item((span, 1))]
        + halo_specs(margin, width)
        + [whole(taps.shape)],
        out_specs=per_item((span, width)),
        scratch_shapes=[
            VM((2, 2 * pairs, PAIR, 2 * PAIR), bf16),
            VM((2, span + 2 * margin, width), bf16),
        ],
        compiler_params=params(),
        name="mix",
    )(blocks, k1, v, use_col, halos, halos, taps)


def erf(x):
    x = jnp.clip(x, -3.832506856900711, 3.832506856900711)
    s = x * x
    a = 0.00022905065861350646
    for c in (0.0034082910107109506, 0.050955695062380861, 0.18520832239976145, 1.128379143519084):
        a = a * s + c
    b = -1.1791602954361697e-7
    for c in (
        0.000023547966471313185,
        0.0010179625278914885,
        0.014070470171167667,
        0.11098505178285362,
        0.49746925110067538,
        1.0,
    ):
        b = b * s + c
    return x * a / b


def normalize(x):
    center = x - jnp.mean(x, axis=-1, keepdims=True)
    inv_root = lax.rsqrt(jnp.mean(center * center, axis=-1, keepdims=True) + epsilon)
    return center * inv_root, inv_root


def norm_back(grad, scaled, inv_root):
    first = jnp.mean(grad, axis=-1, keepdims=True)
    second = jnp.mean(grad * scaled, axis=-1, keepdims=True)
    return inv_root * (grad - first - scaled * second)


def rows_kernel(
    ff_tile,
    x_ref,
    tok_ref,
    cot_ref,
    wo_h,
    wo_l,
    wu_h,
    wu_l,
    wd_h,
    wd_l,
    vec_ref,
    bup_ref,
    out_ref,
    act_ref,
    u_ref,
    r2_ref,
    h1_ref,
    r1_ref,
    og_ref,
    sums_ref,
    bsum_ref,
    slope,
):
    @pl.when(pl.program_id(0) == 0)
    def _():
        sums_ref[...] = jnp.zeros_like(sums_ref)
        bsum_ref[...] = jnp.zeros_like(bsum_ref)

    b_out, gain_one, shift_one = vec_ref[0:1, :], vec_ref[1:2, :], vec_ref[2:3, :]
    b_down, gain_two, shift_two = vec_ref[3:4, :], vec_ref[4:5, :], vec_ref[5:6, :]
    wo = (wo_h[...], wo_l[...])
    attention = dots(split(x_ref[...]), wo, 1, 0) + b_out
    scaled_one, root_one = normalize(tok_ref[...] + attention)
    hidden = scaled_one * gain_one + shift_one
    h1_ref[...] = hidden
    hs = split(hidden)
    ff = wu_h.shape[1]
    tiles = [slice(c, c + ff_tile) for c in range(0, ff, ff_tile)]
    down = b_down
    for c in tiles:
        pre = dots(hs, (wu_h[:, c], wu_l[:, c]), 1, 0) + bup_ref[:, c]
        phi = 0.5 + 0.5 * erf(pre * 0.7071067811865476)
        slope[:, c] = phi + pre * (0.3989422804014327 * jnp.exp(-0.5 * pre * pre))
        act = pre * phi
        act_ref[:, c] = act
        down = down + dots(split(act), (wd_h[c, :], wd_l[c, :]), 1, 0)
    scaled_two, root_two = normalize(hidden + down)
    out_ref[...] = scaled_two * gain_two + shift_two
    cot = cot_ref[...]
    r2 = norm_back(cot * gain_two, scaled_two, root_two)
    r2_ref[...] = r2
    rs = split(r2)
    grad_hidden = r2
    for c in tiles:
        u = dots(rs, (wd_h[c, :], wd_l[c, :]), 1, 1) * slope[:, c]
        u_ref[:, c] = u
        bsum_ref[:, c] += jnp.sum(u, axis=0, keepdims=True)
        grad_hidden = grad_hidden + dots(split(u), (wu_h[:, c], wu_l[:, c]), 1, 1)
    r1 = norm_back(grad_hidden * gain_one, scaled_one, root_one)
    r1_ref[...] = r1
    og_ref[...] = dots(split(r1), wo, 1, 1)
    for row, value in enumerate(
        (cot * scaled_two, cot, r2, grad_hidden * scaled_one, grad_hidden, r1)
    ):
        sums_ref[row : row + 1, :] += jnp.sum(value, axis=0, keepdims=True)


def rows_call(x, tokens, cotangent, wo, wu, wd, vectors, b_up):
    rows, width = x.shape
    ff = wu[0].shape[1]
    tile = 256
    ff_tile = 768
    wide = pl.BlockSpec((tile, width), lambda i: (i, 0))
    hidden = pl.BlockSpec((tile, ff), lambda i: (i, 0))

    def fixed(a):
        return pl.BlockSpec(a.shape, lambda i: (0, 0), pipeline_mode=pl.Buffered(1))

    narrow = jax.ShapeDtypeStruct((rows, width), f32)
    broad = jax.ShapeDtypeStruct((rows, ff), f32)
    return pl.pallas_call(
        functools.partial(rows_kernel, ff_tile),
        out_shape=[
            narrow,
            broad,
            broad,
            narrow,
            narrow,
            narrow,
            narrow,
            jax.ShapeDtypeStruct((8, width), f32),
            jax.ShapeDtypeStruct((1, ff), f32),
        ],
        grid=(rows // tile,),
        in_specs=[wide] * 3
        + [fixed(a) for a in (*wo, *wu, *wd)]
        + [fixed(vectors), fixed(b_up)],
        out_specs=[wide, hidden, hidden, wide, wide, wide, wide]
        + [pl.BlockSpec((8, width), lambda i: (0, 0)), pl.BlockSpec((1, ff), lambda i: (0, 0))],
        scratch_shapes=[VM((tile, ff), f32)],
        compiler_params=params(),
        name="rows",
    )(x, tokens, cotangent, *wo, *wu, *wd, vectors, b_up)


def one_back_kernel(per, pairs, held, k1_ref, og_ref, q_ref, lk_ref, gq_ref, chunk):
    item = pl.program_id(0)

    @pl.when(item == 0)
    def _():
        chunk[...] = jnp.zeros_like(chunk)

    for p in range(pairs):
        lanes = slice(p * PAIR, (p + 1) * PAIR)
        owner, place = owned_by(item * pairs + p, per)
        mixed = spread(held[owner, pl.ds(pl.multiple_of(place * MARKS, MARKS), MARKS), :])
        k1 = k1_ref[0, lanes, :]
        og = split(og_ref[0, :, lanes])
        part_mixed = compacted(dots(split(k1), og, 1, 0))
        grad = dots(split(mixed), og, 1, 1)
        scores = k1 * (grad - block_sum(k1 * grad))
        ss = split(scores)
        gq_ref[0, :, lanes] = dots(ss, split(spread(lk_ref[0, :, lanes])), 0, 0)
        part_key = compacted(dots(ss, split(q_ref[0, :, lanes]), 1, 0))
        chunk[owner, pl.ds(pl.multiple_of(place * 2 * MARKS, 2 * MARKS), MARKS), :] = part_mixed
        chunk[owner, pl.ds(pl.multiple_of(place * 2 * MARKS + MARKS, MARKS), MARKS), :] = part_key


def one_back_call(blocks, k1, og, q, lk, per, pairs):
    items, span, width = q.shape
    out = (blocks.shape[0], 2 * per * MARKS, PAIR)
    wide = per_item((span, width))
    return pl.pallas_call(
        functools.partial(one_back_kernel, per, pairs),
        out_shape=[
            jax.ShapeDtypeStruct((items, span, width), f32),
            jax.ShapeDtypeStruct(out, f32),
        ],
        grid=(items,),
        in_specs=[whole(blocks.shape), per_item((width, span)), wide, wide]
        + [per_item((MARKS, width))],
        out_specs=[wide, whole(out)],
        compiler_params=params(),
        name="one_back",
    )(blocks, k1, og, q, lk)


def conv_back_kernel(pairs, margin, og_ref, gl_ref, gr_ref, v_ref, vl_ref, vr_ref, use_ref, taps_ref, *refs):
    gv_ref, gtaps_ref, taps, gwin, vwin, acc = refs
    item = pl.program_id(0)
    span = v_ref.shape[1]
    window = PAIR + 2 * margin

    @pl.when(item == 0)
    def _():
        keep_taps(taps_ref, taps, 2 * pairs)
        acc[...] = jnp.zeros_like(acc)

    use = use_ref[0]
    keep_window(gwin, gl_ref[0, 0], og_ref[0], gr_ref[0, 0], margin, span)
    keep_window(vwin, vl_ref[0, 0], v_ref[0] * use, vr_ref[0, 0], margin, span)
    for p in range(pairs):
        lanes = slice(p * PAIR, (p + 1) * PAIR)
        for block in range(span // PAIR):
            rows = slice(block * PAIR, (block + 1) * PAIR)
            gv_ref[0, rows, lanes] = convolve(taps, gwin, p, block, window) * use[rows]
            inner = slice(margin + block * PAIR, margin + (block + 1) * PAIR)
            outer = slice(block * PAIR, block * PAIR + window)
            v = (vwin[0, outer, lanes], vwin[1, outer, lanes])
            low = lane_low((PAIR, PAIR))
            hi, lo = gwin[0, inner, lanes], gwin[1, inner, lanes]
            zero = jnp.zeros_like(hi)
            acc[2 * p] += dots((jnp.where(low, hi, zero), jnp.where(low, lo, zero)), v, 1, 1)
            acc[2 * p + 1] += dots((jnp.where(low, zero, hi), jnp.where(low, zero, lo)), v, 1, 1)

    @pl.when(item == pl.num_programs(0) - 1)
    def _():
        rows = lax.broadcasted_iota(jnp.int32, (PAIR, PAIR), 0)
        flip = (rows + lax.broadcasted_iota(jnp.int32, (PAIR, PAIR), 1) == PAIR - 1).astype(bf16)
        for h in range(2 * pairs):
            c = acc[h]
            c = jnp.concatenate([c, jnp.zeros((PAIR, 2 * PAIR - window), f32)], axis=1)
            hi = c.astype(bf16)
            rest = c - hi.astype(f32)
            mid = rest.astype(bf16)
            low = (rest - mid.astype(f32)).astype(bf16)
            c = dg(flip, hi, 1, 0) + dg(flip, mid, 1, 0) + dg(flip, low, 1, 0)
            c = pltpu.roll(c, 0, 1, stride=1, stride_axis=0)
            gtaps_ref[h : h + 1, :] = jnp.sum(c, axis=0, keepdims=True)


def conv_back_call(og, ghalos, v, vhalos, use_col, taps, pairs, margin):
    items, span, width = v.shape
    window = PAIR + 2 * margin
    wide, edge = per_item((span, width)), halo_specs(margin, width)
    rows = -(-2 * pairs // 8) * 8
    return pl.pallas_call(
        functools.partial(conv_back_kernel, pairs, margin),
        out_shape=[
            jax.ShapeDtypeStruct((items, span, width), f32),
            jax.ShapeDtypeStruct((rows, 2 * PAIR), f32),
        ],
        grid=(items,),
        in_specs=[wide, *edge, wide, *edge, per_item((span, 1)), whole(taps.shape)],
        out_specs=[wide, whole((rows, 2 * PAIR))],
        scratch_shapes=[
            VM((2, 2 * pairs, PAIR, 2 * PAIR), bf16),
            VM((2, span + 2 * margin, width), bf16),
            VM((2, span + 2 * margin, width), bf16),
            VM((2 * pairs, PAIR, window), f32),
        ],
        compiler_params=params(),
        name="conv_back",
    )(og, ghalos, ghalos, v, vhalos, vhalos, use_col, taps)


def exchange_back_kernel(n, per, chunk_ref, side_ref, ctx_ref, a_ref, z_ref, lq_ref, lk_ref,
                         out_ref, gq_ref, gk_ref, halo_ref, gm, gz, ga, *scratch):
    seat = Seat(n)
    reduce = Reduce(seat, chunk_ref, *scratch[:5])
    gather = Gather(seat, out_ref, *scratch[5:7])
    edges = Edges(seat, side_ref, *scratch[7:])
    seat.hello(True)
    reduce.start()
    edges.start()
    reduce.middle(add_all)
    diagonal = diagonal_mask()
    eye = unit()
    stats = per * MARKS
    gm[...] = reduce.finish(add_all)
    block = out_ref.at[seat.core, seat.z]
    block[stats:, :] = jnp.zeros((block.shape[0] - stats, PAIR), f32)
    for place in range(per):
        mixed = spread(gm[place * 2 * MARKS : place * 2 * MARKS + MARKS, :])
        context = spread(ctx_ref[place])
        grad = dot3(jnp.transpose(z_ref[NEWTON, place]), mixed)
        block[place * MARKS : (place + 1) * MARKS, :] = compacted(grad)
        dot = jnp.sum(grad * context, axis=1, keepdims=True)
        block[stats + place : stats + place + 1, :] = row_of(dot)
        gz[place] = jnp.where(diagonal, dot3(mixed, context, 1, 1), 0.0)
        ga[place] = jnp.zeros((PAIR, PAIR), f32)
    gather.start()

    def lap(back, _):
        step = NEWTON - 1 - back
        for place in range(per):
            a, z, g = a_ref[place], z_ref[step, place], 0.25 * gz[place]
            pr, n1, n2, n3 = newton_step(a, z, eye)
            back_three = dot3(jnp.transpose(z), g)
            turned = jnp.transpose(pr)
            back_two = -dot3(turned, back_three)
            back_one = -dot3(turned, back_two)
            grad = -dot3(back_three, n2, 1, 1) - dot3(back_two, n1, 1, 1) - back_one
            ga[place] += dot3(grad, z, 1, 1)
            gz[place] = dot3(g, n3, 1, 1) + dot3(jnp.transpose(a), grad)
        return 0

    lax.fori_loop(0, NEWTON - 1, lap, 0)
    gather.forward()
    lax.fori_loop(NEWTON - 1, NEWTON, lap, 0)
    for place in range(per):
        a, g = a_ref[place], jnp.transpose(gz[place])
        norm = head_total(a * a)
        slope = -head_total(g * a) / (norm * norm)
        grad = ga[place] + g / norm + 2.0 * slope * a
        scores = a * (grad - jnp.sum(a * grad, axis=1, keepdims=True))
        gq_ref[place] = compacted(dot3(scores, spread(lk_ref[place])))
        gk_ref[place] = gm[place * 2 * MARKS + MARKS : (place + 1) * 2 * MARKS, :] + compacted(
            dot3(jnp.transpose(scores), spread(lq_ref[place]))
        )
    edges.finish(halo_ref)
    gather.finish()


def exchange_back_call(chunks, sides, ctx, a, z, lq, lk, n, rows):
    per = ctx.shape[0]
    small = jax.ShapeDtypeStruct(ctx.shape, f32)
    chunk = chunks.shape[1:]
    blocks = (2, n // 2, rows, PAIR)
    out = pl.pallas_call(
        functools.partial(exchange_back_kernel, n, per),
        out_shape=[
            jax.ShapeDtypeStruct(blocks, f32),
            small,
            small,
            jax.ShapeDtypeStruct(sides.shape, f32),
        ],
        in_specs=[pl.BlockSpec(memory_space=VM)] * 7,
        out_specs=[pl.BlockSpec(memory_space=VM)] * 4,
        scratch_shapes=[VM(chunk, f32)]
        + [VM((per, PAIR, PAIR), f32)] * 2
        + Reduce.scratch(n, chunk)
        + Gather.scratch(n)
        + Edges.scratch(sides.shape),
        compiler_params=params(collective_id=2, has_side_effects=True),
        name="exchange_back",
    )(chunks.reshape((2, n // 2) + chunk), sides, ctx, a, z, lq, lk)
    return [out[0].reshape(n, rows, PAIR)] + list(out[1:])


def three_back_kernel(per, pairs, held, stat, w3_ref, top_ref, v_ref, k_ref, gvc_ref, lq_ref,
                      gv_ref, gk_ref, chunk):
    item = pl.program_id(0)
    stats = per * MARKS

    @pl.when(item == 0)
    def _():
        chunk[...] = jnp.zeros_like(chunk)

    for p in range(pairs):
        lanes = slice(p * PAIR, (p + 1) * PAIR)
        owner, place = owned_by(item * pairs + p, per)
        grad = split(spread(held[owner, pl.ds(pl.multiple_of(place * MARKS, MARKS), MARKS), :]))
        row_dot = column_of(held[owner, pl.ds(stats + place, 1), :])
        largest = stat[owner, pl.ds(stats + 2 * place, 1), :]
        total = stat[owner, pl.ds(stats + 2 * place + 1, 1), :]
        scale = column_of(jnp.exp(top_ref[0, p : p + 1, :] - largest) / total)
        k3 = w3_ref[0, lanes, :] * scale[:, 0:1]
        gk3 = dots(grad, split(v_ref[0, :, lanes]), 1, 1)
        scores = split(k3 * (gk3 - row_dot[:, 0:1]))
        gv_ref[0, :, lanes] = gvc_ref[0, :, lanes] + dots(split(k3), grad, 0, 0)
        gk_ref[0, :, lanes] = dots(scores, split(spread(lq_ref[0, :, lanes])), 0, 0)
        part = compacted(dots(scores, split(k_ref[0, :, lanes]), 1, 0))
        chunk[owner, pl.ds(pl.multiple_of(place * MARKS, MARKS), MARKS), :] = part


def three_back_call(grads, blocks, w3, top, v, k, gv_conv, lq, per, pairs):
    items, span, width = v.shape
    out = (blocks.shape[0], per * MARKS, PAIR)
    wide = per_item((span, width))
    shape = jax.ShapeDtypeStruct((items, span, width), f32)
    return pl.pallas_call(
        functools.partial(three_back_kernel, per, pairs),
        out_shape=[shape, shape, jax.ShapeDtypeStruct(out, f32)],
        grid=(items,),
        in_specs=[whole(blocks.shape)] * 2
        + [per_item((width, span)), per_item((8, PAIR)), wide, wide, wide]
        + [per_item((MARKS, width))],
        out_specs=[wide, wide, whole(out)],
        compiler_params=params(),
        name="three_back",
    )(grads, blocks, w3, top, v, k, gv_conv, lq)


def land_exchange_kernel(n, per, chunk_ref, q_ref, k_ref, out_ref, *scratch):
    seat = Seat(n)
    reduce = Reduce(seat, chunk_ref, *scratch[:5])
    gather = Gather(seat, out_ref, *scratch[5:])
    seat.hello(False)
    reduce.start()
    reduce.middle(add_all)
    half = per * MARKS
    block = out_ref.at[seat.core, seat.z]
    block[half:, :] = k_ref[...]
    block[:half, :] = q_ref[...] + reduce.finish(add_all)
    gather.start()
    gather.forward()
    gather.finish()


def land_exchange_call(chunks, own_q, own_k, n):
    per = own_q.shape[0]
    half = per * MARKS
    blocks = (2, n // 2, 2 * half, PAIR)
    return pl.pallas_call(
        functools.partial(land_exchange_kernel, n, per),
        out_shape=jax.ShapeDtypeStruct(blocks, f32),
        in_specs=[pl.BlockSpec(memory_space=VM)] * 3,
        out_specs=pl.BlockSpec(memory_space=VM),
        scratch_shapes=Reduce.scratch(n, (half, PAIR)) + Gather.scratch(n),
        compiler_params=params(collective_id=3, has_side_effects=True),
        name="land_exchange",
    )(chunks.reshape(2, n // 2, half, PAIR), own_q.reshape(half, PAIR), own_k.reshape(half, PAIR)).reshape(
        n, 2 * half, PAIR
    )


def land_back_kernel(per, pairs, factor, held, gq_ref, gk_ref, gv_ref, mem_ref, inv_ref, oq_ref, ok_ref, sums_ref):
    item = pl.program_id(0)
    half = per * MARKS

    @pl.when(item == 0)
    def _():
        sums_ref[...] = jnp.zeros_like(sums_ref)

    member = mem_ref[0].astype(bf16)
    inv = inv_ref[0]
    for p in range(pairs):
        lanes = slice(p * PAIR, (p + 1) * PAIR)
        slot, place = owned_by(item * pairs + p, per)
        for ref, out, base in ((gq_ref, oq_ref, 0), (gk_ref, ok_ref, half)):
            grad = held[slot, pl.ds(pl.multiple_of(base + place * MARKS, MARKS), MARKS), :]
            hi, lo = split(grad * inv)
            landed = dg(member, hi, 0, 0) + dg(member, lo, 0, 0)
            out[0, :, lanes] = (ref[0, :, lanes] + landed) * factor
        sums_ref[0:1, lanes] += jnp.sum(oq_ref[0, :, lanes], axis=0, keepdims=True)
        sums_ref[1:2, lanes] += jnp.sum(gv_ref[0, :, lanes], axis=0, keepdims=True)


def land_back_call(blocks, gq, gk, gv, member_t, inv, per, pairs, factor):
    items, span, width = gq.shape
    wide = per_item((span, width))
    shape = jax.ShapeDtypeStruct((items, span, width), f32)
    return pl.pallas_call(
        functools.partial(land_back_kernel, per, pairs, factor),
        out_shape=[shape, shape, jax.ShapeDtypeStruct((8, width), f32)],
        grid=(items,),
        in_specs=[whole(blocks.shape), wide, wide, wide]
        + [per_item((MARKS, span)), per_item((MARKS, PAIR))],
        out_specs=[wide, wide, whole((8, width))],
        compiler_params=params(),
        name="land_back",
    )(blocks, gq, gk, gv, member_t, inv)


def swap(x, axis, offset):
    count = lax.axis_size(axis)
    return lax.ppermute(x, axis, [(i, i ^ offset) for i in range(count)])


def both_sides(x, margin):
    return jnp.stack([x[:, :margin], x[:, -margin:]])


def bit_of(axis, bit):
    return lax.axis_index(axis) // bit % 2


def halve_rows(x, bit):
    blocks, rows, columns = x.shape
    y = x.reshape(blocks // 2, 2, rows, columns)
    mine = bit_of("seq", bit)
    keep = lax.dynamic_index_in_dim(y, mine, 1, False)
    send = lax.dynamic_index_in_dim(y, 1 - mine, 1, False)
    return keep + swap(send, "seq", bit)


def halve_columns(x, bits, bit):
    mine = bit_of("dp", bit)
    columns = x.shape[2]
    groups = 2 ** bits.index(bit)
    size = columns // (2 * groups)

    def pick(which):
        parts = [
            lax.dynamic_slice_in_dim(x, 2 * g * size + which * size, size, 2)
            for g in range(groups)
        ]
        return parts[0] if groups == 1 else jnp.concatenate(parts, axis=2)

    return pick(mine) + swap(pick(1 - mine), "dp", bit)


def powers(axis):
    count = lax.axis_size(axis)
    return [2**i for i in range(count.bit_length() - 1)]


def scatter_sum(x, order):
    seq_bits, dp_bits = powers("seq"), powers("dp")[::-1]
    count = lax.axis_size("seq")
    x = x.reshape(count, x.shape[0] // count, x.shape[1])
    x = halve_rows(x, seq_bits.pop(0))
    for axis in order:
        if axis == "z" and seq_bits:
            x = halve_rows(x, seq_bits.pop(0))
        elif axis in "xy" and dp_bits:
            half = len(powers("dp")) // 2
            low = [b for b in dp_bits if b < 2**half]
            high = [b for b in dp_bits if b >= 2**half]
            chosen = (low if axis == "x" else high) or dp_bits
            x = halve_columns(x, dp_bits, chosen[0])
            dp_bits.remove(chosen[0])
    while seq_bits:
        x = halve_rows(x, seq_bits.pop(0))
    while dp_bits:
        x = halve_columns(x, dp_bits, dp_bits[0])
        dp_bits.pop(0)
    return x[0]


def sum_everywhere(x):
    for axis in ("seq", "dp"):
        for bit in powers(axis):
            x = x + swap(x, axis, bit)
    return x


def rounded_pair(w):
    hi = lax.reduce_precision(w, 8, 7)
    return hi.astype(bf16), (w - hi).astype(bf16)


def product(a, b, ca, cb):
    return lax.dot_general(a, b, (((ca,), (cb,)), ((), ())), precision=HIGH)


def on_device(
    tokens,
    lengths,
    keep,
    w_query,
    b_query,
    w_key,
    w_value,
    b_value,
    conv_weight,
    w_out,
    b_out,
    gain_one,
    shift_one,
    w_up,
    b_up,
    w_down,
    b_down,
    gain_two,
    shift_two,
    cotangent,
):
    items, span, width = tokens.shape
    heads, taps = conv_weight.shape
    head_size = width // heads
    margin = taps // 2
    factor = head_size ** (-0.25)
    pairs = heads // 2
    n = lax.axis_size("seq")
    per = -(-items * pairs // n)
    chunk_rows = per * MARKS + 8
    position = lax.axis_index("seq") * span + jnp.arange(span, dtype=jnp.int32)
    inside = position[None, :] < lengths[:, None]
    usable = (inside & (keep > 0)).astype(f32)
    use_row, use_col = usable[:, None, :], usable[:, :, None]
    segment = jnp.where(inside, position[None, :] * MARKS // lengths[:, None], MARKS)
    marks = jnp.arange(MARKS, dtype=jnp.int32)
    member_t = (segment[:, None, :] == marks[None, :, None]).astype(f32) * use_row
    rows = tokens.reshape(items * span, width)
    taps_forward = jnp.pad(conv_weight, ((0, 4), (0, 2 * PAIR - taps)))
    taps_backward = jnp.pad(conv_weight[:, ::-1], ((0, 4), (0, 2 * PAIR - taps)))

    queries, key_rows, values, land_q, land_k, inverse_divisor = project_call(
        tokens, member_t, w_query, w_key, w_value, jnp.stack([b_query, b_value]), n, factor
    )
    k1, w3, top, chunks = scores_call(
        queries, key_rows, values, land_q, land_k, use_row, n, per, pairs, chunk_rows
    )
    use_sides = both_sides(use_col, margin)
    kernel_two, z, owned_q, owned_k, context, mixed, vhalos = exchange_call(
        chunks, land_q, land_k, both_sides(values, margin) * use_sides, n, per, pairs
    )
    attn_input = mix_call(mixed, k1, values, use_col, vhalos, taps_forward, per, pairs, margin)

    vectors = jnp.stack(
        [b_out, gain_one, shift_one, b_down, gain_two, shift_two, b_out, b_out]
    )
    x = attn_input.reshape(items * span, width)
    output, act, u, r2, hidden, r1, og, row_sums, up_sums = rows_call(
        x,
        rows,
        cotangent.reshape(items * span, width),
        rounded_pair(w_out),
        rounded_pair(w_up),
        rounded_pair(w_down),
        vectors,
        b_up[None, :],
    )
    og = og.reshape(items, span, width)
    grad_queries, chunks = one_back_call(mixed, k1, og, queries, land_k, per, pairs)
    grad_context, own_q, own_k, ghalos = exchange_back_call(
        chunks, both_sides(og, margin), context, kernel_two, z, owned_q, owned_k, n, chunk_rows
    )
    gv_conv, grad_taps = conv_back_call(
        og, ghalos, values, vhalos, use_col, taps_backward, pairs, margin
    )
    grad_values, grad_keys, chunks = three_back_call(
        grad_context, mixed, w3, top, values, key_rows, gv_conv, land_q, per, pairs
    )
    land_grads = land_exchange_call(chunks, own_q, own_k, n)
    grad_queries, grad_keys, late_sums = land_back_call(
        land_grads, grad_queries, grad_keys, grad_values, member_t, inverse_divisor,
        per, pairs, factor,
    )
    grad_w_down = scatter_sum(product(r2, act, 0, 0), "yxzz")
    grad_w_up = scatter_sum(product(u, hidden, 0, 0), "xzyz")
    grad_w_out = scatter_sum(product(r1, x, 0, 0), "zyxz")
    grad_queries = grad_queries.reshape(items * span, width)
    grad_keys = grad_keys.reshape(items * span, width)
    grad_values = grad_values.reshape(items * span, width)
    grad_w_value = scatter_sum(product(grad_values, rows, 0, 0), "zyxz")
    grad_w_query = scatter_sum(product(grad_queries, rows, 0, 0), "yxzz")
    grad_w_key = scatter_sum(product(grad_keys, rows, 0, 0), "xzyz")
    grad_tokens = (
        r1
        + product(grad_values, w_value, 1, 1)
        + product(grad_queries, w_query, 1, 1)
        + product(grad_keys, w_key, 1, 1)
    )

    early = sum_everywhere(
        jnp.concatenate([row_sums.reshape(-1), up_sums.reshape(-1), grad_taps.reshape(-1)]).reshape(
            -1, PAIR
        )
    ).reshape(-1)
    late = sum_everywhere(late_sums)
    row_sums = early[: 8 * width].reshape(8, width)
    ff = w_up.shape[1]
    up_sums = early[8 * width : 8 * width + ff]
    grad_taps = early[8 * width + ff :].reshape(-1, 2 * PAIR)
    grad_conv = grad_taps[:heads, PAIR - 1 : PAIR - 1 + taps]
    return (
        output.reshape(tokens.shape),
        grad_tokens.reshape(tokens.shape),
        grad_w_query.T,
        late[0],
        grad_w_key.T,
        grad_w_value.T,
        late[1],
        grad_conv,
        grad_w_out.T,
        row_sums[5],
        row_sums[3],
        row_sums[4],
        grad_w_up.T,
        up_sums,
        grad_w_down.T,
        row_sums[2],
        row_sums[0],
        row_sums[1],
    )


def solution(mesh):
    rows = P("dp", "seq", None)
    block = P("dp", "seq")
    in_specs = (rows, P("dp"), block) + (P(),) * 16 + (rows,)
    out_specs = (
        rows, rows, block, P(), block, block, P(), P(), block,
        P(), P(), P(), block, P(), block, P(), P(), P(),
    )
    return jax.shard_map(
        on_device, mesh=mesh, in_specs=in_specs, out_specs=out_specs, check_vma=False
    )
```

time: 754 us -> 747 us (level); the launches traced: 744 us -> 749 us
  Pallas kernels: 229 us -> 359 us
  starting transfers between devices: 120 us -> 39.8 us
  matrix products: 113 us -> 82.4 us
  waiting for transfers between devices: 148 us -> 136 us
  other arithmetic: 66.7 us -> 56.7 us
  local copies, waits for them, and re-layouts: 64.2 us -> 74.1 us
    pallas_call x9, Pallas kernels: 101 us -> 218 us  [the longest x1 47 us: exchange_back_call(): pl.pallas_call(functools.partial(exchange_back_kernel, n, per), out_shape...]
    ppermute x96 -> x40, starting transfers between devices: 112 us -> 39.8 us  [swap(): return lax.ppermute(x, axis, [(i, i ^ offset) for i in range(count)])]
    dot_general x14 -> x9, matrix products: 110 us -> 82.4 us  [product(): return lax.dot_general(a, b, (((ca,), (cb,)), ((), ())), precision=HIGH)]
    pallas_call x1, Pallas kernels: 110 us -> 124 us  [rows_call(): pl.pallas_call(functools.partial(rows_kernel, ff_tile), out_shape=[narrow...]
    ppermute x96 -> x40, waiting for transfers between devices: 148 us -> 136 us  [swap(): return lax.ppermute(x, axis, [(i, i ^ offset) for i in range(count)])]
    ppermute x4 -> x0, starting transfers between devices: 8.36 us -> none  [the longest x2 5.8 us: edges(): lax.ppermute(x[:, -margin:], 'seq', [(i, i + 1) for i in range(count - 1)])]
  transfers between devices with their start and end apart: 100 -> 40, of which waited for: 24 -> 15; matrix products, arithmetic and copies ran while one was open for 29% -> 19% of each run, Pallas kernels for 13% -> 19%
where the time goes in v2:
time: 747 us; the launch traced here: 749 us
  Pallas kernels  359 us (48%)
  waiting for transfers between devices  136 us (18%)
  matrix products  82.4 us (11%)
  local copies, waits for them, and re-layouts  74.1 us (10%)
  other arithmetic  56.7 us (8%)
  starting transfers between devices  39.8 us (5%)
    ppermute x40, waiting for transfers between devices, swap(): return lax.ppermute(x, axis, [(i, i ^ offset) for i in range(count)])  136 us
    pallas_call x1, Pallas kernels, rows_call(): pl.pallas_call(functools.partial(rows_kernel, ff_tile), out_shape=[narrow...  124 us
    dot_general x9, matrix products, product(): return lax.dot_general(a, b, (((ca,), (cb,)), ((), ())), precision=HIGH)  82.4 us
    pallas_call x1, Pallas kernels, exchange_back_call(): pl.pallas_call(functools.partial(exchange_back_kernel, n, per), out_shape...  47 us
    pallas_call x1, Pallas kernels, project_call(): pl.pallas_call(functools.partial(project_kernel, n, items, factor), out_s...  41.5 us
    ppermute x40, starting transfers between devices, swap(): return lax.ppermute(x, axis, [(i, i ^ offset) for i in range(count)])  39.8 us
    pallas_call x1, Pallas kernels, land_exchange_call(): pl.pallas_call(functools.partial(land_exchange_kernel, n, per), out_shape...  39.1 us
    pallas_call x1, Pallas kernels, exchange_call(): pl.pallas_call(functools.partial(exchange_kernel, n, per, pairs), out_sha...  30.4 us
  transfers between devices with their start and end apart: 40, of which 15 were waited for; matrix products, arithmetic and copies ran while one was open for 19% of the time, Pallas kernels for 19%

profile of v2, /device:TPU:0, one launch (start us, length us, event | category | flops | bytes accessed | tf_op | source)
XLA Modules:
  0.0 749.4 jit_solution(15634269168868057150)
XLA Ops:
  8.8 41.5 %project.1 = (f32[4,256,768]{2,1,0:T(8,128)}, f32[4,256,768]{2,1,0:T(8,128)}, f32[4,256,768]{2,1,0:T(8,128)}, f32[4,64,768]{2,1,0:T(8,128)}, f32[4,64,768]{2,1,0:T(8,128)}, /*index=5*/f32[4,64,128]{2,1,0:T(8,128)}) custom-call(f32[4,256,768]{2,1,0:T(8,128)} %tok_ref.1, f32[4,64,256]{2,1,0:T(8,128)} %fusion.3.mem_ref, f32[768,768]{1,0:T(8,128)} %wq_ref.1, ...), custom_call_target="tpu_custom_call" | custom-call | tf_op jit(solution)/shard_map/project/pallas_call | solution.py:295
  51.5 9.0 %fusion.1 = (bf16[3072,768]{1,0:T(8,128)(2,1)}, bf16[3072,768]{1,0:T(8,128)(2,1)}) fusion(f32[3072,768]{1,0:T(8,128)} %param.35), kind=kLoop, calls=%fused_computation.5 | loop fusion | flops 9437184 | bytes 18874368 | tf_op jit(solution)/shard_map/convert_element_type | solution.py:1089
  60.5 5.7 fusion
  66.3 3.5 fusion.2
  74.1 12.8 %scores.1 = (f32[4,768,256]{2,1,0:T(8,128)}, f32[4,768,256]{2,1,0:T(8,128)}, f32[4,8,128]{2,1,0:T(8,128)}, f32[8,200,128]{2,1,0:T(8,128)}) custom-call(f32[4,256,768]{2,1,0:T(8,128)} %get-tuple-element.58.q_ref, f32[4,256,768]{2,1,0:T(8,128)} %get-tuple-element.59.k_ref, f32[4,256,768]{2,1,0:T(8,128)} %get-tuple-element.60.v_ref, ...), custom_call_target="tpu_custom_call" | custom-call | tf_op jit(solution)/shard_map/scores/pallas_call | solution.py:345
  87.0 30.4 %exchange.1 = (f32[3,128,128]{2,1,0:T(8,128)}, f32[7,3,128,128]{3,2,1,0:T(8,128)}, f32[3,64,128]{2,1,0:T(8,128)}, f32[3,64,128]{2,1,0:T(8,128)}, f32[3,64,128]{2...) custom-call(f32[2,4,200,128]{3,2,1,0:T(8,128)} %bitcast.223, ...), custom_call_target="tpu_custom_call" | custom-call | tf_op jit(solution)/shard_map/exchange/pallas_call | solution.py:459
  118.6 10.7 %mix.1 = f32[4,256,768]{2,1,0:T(8,128)} custom-call(f32[8,200,128]{2,1,0:T(8,128)} %bitcast.206, f32[4,768,256]{2,1,0:T(8,128)} %get-tuple-element.65.k1_ref, f32[4,256,768]{2,1,0:T(8,128)} %get-tuple-element.60.v_ref, f32[4,256,1]{2,1,0:T(8,128)} %copy.60.use_ref, f32[2,4,16,768]{3,2,1,0:T(8,128)} %get-tuple-element.66.left_ref.right_ref.vl_ref.vr_ref, ...), custom_call_target="tpu_custom_call" | custom-call | tf_op jit(solution)/shard_map/mix/pallas_call | solution.py:549
  130.8 123.5 %rows.1 = (f32[1024,768]{1,0:T(8,128)}, f32[1024,3072]{1,0:T(8,128)}, f32[1024,3072]{1,0:T(8,128)}, f32[1024,768]{1,0:T(8,128)}, f32[1024,768]{1,0:T(8,128)}, /*...) custom-call(f32[1024,768]{1,0:T(8,128)} %bitcast.178, f32[1024,768]{1,0:T(8,128)} %bitcast.174, ...), custom_call_target="tpu_custom_call" | custom-call | tf_op jit(solution)/shard_map/rows/pallas_call | solution.py:679
  254.4 22.1 %fusion.14 = f32[3072,768]{1,0:T(8,128)S(1)} fusion(f32[1024,3072]{1,0:T(8,128)} %get-tuple-element.94, f32[1024,768]{1,0:T(8,128)} %get-tuple-element.95), kind=kOutput, calls=%fused_computation.116 | convolution fusion | flops 14495514624 | bytes 25165824 | tf_op jit(solution)/shard_map/dot_general | solution.py:1093
  276.5 2.7 dynamic-slice_bitcast_fusion.1
  279.1 2.3 copy-done.9
  281.8 3.7 copy.65
  285.5 5.9 fusion.13
  296.0 13.0 %one_back.1 = (f32[4,256,768]{2,1,0:T(8,128)}, f32[8,384,128]{2,1,0:T(8,128)}) custom-call(f32[8,200,128]{2,1,0:T(8,128)} %bitcast.207, f32[4,768,256]{2,1,0:T(8,128)} %get-tuple-element.65.k1_ref, f32[4,256,768]{2,1,0:T(8,128)} %bitcast.183, f32[4,256,768]{2,1,0:T(8,128)} %get-tuple-element.58.q_ref, f32[4,64,768]{2,1,0:T(8,128)} %get-tuple-element.62.lk_ref), custom_call_target="tpu_custom_call" | custom-call | tf_op jit(solution)/shard_map/one_back/pallas_call | solution.py:731
  312.1 47.0 %exchange_back.1 = (f32[2,4,200,128]{3,2,1,0:T(8,128)}, f32[3,64,128]{2,1,0:T(8,128)}, f32[3,64,128]{2,1,0:T(8,128)}, f32[2,4,16,768]{3,2,1,0:T(8,128)}) custom-call(f32[2,4,384,128]{3,2,1,0:T(8,128)} %bitcast.220, f32[2,4,16,768]{3,2,1,0:T(8,128)} %pad_maximum_fusion.2.side_ref, f32[3,64,128]{2,1,0:T(8,128)} %get-tuple-element.71.ctx_ref, ...), custom_call_target="tpu_custom_call" | custom-call | tf_op jit(solution)/shard_map/exchange_back/pallas_call | solution.py:878
  359.1 17.5 %conv_back.1 = (f32[4,256,768]{2,1,0:T(8,128)}, f32[16,256]{1,0:T(8,128)}) custom-call(f32[4,256,768]{2,1,0:T(8,128)} %bitcast.184, f32[2,4,16,768]{3,2,1,0:T(8,128)} %get-tuple-element.79.gl_ref.gr_ref, f32[2,4,16,768]{3,2,1,0:T(8,128)} %get-tuple-element.79.gl_ref.gr_ref, f32[4,256,768]{2,1,0:T(8,128)} %get-tuple-element.60.v_ref, ...), custom_call_target="tpu_custom_call" | custom-call | tf_op jit(solution)/shard_map/conv_back/pallas_call | solution.py:795
  380.1 14.7 %three_back.1 = (f32[4,256,768]{2,1,0:T(8,128)}, f32[4,256,768]{2,1,0:T(8,128)}, f32[8,192,128]{2,1,0:T(8,128)}) custom-call(f32[8,200,128]{2,1,0:T(8,128)} %bitcast.224, f32[8,200,128]{2,1,0:T(8,128)} %bitcast.208, f32[4,768,256]{2,1,0:T(8,128)} %get-tuple-element.77.w3_ref, f32[4,8,128]{2,1,0:T(8,128)} %get-tuple-element.78.top_ref, ...), custom_call_target="tpu_custom_call" | custom-call | tf_op jit(solution)/shard_map/three_back/pallas_call | solution.py:930
  394.8 3.7 copy.64
  398.5 5.9 fusion.12
  407.5 39.1 %land_exchange.1 = f32[2,4,384,128]{3,2,1,0:T(8,128)} custom-call(f32[2,4,192,128]{3,2,1,0:T(8,128)} %bitcast.225, f32[192,128]{1,0:T(8,128)} %bitcast.232, f32[192,128]{1,0:T(8,128)} %bitcast.233), custom_call_target="tpu_custom_call" | custom-call | tf_op jit(solution)/shard_map/land_exchange/pallas_call | solution.py:963
  446.6 8.4 %land_back.1 = (f32[4,256,768]{2,1,0:T(8,128)}, f32[4,256,768]{2,1,0:T(8,128)}, f32[8,768]{1,0:T(8,128)}) custom-call(f32[8,384,128]{2,1,0:T(8,128)} %bitcast.209, f32[4,256,768]{2,1,0:T(8,128)} %get-tuple-element.85.gq_ref, f32[4,256,768]{2,1,0:T(8,128)} %get-tuple-element.86.gk_ref, f32[4,256,768]{2,1,0:T(8,128)} %get-tuple-element.81.gv_ref, ...), custom_call_target="tpu_custom_call" | custom-call | tf_op jit(solution)/shard_map/land_back/pallas_call | solution.py:1002
  455.4 3.9 copy.63
  459.4 5.9 fusion.9
  465.3 4.1 fusion.8
  469.5 20.9 %fusion.15 = f32[768,3072]{1,0:T(8,128)} fusion(f32[1024,768]{1,0:T(8,128)S(1)} %copy-done.43, f32[1024,3072]{1,0:T(8,128)} %get-tuple-element.97), kind=kOutput, calls=%fused_computation.117 | convolution fusion | flops 14495514624 | bytes 25165824 | tf_op jit(solution)/shard_map/dot_general | solution.py:1093
  490.4 6.2 add_add_fusion
  496.6 5.5 fusion.11
  502.1 3.7 copy.62
  505.9 4.0 collective-permute-start.6
  509.9 5.9 fusion.10
  515.8 3.7 collective-permute-start.7
  520.4 5.2 dynamic-slice_bitcast_fusion
  558.1 8.9 %collective-permute-done.26 = f32[2,96,768]{2,1,0:T(8,128)S(1)} collective-permute-done((f32[2,96,768]{2,1,0:T(8,128)S(1)}, f32[2,96,768]{2,1,0:T(8,128)S(1)}, u32[]{:S(2)}, u32[]{:S(2)}) %collective-permute-start.26) | collective-permute-done | bytes 589856 | tf_op jit(solution)/shard_map/ppermute | solution.py:1016
  568.7 10.3 %collective-permute-done.16 = f32[2,96,768]{2,1,0:T(8,128)S(1)} collective-permute-done((f32[2,96,768]{2,1,0:T(8,128)S(1)}, f32[2,96,768]{2,1,0:T(8,128)S(1)}, u32[]{:S(2)}, u32[]{:S(2)}) %collective-permute-start.16) | collective-permute-done | bytes 589856 | tf_op jit(solution)/shard_map/ppermute | solution.py:1016
  584.9 4.1 collective-permute-done.27
  589.6 4.0 collective-permute-done.17
  594.3 3.1 bitcast_add_fusion.1
  602.6 3.1 bitcast_add_fusion
  613.0 43.9 %collective-permute-done.18 = f32[2,96,192]{2,1,0:T(8,128)S(1)} collective-permute-done((f32[2,96,192]{2,1,0:T(8,128)S(1)}, f32[2,96,192]{2,1,0:T(8,128)S(1)}, u32[]{:S(2)}, u32[]{:S(2)}) %collective-permute-start.18) | collective-permute-done | bytes 147488 | tf_op jit(solution)/shard_map/ppermute | solution.py:1016
  657.3 4.2 collective-permute-done.13
  662.7 2.6 collective-permute-start.14
  671.5 25.4 %collective-permute-done.32 = f32[2,384,384]{2,1,0:T(8,128)S(1)} collective-permute-done((f32[2,384,384]{2,1,0:T(8,128)S(1)}, f32[2,384,384]{2,1,0:T(8,128)S(1)}, u32[]{:S(2)}, u32[]{:S(2)}) %collective-permute-start.32) | collective-permute-done | bytes 1179680 | tf_op jit(solution)/shard_map/ppermute | solution.py:1016
  698.2 2.2 copy.66
  707.0 7.4 collective-permute-done.33
  714.3 2.2 copy.67
  720.1 2.9 collective-permute-start.39
  726.9 15.3 %collective-permute-done.34 = f32[1,384,192]{2,1,0:T(8,128)S(1)} collective-permute-done((f32[1,384,192]{2,1,0:T(8,128)}, f32[1,384,192]{2,1,0:T(8,128)S(1)}, u32[]{:S(2)}, u32[]{:S(2)}) %collective-permute-start.34) | collective-permute-done | bytes 294944 | tf_op jit(solution)/shard_map/ppermute | solution.py:1016
  743.1 5.3 collective-permute-done.39
  (284 shorter events, 110.3 us)
Async XLA Ops:
  281.5 312.8 %collective-permute-start.30 = (f32[4,384,768]{2,1,0:T(8,128)}, f32[4,384,768]{2,1,0:T(8,128)}, u32[]{:S(2)}, u32[]{:S(2)}) collective-permute-start(f32[4,384,768]{2,1,0:T(8,128)} %dynamic-slice_bitcast_fusion.1), channel_id=1, source_target_pairs={{0,1},{1,0},{2,3},{3,2},{4,5},{5,4},{6,7},{7,6},{8,9},{9,8},{10,11... | collective-permute-start | bytes 14155784 | tf_op jit(solution)/shard_map/ppermute | solution.py:1016
  294.0 254.6 %collective-permute-start.25 = (f32[4,96,768]{2,1,0:T(8,128)}, f32[4,96,768]{2,1,0:T(8,128)}, u32[]{:S(2)}, u32[]{:S(2)}) collective-permute-start(f32[4,96,768]{2,1,0:T(8,128)} %dynamic-slice_bitcast_fusion.3), channel_id=1, source_target_pairs={{0,1},{1,0},{2,3},{3,2},{4,5},{5,4},{6,7},{7,6},{8,9},{9,8},{10,11... | collective-permute-start | bytes 3538952 | tf_op jit(solution)/shard_map/ppermute | solution.py:1016
  380.1 139.4 %collective-permute-start.20 = (f32[104,128]{1,0:T(8,128)}, f32[104,128]{1,0:T(8,128)}, u32[]{:S(2)}, u32[]{:S(2)}) collective-permute-start(f32[104,128]{1,0:T(8,128)} %maximum_bitcast_fusion), channel_id=1, source_target_pairs={{0,1},{1,0},{2,3},{3,2},{4,5},{5,4},{6,7},{7,6},{8,9},{9,8},{10,11... | collective-permute-start | bytes 159752 | tf_op jit(solution)/shard_map/ppermute | solution.py:1016
  407.0 143.8 %collective-permute-start.15 = (f32[4,96,768]{2,1,0:T(8,128)}, f32[4,96,768]{2,1,0:T(8,128)}, u32[]{:S(2)}, u32[]{:S(2)}) collective-permute-start(f32[4,96,768]{2,1,0:T(8,128)} %dynamic-slice_bitcast_fusion.4), channel_id=1, source_target_pairs={{0,1},{1,0},{2,3},{3,2},{4,5},{5,4},{6,7},{7,6},{8,9},{9,8},{10,11... | collective-permute-start | bytes 3538952 | tf_op jit(solution)/shard_map/ppermute | solution.py:1016
  455.0 50.8 %collective-permute-start.5 = (f32[8,768]{1,0:T(8,128)}, f32[8,768]{1,0:T(8,128)S(1)}, u32[]{:S(2)}, u32[]{:S(2)}) collective-permute-start(f32[8,768]{1,0:T(8,128)} %get-tuple-element.90), channel_id=1, source_target_pairs={{0,1},{1,0},{2,3},{3,2},{4,5},{5,4},{6,7},{7,6},{8,9},{9,8},{10,11... | collective-permute-start | bytes 73736 | tf_op jit(solution)/shard_map/ppermute | solution.py:1016
  469.4 21.0 %copy-start.6 = (f32[1024,768]{1,0:T(8,128)S(1)}, f32[1024,768]{1,0:T(8,128)}, u32[]{:S(2)}) copy-start(f32[1024,768]{1,0:T(8,128)} %get-tuple-element.68) | copy-start | bytes 9437188
  469.4 21.0 %copy-start.7 = (f32[4,256,768]{2,1,0:T(8,128)S(1)}, f32[4,256,768]{2,1,0:T(8,128)}, u32[]{:S(2)}) copy-start(f32[4,256,768]{2,1,0:T(8,128)} %get-tuple-element.89) | copy-start | bytes 9437188
  469.4 21.0 %copy-start.8 = (f32[768,768]{1,0:T(8,128)S(1)}, f32[768,768]{1,0:T(8,128)}, u32[]{:S(2)}) copy-start(f32[768,768]{1,0:T(8,128)} %wk_ref.1) | copy-start | bytes 7077892
  505.9 9.9 %collective-permute-start.6 = (f32[8,768]{1,0:T(8,128)S(1)}, f32[8,768]{1,0:T(8,128)S(1)}, u32[]{:S(2)}, u32[]{:S(2)}) collective-permute-start(f32[8,768]{1,0:T(8,128)S(1)} %add.350), channel_id=1, source_target_pairs={{0,2},{1,3},{2,0},{3,1},{4,6},{5,7},{6,4},{7,5},{8,10},{9,11},{10,... | collective-permute-start | bytes 73736 | tf_op jit(solution)/shard_map/ppermute | solution.py:1016
  515.8 9.8 %collective-permute-start.7 = (f32[8,768]{1,0:T(8,128)S(1)}, f32[8,768]{1,0:T(8,128)S(1)}, u32[]{:S(2)}, u32[]{:S(2)}) collective-permute-start(f32[8,768]{1,0:T(8,128)S(1)} %add.351), channel_id=1, source_target_pairs={{0,4},{1,5},{2,6},{3,7},{4,0},{5,1},{6,2},{7,3},{8,12},{9,13},{10,... | collective-permute-start | bytes 73736 | tf_op jit(solution)/shard_map/ppermute | solution.py:1016
  520.3 6.8 collective-permute-start.21
  525.6 3.9 collective-permute-start.8
  528.0 21.2 %copy-start.11 = (f32[4,2,96,768]{3,2,1,0:T(8,128)S(1)}, f32[4,2,96,768]{3,2,1,0:T(8,128)}, u32[]{:S(2)}) copy-start(f32[4,2,96,768]{3,2,1,0:T(8,128)} %copy-done.10) | copy-start | bytes 7077892
  528.0 5.1 collective-permute-start.22
  530.1 5.3 collective-permute-start.9
  533.8 4.5 collective-permute-start.23
  535.4 67.2 %collective-permute-start.35 = (f32[4,96,3072]{2,1,0:T(8,128)}, f32[4,96,3072]{2,1,0:T(8,128)}, u32[]{:S(2)}, u32[]{:S(2)}) collective-permute-start(f32[4,96,3072]{2,1,0:T(8,128)} %dynamic-slice_bitcast_fusion), channel_id=1, source_target_pairs={{0,1},{1,0},{2,3},{3,2},{4,5},{5,4},{6,7},{7,6},{8,9},{9,8},{10,11... | collective-permute-start | bytes 14155784 | tf_op jit(solution)/shard_map/ppermute | solution.py:1016
  539.1 4.2 collective-permute-start.24
  543.3 11.0 %collective-permute-start.10 = (f32[4,96,768]{2,1,0:T(8,128)S(1)}, f32[4,96,768]{2,1,0:T(8,128)}, u32[]{:S(2)}, u32[]{:S(2)}) collective-permute-start(f32[4,96,768]{2,1,0:T(8,128)S(1)} %dynamic-slice_bitcast_fusion.5), channel_id=1, source_target_pairs={{0,1},{1,0},{2,3},{3,2},{4,5},{5,4},{6,7},{7,6},{8,9},{9,8},{10,11... | collective-permute-start | bytes 3538952 | tf_op jit(solution)/shard_map/ppermute | solution.py:1016
  548.6 8.2 %collective-permute-start = (f32[4,96,768]{2,1,0:T(8,128)}, f32[4,96,768]{2,1,0:T(8,128)S(1)}, u32[]{:S(2)}, u32[]{:S(2)}) collective-permute-start(f32[4,96,768]{2,1,0:T(8,128)} %dynamic-slice_bitcast_fusion.6), channel_id=1, source_target_pairs={{0,1},{1,0},{2,3},{3,2},{4,5},{5,4},{6,7},{7,6},{8,9},{9,8},{10,11... | collective-permute-start | bytes 3538952 | tf_op jit(solution)/shard_map/ppermute | solution.py:1016
  550.8 16.2 %collective-permute-start.26 = (f32[2,96,768]{2,1,0:T(8,128)S(1)}, f32[2,96,768]{2,1,0:T(8,128)S(1)}, u32[]{:S(2)}, u32[]{:S(2)}) collective-permute-start(f32[2,96,768]{2,1,0:T(8,128)S(1)} %dynamic-slice_bitcast_fusion.8), channel_id=1, source_target_pairs={{0,2},{1,3},{2,0},{3,1},{4,6},{5,7},{6,4},{7,5},{8,10},{9,11},{10,... | collective-permute-start | bytes 1769480 | tf_op jit(solution)/shard_map/ppermute | solution.py:1016
  554.3 24.7 %collective-permute-start.16 = (f32[2,96,768]{2,1,0:T(8,128)S(1)}, f32[2,96,768]{2,1,0:T(8,128)S(1)}, u32[]{:S(2)}, u32[]{:S(2)}) collective-permute-start(f32[2,96,768]{2,1,0:T(8,128)S(1)} %dynamic-slice_bitcast_fusion.9), channel_id=1, source_target_pairs={{0,2},{1,3},{2,0},{3,1},{4,6},{5,7},{6,4},{7,5},{8,10},{9,11},{10,... | collective-permute-start | bytes 1769480 | tf_op jit(solution)/shard_map/ppermute | solution.py:1016
  554.6 39.6 %slice-start.3 = ((s8[9437184]{0:T(1024)(128)(4,1)}), s8[4194304]{0:T(1024)(128)(4,1)S(1)}, s32[]{:S(2)}) async-start(s8[9437184]{0:T(1024)(128)(4,1)} %bitcast.197), calls=%async_computation.3 | async-start | bytes 8388608
  556.9 37.4 %slice-start.4 = ((s8[9437184]{0:T(1024)(128)(4,1)}), s8[4194304]{0:T(1024)(128)(4,1)S(1)}, s32[]{:S(2)}) async-start(s8[9437184]{0:T(1024)(128)(4,1)} %bitcast.197), calls=%async_computation.4 | async-start | bytes 8388608
  556.9 23.7 %collective-permute-start.11 = (f32[4,96,384]{2,1,0:T(8,128)S(1)}, f32[4,96,384]{2,1,0:T(8,128)S(1)}, u32[]{:S(2)}, u32[]{:S(2)}) collective-permute-start(f32[4,96,384]{2,1,0:T(8,128)S(1)} %pad_maximum_fusion.1), channel_id=1, source_target_pairs={{0,8},{8,0},{16,24},{24,16},{1,9},{9,1},{17,25},{25,17},{2,10},{10... | collective-permute-start | bytes 1769480 | tf_op jit(solution)/shard_map/ppermute | solution.py:1016
  567.0 15.1 %collective-permute-start.1 = (f32[4,96,384]{2,1,0:T(8,128)S(1)}, f32[4,96,384]{2,1,0:T(8,128)S(1)}, u32[]{:S(2)}, u32[]{:S(2)}) collective-permute-start(f32[4,96,384]{2,1,0:T(8,128)S(1)} %constant_dynamic-slice_fusion.23), channel_id=1, source_target_pairs={{0,16},{8,24},{16,0},{24,8},{1,17},{9,25},{17,1},{25,9},{2,18},{10... | collective-permute-start | bytes 1769480 | tf_op jit(solution)/shard_map/ppermute | solution.py:1016
  568.7 25.6 %slice-start.5 = ((s8[9437184]{0:T(1024)(128)(4,1)}), s8[1048576]{0:T(1024)(128)(4,1)S(1)}, s32[]{:S(2)}) async-start(s8[9437184]{0:T(1024)(128)(4,1)} %bitcast.197), calls=%async_computation.5 | async-start | bytes 2097152
  579.0 9.9 %collective-permute-start.27 = (f32[2,96,384]{2,1,0:T(8,128)S(1)}, f32[2,96,384]{2,1,0:T(8,128)S(1)}, u32[]{:S(2)}, u32[]{:S(2)}) collective-permute-start(f32[2,96,384]{2,1,0:T(8,128)S(1)} %constant_dynamic-slice_fusion.11), channel_id=1, source_target_pairs={{0,16},{8,24},{16,0},{24,8},{1,17},{9,25},{17,1},{25,9},{2,18},{10... | collective-permute-start | bytes 884744 | tf_op jit(solution)/shard_map/ppermute | solution.py:1016
  580.6 13.0 %collective-permute-start.17 = (f32[2,96,384]{2,1,0:T(8,128)S(1)}, f32[2,96,384]{2,1,0:T(8,128)S(1)}, u32[]{:S(2)}, u32[]{:S(2)}) collective-permute-start(f32[2,96,384]{2,1,0:T(8,128)S(1)} %constant_dynamic-slice_fusion.14), channel_id=1, source_target_pairs={{0,16},{8,24},{16,0},{24,8},{1,17},{9,25},{17,1},{25,9},{2,18},{10... | collective-permute-start | bytes 884744 | tf_op jit(solution)/shard_map/ppermute | solution.py:1016
  582.1 25.8 %collective-permute-start.12 = (f32[2,96,384]{2,1,0:T(8,128)}, f32[2,96,384]{2,1,0:T(8,128)}, u32[]{:S(2)}, u32[]{:S(2)}) collective-permute-start(f32[2,96,384]{2,1,0:T(8,128)} %dynamic-slice_bitcast_fusion.10), channel_id=1, source_target_pairs={{0,2},{1,3},{2,0},{3,1},{4,6},{5,7},{6,4},{7,5},{8,10},{9,11},{10,... | collective-permute-start | bytes 884744 | tf_op jit(solution)/shard_map/ppermute | solution.py:1016
  588.9 20.7 %collective-permute-start.2 = (f32[4,96,192]{2,1,0:T(8,128)}, f32[4,96,192]{2,1,0:T(8,128)S(1)}, u32[]{:S(2)}, u32[]{:S(2)}) collective-permute-start(f32[4,96,192]{2,1,0:T(8,128)} %constant_dynamic-slice_fusion.22), channel_id=1, source_target_pairs={{0,8},{8,0},{16,24},{24,16},{1,9},{9,1},{17,25},{25,17},{2,10},{10... | collective-permute-start | bytes 884744 | tf_op jit(solution)/shard_map/ppermute | solution.py:1016
  593.7 16.7 %collective-permute-start.28 = (f32[2,96,192]{2,1,0:T(8,128)S(1)}, f32[2,96,192]{2,1,0:T(8,128)}, u32[]{:S(2)}, u32[]{:S(2)}) collective-permute-start(f32[2,96,192]{2,1,0:T(8,128)S(1)} %constant_dynamic-slice_fusion.10), channel_id=1, source_target_pairs={{0,8},{8,0},{16,24},{24,16},{1,9},{9,1},{17,25},{25,17},{2,10},{10... | collective-permute-start | bytes 442376 | tf_op jit(solution)/shard_map/ppermute | solution.py:1016
  601.1 61.6 %collective-permute-start.31 = (f32[4,384,384]{2,1,0:T(8,128)}, f32[4,384,384]{2,1,0:T(8,128)S(1)}, u32[]{:S(2)}, u32[]{:S(2)}) collective-permute-start(f32[4,384,384]{2,1,0:T(8,128)} %pad_maximum_fusion), channel_id=1, source_target_pairs={{0,8},{8,0},{16,24},{24,16},{1,9},{9,1},{17,25},{25,17},{2,10},{10... | collective-permute-start | bytes 7077896 | tf_op jit(solution)/shard_map/ppermute | solution.py:1016
  606.2 59.7 %collective-permute-start.36 = (f32[4,96,1536]{2,1,0:T(8,128)S(1)}, f32[4,96,1536]{2,1,0:T(8,128)S(1)}, u32[]{:S(2)}, u32[]{:S(2)}) collective-permute-start(f32[4,96,1536]{2,1,0:T(8,128)S(1)} %constant_dynamic-slice_fusion.2), channel_id=1, source_target_pairs={{0,16},{8,24},{16,0},{24,8},{1,17},{9,25},{17,1},{25,9},{2,18},{10... | collective-permute-start | bytes 7077896 | tf_op jit(solution)/shard_map/ppermute | solution.py:1016
  607.9 49.0 %collective-permute-start.18 = (f32[2,96,192]{2,1,0:T(8,128)S(1)}, f32[2,96,192]{2,1,0:T(8,128)S(1)}, u32[]{:S(2)}, u32[]{:S(2)}) collective-permute-start(f32[2,96,192]{2,1,0:T(8,128)S(1)} %constant_dynamic-slice_fusion.13), channel_id=1, source_target_pairs={{0,8},{8,0},{16,24},{24,16},{1,9},{9,1},{17,25},{25,17},{2,10},{10... | collective-permute-start | bytes 442376 | tf_op jit(solution)/shard_map/ppermute | solution.py:1016
  609.6 51.9 %collective-permute-start.13 = (f32[2,96,192]{2,1,0:T(8,128)S(1)}, f32[2,96,192]{2,1,0:T(8,128)S(1)}, u32[]{:S(2)}, u32[]{:S(2)}) collective-permute-start(f32[2,96,192]{2,1,0:T(8,128)S(1)} %constant_dynamic-slice_fusion.16), channel_id=1, source_target_pairs={{0,16},{8,24},{16,0},{24,8},{1,17},{9,25},{17,1},{25,9},{2,18},{10... | collective-permute-start | bytes 442376 | tf_op jit(solution)/shard_map/ppermute | solution.py:1016
  610.4 58.4 %collective-permute-start.3 = (f32[2,96,192]{2,1,0:T(8,128)S(1)}, f32[2,96,192]{2,1,0:T(8,128)S(1)}, u32[]{:S(2)}, u32[]{:S(2)}) collective-permute-start(f32[2,96,192]{2,1,0:T(8,128)S(1)} %dynamic-slice_bitcast_fusion.11), channel_id=1, source_target_pairs={{0,2},{1,3},{2,0},{3,1},{4,6},{5,7},{6,4},{7,5},{8,10},{9,11},{10,... | collective-permute-start | bytes 442376 | tf_op jit(solution)/shard_map/ppermute | solution.py:1016
  656.9 13.1 %collective-permute-start.29 = (f32[1,96,192]{2,1,0:T(8,128)S(1)}, f32[1,96,192]{2,1,0:T(8,128)S(1)}, u32[]{:S(2)}, u32[]{:S(2)}) collective-permute-start(f32[1,96,192]{2,1,0:T(8,128)S(1)} %constant_dynamic-slice_fusion.9), channel_id=1, source_target_pairs={{0,4},{1,5},{2,6},{3,7},{4,0},{5,1},{6,2},{7,3},{8,12},{9,13},{10,... | collective-permute-start | bytes 221192 | tf_op jit(solution)/shard_map/ppermute | solution.py:1016
  661.5 9.3 %collective-permute-start.19 = (f32[1,96,192]{2,1,0:T(8,128)S(1)}, f32[1,96,192]{2,1,0:T(8,128)S(1)}, u32[]{:S(2)}, u32[]{:S(2)}) collective-permute-start(f32[1,96,192]{2,1,0:T(8,128)S(1)} %constant_dynamic-slice_fusion.12), channel_id=1, source_target_pairs={{0,4},{1,5},{2,6},{3,7},{4,0},{5,1},{6,2},{7,3},{8,12},{9,13},{10,... | collective-permute-start | bytes 221192 | tf_op jit(solution)/shard_map/ppermute | solution.py:1016
  662.7 42.6 %collective-permute-start.14 = (f32[1,96,192]{2,1,0:T(8,128)}, f32[1,96,192]{2,1,0:T(8,128)}, u32[]{:S(2)}, u32[]{:S(2)}) collective-permute-start(f32[1,96,192]{2,1,0:T(8,128)} %constant_dynamic-slice_fusion.15), channel_id=1, source_target_pairs={{0,4},{1,5},{2,6},{3,7},{4,0},{5,1},{6,2},{7,3},{8,12},{9,13},{10,... | collective-permute-start | bytes 221192 | tf_op jit(solution)/shard_map/ppermute | solution.py:1016
  665.9 31.0 %collective-permute-start.32 = (f32[2,384,384]{2,1,0:T(8,128)S(1)}, f32[2,384,384]{2,1,0:T(8,128)S(1)}, u32[]{:S(2)}, u32[]{:S(2)}) collective-permute-start(f32[2,384,384]{2,1,0:T(8,128)S(1)} %dynamic-slice_bitcast_fusion.2), channel_id=1, source_target_pairs={{0,2},{1,3},{2,0},{3,1},{4,6},{5,7},{6,4},{7,5},{8,10},{9,11},{10,... | collective-permute-start | bytes 3538952 | tf_op jit(solution)/shard_map/ppermute | solution.py:1016
  668.8 33.2 %collective-permute-start.37 = (f32[4,96,768]{2,1,0:T(8,128)}, f32[4,96,768]{2,1,0:T(8,128)}, u32[]{:S(2)}, u32[]{:S(2)}) collective-permute-start(f32[4,96,768]{2,1,0:T(8,128)} %constant_dynamic-slice_fusion.1), channel_id=1, source_target_pairs={{0,8},{8,0},{16,24},{24,16},{1,9},{9,1},{17,25},{25,17},{2,10},{10... | collective-permute-start | bytes 3538952 | tf_op jit(solution)/shard_map/ppermute | solution.py:1016
  669.3 27.7 %copy-start.23 = (f32[2,96,192]{2,1,0:T(8,128)}, f32[2,96,192]{2,1,0:T(8,128)S(1)}, u32[]{:S(2)}) copy-start(f32[2,96,192]{2,1,0:T(8,128)S(1)} %bitcast_add_fusion.11) | copy-start | bytes 442372
  670.0 53.0 %collective-permute-start.4 = (f32[1,96,192]{2,1,0:T(8,128)}, f32[1,96,192]{2,1,0:T(8,128)}, u32[]{:S(2)}, u32[]{:S(2)}) collective-permute-start(f32[1,96,192]{2,1,0:T(8,128)} %constant_dynamic-slice_fusion.21), channel_id=1, source_target_pairs={{0,4},{1,5},{2,6},{3,7},{4,0},{5,1},{6,2},{7,3},{8,12},{9,13},{10,... | collective-permute-start | bytes 221192 | tf_op jit(solution)/shard_map/ppermute | solution.py:1016
  700.4 13.9 %collective-permute-start.33 = (f32[2,384,192]{1,2,0:T(8,128)}, f32[2,384,192]{1,2,0:T(8,128)}, u32[]{:S(2)}, u32[]{:S(2)}) collective-permute-start(f32[2,384,192]{1,2,0:T(8,128)} %copy.66), channel_id=1, source_target_pairs={{0,16},{8,24},{16,0},{24,8},{1,17},{9,25},{17,1},{25,9},{2,18},{10... | collective-permute-start | bytes 1769480 | tf_op jit(solution)/shard_map/ppermute | solution.py:1016
  705.3 13.6 %collective-permute-start.38 = (f32[2,96,768]{2,1,0:T(8,128)}, f32[2,96,768]{2,1,0:T(8,128)}, u32[]{:S(2)}, u32[]{:S(2)}) collective-permute-start(f32[2,96,768]{2,1,0:T(8,128)} %dynamic-slice_bitcast_fusion.7), channel_id=1, source_target_pairs={{0,2},{1,3},{2,0},{3,1},{4,6},{5,7},{6,4},{7,5},{8,10},{9,11},{10,... | collective-permute-start | bytes 1769480 | tf_op jit(solution)/shard_map/ppermute | solution.py:1016
  718.8 23.4 %collective-permute-start.34 = (f32[1,384,192]{2,1,0:T(8,128)}, f32[1,384,192]{2,1,0:T(8,128)S(1)}, u32[]{:S(2)}, u32[]{:S(2)}) collective-permute-start(f32[1,384,192]{2,1,0:T(8,128)} %constant_dynamic-slice_fusion.3), channel_id=1, source_target_pairs={{0,4},{1,5},{2,6},{3,7},{4,0},{5,1},{6,2},{7,3},{8,12},{9,13},{10,... | collective-permute-start | bytes 884744 | tf_op jit(solution)/shard_map/ppermute | solution.py:1016
  720.1 28.3 %collective-permute-start.39 = (f32[1,96,768]{2,1,0:T(8,128)S(1)}, f32[1,96,768]{2,1,0:T(8,128)S(1)}, u32[]{:S(2)}, u32[]{:S(2)}) collective-permute-start(f32[1,96,768]{2,1,0:T(8,128)S(1)} %constant_dynamic-slice_fusion), channel_id=1, source_target_pairs={{0,4},{1,5},{2,6},{3,7},{4,0},{5,1},{6,2},{7,3},{8,12},{9,13},{10,... | collective-permute-start | bytes 884744 | tf_op jit(solution)/shard_map/ppermute | solution.py:1016
  (45 other events, 264.1 us)

commit v3 on v2

--- a/solution.py
+++ b/solution.py
@@ -1009,6 +1009,350 @@
         compiler_params=params(),
         name="land_back",
     )(blocks, gq, gk, gv, member_t, inv)
+
+
+def partner_of(index, bit):
+    return index + bit - 2 * bit * lax.rem(index // bit, 2)
+
+
+class Loads:
+    def __init__(self, sources, slots, sems):
+        self.count = slots.shape[0]
+        self.views = [slots.at[i % self.count, : src.shape[0]] for i, src in enumerate(sources)]
+        self.copies = [
+            pltpu.make_async_copy(src, view, sems.at[i % self.count])
+            for i, (src, view) in enumerate(zip(sources, self.views))
+        ]
+        for copy in self.copies[: self.count]:
+            copy.start()
+
+    def get(self, i):
+        self.copies[i].wait()
+        return self.views[i]
+
+    def release(self, i):
+        if i + self.count < len(self.copies):
+            self.copies[i + self.count].start()
+
+
+ORDERS = ((2, 1, 3, 0), (3, 2, 1, 0), (1, 3, 2, 0))
+
+
+class Scatter:
+    def __init__(self, base, buffer, landings, send, recv, mine, devices):
+        self.buffer, self.landings, self.mine = buffer, landings, mine
+        self.stage = 0
+        self.copies = []
+        for stage in range(4):
+            row = []
+            for color, order in enumerate(ORDERS):
+                dim = order[stage]
+                k = (base * 3 + color) * 4 + stage
+                row.append(
+                    pltpu.make_async_remote_copy(
+                        src_ref=self.part(color, stage, 1 - mine[dim]),
+                        dst_ref=landings[stage].at[color],
+                        send_sem=send.at[k],
+                        recv_sem=recv.at[k],
+                        device_id=devices[dim],
+                        device_id_type=MESH,
+                    )
+                )
+            self.copies.append(row)
+
+    def part(self, color, stage, index):
+        order = ORDERS[color]
+        place = [slice(None)] * 4
+        for dim in order[:stage]:
+            place[dim] = self.mine[dim]
+        place[order[stage]] = index
+        return self.buffer.at[(color, *place)]
+
+    def start(self):
+        for copy in self.copies[0]:
+            copy.start()
+
+    def advance(self):
+        stage = self.stage
+        self.stage += 1
+        for color, order in enumerate(ORDERS):
+            self.copies[stage][color].wait()
+            kept = self.part(color, stage, self.mine[order[stage]])
+            kept[...] = kept[...] + self.landings[stage][color]
+            if stage < 3:
+                self.copies[stage + 1][color].start()
+
+    def store(self, out):
+        for color in range(3):
+            out[color] = self.buffer[(color, *self.mine)]
+
+
+def grads_kernel(
+    r2_ref, act_ref, hid_ref, u_ref, r1_ref, x_ref, gq_ref, gk_ref, gv_ref, tok_ref,
+    wq_ref, wk_ref, wv_ref, sums_ref, late_ref, bsum_ref, taps_ref,
+    vo_ref, down_ref, up_ref, qk_ref, gt_ref, total_ref,
+    slots, sa_h, sa_l, sb_h, sb_l, p_big, p_pair, r_down, r_up, r_vo, r_qk, *scratch
+):
+    lands = [scratch[4 * g : 4 * g + 4] for g in range(4)]
+    held, caught, load_sem, core_send, core_recv, send, recv, sum_send, sum_recv = scratch[16:]
+    me, dp = lax.axis_index("seq"), lax.axis_index("dp")
+    core, z = lax.rem(me, 2), me // 2
+    mine = (z // 2, lax.rem(z, 2), dp // 2, lax.rem(dp, 2))
+    partner = {"seq": partner_of(me, 1)}
+    devices = (
+        {"seq": partner_of(me, 4)},
+        {"seq": partner_of(me, 2)},
+        {"dp": partner_of(dp, 2)},
+        {"dp": partner_of(dp, 1)},
+    )
+    width = tok_ref.shape[1]
+    ff = act_ref.shape[1]
+    tiles = [pl.ds(c, width) for c in range(0, ff, width)]
+    loads = Loads(
+        [gv_ref, tok_ref, r1_ref, x_ref, r2_ref]
+        + [act_ref.at[:, t] for t in tiles]
+        + [hid_ref]
+        + [u_ref.at[:, t] for t in tiles]
+        + [gq_ref, gk_ref, tok_ref, gv_ref, wv_ref, gq_ref, wq_ref, gk_ref, wk_ref],
+        slots,
+        load_sem,
+    )
+    residual = pltpu.make_async_copy(r1_ref, gt_ref, load_sem.at[slots.shape[0]])
+    residual.start()
+    barrier = pltpu.get_barrier_semaphore()
+    for device in (partner, *devices):
+        pl.semaphore_signal(barrier, inc=1, device_id=device, device_id_type=MESH)
+    pl.semaphore_wait(barrier, 5)
+
+    def halfway(step):
+        return pltpu.make_async_remote_copy(
+            src_ref=held.at[step], dst_ref=caught.at[step],
+            send_sem=sum_send.at[step], recv_sem=sum_recv.at[step],
+            device_id=(partner, *devices)[step], device_id_type=MESH,
+        )
+
+    held[0] = jnp.zeros(held.shape[1:], f32)
+    held[0, 0:8, :] = sums_ref[...]
+    held[0, 8:16, :] = late_ref[...]
+    for i, t in enumerate(range(0, ff, width)):
+        held[0, 16 + i : 17 + i, :] = bsum_ref[:, t : t + width]
+    held[0, 24:40, : 2 * PAIR] = taps_ref[...]
+    step_of = [0]
+    halfway(0).start()
+
+    def sums_on():
+        step = step_of[0]
+        if step < 5:
+            step_of[0] += 1
+            halfway(step).wait()
+            added = held[step] + caught[step]
+            if step < 4:
+                held[step + 1] = added
+                halfway(step + 1).start()
+            else:
+                total_ref[...] = added
+
+    def turn(view, hi_ref, lo_ref):
+        for c in range(0, view.shape[0], 2 * PAIR):
+            rows = slice(c, c + 2 * PAIR)
+            hi, lo = split(jnp.transpose(view[rows, :]))
+            hi_ref[:, rows] = hi
+            lo_ref[:, rows] = lo
+
+    def core_copy(k, src, dst):
+        return pltpu.make_async_remote_copy(
+            src_ref=src, dst_ref=dst, send_sem=core_send.at[k], recv_sem=core_recv.at[k],
+            device_id=partner, device_id_type=MESH,
+        )
+
+    apart = [core, 1 - core]
+    sa = (sa_h, sa_l)
+    sb = (sb_h, sb_l)
+
+    def times(s, t):
+        return dots((s[0][...], s[1][...]), split(t), 1, 0)
+
+    def pair_job(first, second, t_first, t_second):
+        half = width // 2
+        for c in range(2):
+            lanes = slice(c * half, (c + 1) * half)
+            a = times(first, t_first[:, lanes])
+            b = times(second, t_second[:, lanes])
+            for i in range(2):
+                block = slice(i * 192, (i + 1) * 192)
+                both = jnp.concatenate([a[:, block], b[:, block]], axis=1)
+                for j in range(8):
+                    for color in range(3):
+                        p_pair[apart[j % 2], color, j // 4, j // 2 % 2, c, i] = both[
+                            j * 96 : (j + 1) * 96, color * PAIR : (color + 1) * PAIR
+                        ]
+
+    def down_job(slot, t):
+        for color in range(3):
+            g = times(sa, t[:, color * 256 : (color + 1) * 256])
+            for j in range(8):
+                for side in range(2):
+                    p_big[slot, apart[j % 2], color, j // 4, j // 2 % 2, side * 96 : side * 96 + 96] = g[
+                        j * 96 : (j + 1) * 96, side * PAIR : (side + 1) * PAIR
+                    ]
+
+    def up_job(slot, t):
+        half = width // 2
+        for parity in range(2):
+            g = times(sa, t[:, parity * half : (parity + 1) * half])
+            for i in range(4):
+                for color in range(3):
+                    p_big[slot, apart[parity], color, i // 2, i % 2] = g[
+                        i * 192 : (i + 1) * 192, color * PAIR : (color + 1) * PAIR
+                    ]
+
+    groups = [
+        Scatter(g, buffer, lands[g], send, recv, mine, devices)
+        for g, buffer in enumerate((r_vo, r_down, r_up, r_qk))
+    ]
+    vo, down, up, qk = groups
+
+    turn(loads.get(0), sa_h, sa_l)
+    loads.release(0)
+    turn(loads.get(2), sb_h, sb_l)
+    loads.release(2)
+    pair_job(sa, sb, loads.get(1), loads.get(3))
+    loads.release(1)
+    loads.release(3)
+    vo_copy = core_copy(0, p_pair.at[1], r_vo)
+    vo_copy.start()
+    turn(loads.get(4), sa_h, sa_l)
+    loads.release(4)
+
+    big = []
+    for i in range(4):
+        big.append((r_down.at[:, :, :, i // 2, i % 2], i % 2))
+    for i in range(4):
+        big.append((r_up.at[:, i // 2, i % 2], i % 2))
+    copies = [
+        core_copy(1 + i, p_big.at[slot, 1], place) for i, (place, slot) in enumerate(big)
+    ]
+
+    def absorb(i):
+        place, slot = big[i]
+        copies[i].wait()
+        place[...] = place[...] + p_big[slot, 0]
+
+    for i in range(8):
+        if i == 4:
+            turn(loads.get(9), sa_h, sa_l)
+            loads.release(9)
+        at = 5 + i + (i >= 4)
+        (down_job if i < 4 else up_job)(i % 2, loads.get(at))
+        loads.release(at)
+        copies[i].start()
+        sums_on()
+        if i == 0:
+            vo_copy.wait()
+            r_vo[...] = r_vo[...] + p_pair[0]
+            vo.start()
+        else:
+            absorb(i - 1)
+        if i == 4:
+            down.start()
+        if i in (3, 4, 5, 6):
+            vo.advance()
+    vo.store(vo_ref)
+    turn(loads.get(14), sa_h, sa_l)
+    loads.release(14)
+    turn(loads.get(15), sb_h, sb_l)
+    loads.release(15)
+    absorb(7)
+    up.start()
+    tokens = loads.get(16)
+    pair_job(sa, sb, tokens, tokens)
+    loads.release(16)
+    qk_copy = core_copy(9, p_pair.at[1], r_qk)
+    qk_copy.start()
+    down.advance()
+
+    def token_job(x, w):
+        for c in range(0, width, 2 * PAIR):
+            rows = slice(c, c + 2 * PAIR)
+            hi, lo = split(w[rows, :])
+            sa_h[rows, :width] = hi
+            sa_l[rows, :width] = lo
+        for c in range(0, x.shape[0], 2 * PAIR):
+            rows = slice(c, c + 2 * PAIR)
+            y = dots(split(x[rows, :]), (sa_h[:, :width], sa_l[:, :width]), 1, 1)
+            gt_ref[rows, :] += y
+
+    residual.wait()
+    for i in range(3):
+        token_job(loads.get(17 + 2 * i), loads.get(18 + 2 * i))
+        loads.release(17 + 2 * i)
+        loads.release(18 + 2 * i)
+        if i == 0:
+            qk_copy.wait()
+            r_qk[...] = r_qk[...] + p_pair[0]
+            qk.start()
+        if i == 1:
+            down.advance()
+        if i == 2:
+            up.advance()
+            down.advance()
+    for group in (qk, up, down, qk, up, qk, up, qk):
+        group.advance()
+    down.store(down_ref)
+    up.store(up_ref)
+    qk.store(qk_ref)
+
+
+def grads_call(r2, act, hidden, u, r1, x, gq, gk, gv, tokens, wq, wk, wv, sums, late, bsum, taps):
+    rows, width = tokens.shape
+    big, small = (2 * 96, PAIR), (96, PAIR)
+    any_space = pl.BlockSpec(memory_space=pl.ANY)
+    vmem = pl.BlockSpec(memory_space=VM)
+
+    def lands(block):
+        return [VM((3,) + (2,) * (3 - stage) + block, f32) for stage in range(4)]
+
+    dma = pltpu.SemaphoreType.DMA
+    return pl.pallas_call(
+        grads_kernel,
+        out_shape=[
+            jax.ShapeDtypeStruct((3,) + small, f32),
+            jax.ShapeDtypeStruct((3,) + big, f32),
+            jax.ShapeDtypeStruct((3,) + big, f32),
+            jax.ShapeDtypeStruct((3,) + small, f32),
+            jax.ShapeDtypeStruct((rows, width), f32),
+            jax.ShapeDtypeStruct((40, width), f32),
+        ],
+        in_specs=[any_space] * 13 + [vmem] * 4,
+        out_specs=[vmem] * 6,
+        scratch_shapes=[
+            VM((3, rows, width), f32),
+            VM((width, rows), bf16),
+            VM((width, rows), bf16),
+            VM((width, rows), bf16),
+            VM((width, rows), bf16),
+            VM((2, 2, 3, 2, 2) + big, f32),
+            VM((2, 3, 2, 2, 2, 2) + small, f32),
+            VM((3, 2, 2, 2, 2) + big, f32),
+            VM((3, 2, 2, 2, 2) + big, f32),
+            VM((3, 2, 2, 2, 2) + small, f32),
+            VM((3, 2, 2, 2, 2) + small, f32),
+        ]
+        + lands(small) + lands(big) + lands(big) + lands(small)
+        + [
+            VM((5, 40, width), f32),
+            VM((5, 40, width), f32),
+            dma((4,)),
+            dma((10,)),
+            dma((10,)),
+            dma((48,)),
+            dma((48,)),
+            dma((5,)),
+            dma((5,)),
+        ],
+        compiler_params=params(collective_id=4, has_side_effects=True),
+        name="grads",
+    )(r2, act, hidden, u, r1, x, gq, gk, gv, tokens, wq, wk, wv, sums, late, bsum, taps)
 
 
 def swap(x, axis, offset):
@@ -1177,49 +1521,56 @@
         land_grads, grad_queries, grad_keys, grad_values, member_t, inverse_divisor,
         per, pairs, factor,
     )
-    grad_w_down = scatter_sum(product(r2, act, 0, 0), "yxzz")
-    grad_w_up = scatter_sum(product(u, hidden, 0, 0), "xzyz")
-    grad_w_out = scatter_sum(product(r1, x, 0, 0), "zyxz")
     grad_queries = grad_queries.reshape(items * span, width)
     grad_keys = grad_keys.reshape(items * span, width)
     grad_values = grad_values.reshape(items * span, width)
-    grad_w_value = scatter_sum(product(grad_values, rows, 0, 0), "zyxz")
-    grad_w_query = scatter_sum(product(grad_queries, rows, 0, 0), "yxzz")
-    grad_w_key = scatter_sum(product(grad_keys, rows, 0, 0), "xzyz")
-    grad_tokens = (
-        r1
-        + product(grad_values, w_value, 1, 1)
-        + product(grad_queries, w_query, 1, 1)
-        + product(grad_keys, w_key, 1, 1)
-    )
-
-    early = sum_everywhere(
-        jnp.concatenate([row_sums.reshape(-1), up_sums.reshape(-1), grad_taps.reshape(-1)]).reshape(
-            -1, PAIR
+    ff = w_up.shape[1]
+    if (n, lax.axis_size("dp"), width, ff) == (8, 4, 768, 3072):
+        vo, down, up, qk, grad_tokens, totals = grads_call(
+            r2, act, hidden, u, r1, x, grad_queries, grad_keys, grad_values, rows,
+            w_query, w_key, w_value, row_sums, late_sums, up_sums, grad_taps,
         )
-    ).reshape(-1)
-    late = sum_everywhere(late_sums)
-    row_sums = early[: 8 * width].reshape(8, width)
-    ff = w_up.shape[1]
-    up_sums = early[8 * width : 8 * width + ff]
-    grad_taps = early[8 * width + ff :].reshape(-1, 2 * PAIR)
-    grad_conv = grad_taps[:heads, PAIR - 1 : PAIR - 1 + taps]
+        vo, qk = (jnp.transpose(both, (0, 2, 1)).reshape(2, -1, both.shape[1]) for both in (vo, qk))
+        grad_w_value, grad_w_out = vo[0], vo[1]
+        grad_w_query, grad_w_key = qk[0], qk[1]
+        down = down.reshape(3, 2, -1, PAIR)
+        grad_w_down = jnp.transpose(down, (0, 1, 3, 2)).reshape(-1, down.shape[2])
+        grad_w_up = jnp.transpose(up, (1, 0, 2)).reshape(up.shape[1], -1)
+    else:
+        grad_w_down = scatter_sum(product(r2, act, 0, 0), "yxzz").T
+        grad_w_up = scatter_sum(product(u, hidden, 0, 0), "xzyz").T
+        grad_w_out = scatter_sum(product(r1, x, 0, 0), "zyxz").T
+        grad_w_value = scatter_sum(product(grad_values, rows, 0, 0), "zyxz").T
+        grad_w_query = scatter_sum(product(grad_queries, rows, 0, 0), "yxzz").T
+        grad_w_key = scatter_sum(product(grad_keys, rows, 0, 0), "xzyz").T
+        grad_tokens = (
+            r1
+            + product(grad_values, w_value, 1, 1)
+            + product(grad_queries, w_query, 1, 1)
+            + product(grad_keys, w_key, 1, 1)
+        )
+        taps_rows = jnp.pad(grad_taps, ((0, 0), (0, width - grad_taps.shape[1])))
+        up_rows = jnp.pad(up_sums.reshape(-1, width), ((0, 8 - ff // width), (0, 0)))
+        totals = sum_everywhere(jnp.concatenate([row_sums, late_sums, up_rows, taps_rows]))
+    row_sums, late = totals[:8], totals[8:16]
+    up_sums = totals[16 : 16 + ff // width].reshape(ff)
+    grad_conv = totals[24 : 24 + heads, PAIR - 1 : PAIR - 1 + taps]
     return (
         output.reshape(tokens.shape),
         grad_tokens.reshape(tokens.shape),
-        grad_w_query.T,
+        grad_w_query,
         late[0],
-        grad_w_key.T,
-        grad_w_value.T,
+        grad_w_key,
+        grad_w_value,
         late[1],
         grad_conv,
-        grad_w_out.T,
+        grad_w_out,
         row_sums[5],
         row_sums[3],
         row_sums[4],
-        grad_w_up.T,
+        grad_w_up,
         up_sums,
-        grad_w_down.T,
+        grad_w_down,
         row_sums[2],
         row_sums[0],
         row_sums[1],

time: 747 us -> 583 us (0.78)
  Pallas kernels: 359 us -> 536 us
  waiting for transfers between devices: 136 us -> 0 us
  matrix products: 82.4 us -> 0 us
  local copies, waits for them, and re-layouts: 74.1 us -> 24.6 us
  starting transfers between devices: 39.8 us -> 0 us
  other arithmetic: 56.7 us -> 24 us
    pallas_call x0 -> x1, Pallas kernels: none -> 178 us  [grads_call(): pl.pallas_call(grads_kernel, out_shape=[jax.ShapeDtypeStruct((3,) + small...]
    ppermute x40 -> x0, waiting for transfers between devices: 136 us -> none  [swap(): return lax.ppermute(x, axis, [(i, i ^ offset) for i in range(count)])]
    dot_general x9 -> x0, matrix products: 82.4 us -> none  [product(): return lax.dot_general(a, b, (((ca,), (cb,)), ((), ())), precision=HIGH)]
    ppermute x40 -> x0, starting transfers between devices: 39.8 us -> none  [swap(): return lax.ppermute(x, axis, [(i, i ^ offset) for i in range(count)])]
    add x34 -> x0, other arithmetic: 23.3 us -> none  [the longest x12 13.3 us: halve_rows(): return keep + swap(send, 'seq', bit)]
    squeeze x19 -> x2, local copies, waits for them, and re-layouts: 16.8 us -> 1.38 us  [the longest x1 0.69 us: on_device(): grad_w_query, grad_w_key = (qk[0], qk[1])]
    dot_general x4 -> x0, local copies, waits for them, and re-layouts: 14.9 us -> none  [product(): return lax.dot_general(a, b, (((ca,), (cb,)), ((), ())), precision=HIGH)]
    unnamed x112 -> x27, local copies, waits for them, and re-layouts: 12.6 us -> 2.9 us
  transfers between devices with their start and end apart: 40 -> 0, of which waited for: 15 -> 0; matrix products, arithmetic and copies ran while one was open for 19% -> 0% of each run, Pallas kernels for 19% -> 0%
where the time goes in v3:
time: 583 us; the launch traced here: 586 us
  Pallas kernels  536 us (92%)
  local copies, waits for them, and re-layouts  24.6 us (4%)
  other arithmetic  24 us (4%)
    pallas_call x1, Pallas kernels, grads_call(): pl.pallas_call(grads_kernel, out_shape=[jax.ShapeDtypeStruct((3,) + small...  178 us
    pallas_call x1, Pallas kernels, rows_call(): pl.pallas_call(functools.partial(rows_kernel, ff_tile), out_shape=[narrow...  124 us
    pallas_call x1, Pallas kernels, exchange_back_call(): pl.pallas_call(functools.partial(exchange_back_kernel, n, per), out_shape...  46.9 us
    pallas_call x1, Pallas kernels, project_call(): pl.pallas_call(functools.partial(project_kernel, n, items, factor), out_s...  41.2 us
    pallas_call x1, Pallas kernels, land_exchange_call(): pl.pallas_call(functools.partial(land_exchange_kernel, n, per), out_shape...  38.8 us
    pallas_call x1, Pallas kernels, exchange_call(): pl.pallas_call(functools.partial(exchange_kernel, n, per, pairs), out_sha...  30.4 us
    convert_element_type x3, other arithmetic, rounded_pair(): return (hi.astype(bf16), (w - hi).astype(bf16))  18 us
    pallas_call x1, Pallas kernels, conv_back_call(): pl.pallas_call(functools.partial(conv_back_kernel, pairs, margin), out_sh...  17.5 us

profile of v3, /device:TPU:0, one launch (start us, length us, event | category | flops | bytes accessed | tf_op | source)
XLA Modules:
  0.0 586.0 jit_solution(13210634521841004389)
XLA Ops:
  0.7 0.7 sign.15
  1.4 0.8 compare_select_fusion
  2.2 0.8 fusion.5
  3.0 0.6 copy-done.2
  3.6 0.7 fusion.3.mem_ref
  4.3 0.7 stack.59
  5.0 0.7 stack.60
  5.7 0.6 pad_maximum_fusion.1.vec_ref
  6.3 41.2 %project.1 = (f32[4,256,768]{2,1,0:T(8,128)}, f32[4,256,768]{2,1,0:T(8,128)}, f32[4,256,768]{2,1,0:T(8,128)}, f32[4,64,768]{2,1,0:T(8,128)}, f32[4,64,768]{2,1,0:T(8,128)}, /*index=5*/f32[4,64,128]{2,1,0:T(8,128)}) custom-call(f32[4,256,768]{2,1,0:T(8,128)} %tok_ref.1, f32[4,64,256]{2,1,0:T(8,128)} %fusion.3.mem_ref, f32[768,768]{1,0:T(8,128)} %wq_ref.3, ...), custom_call_target="tpu_custom_call" | custom-call | tf_op jit(solution)/shard_map/project/pallas_call | solution.py:295
  47.5 1.3 broadcast_in_dim.20.use_ref
  48.8 12.8 %scores.1 = (f32[4,768,256]{2,1,0:T(8,128)}, f32[4,768,256]{2,1,0:T(8,128)}, f32[4,8,128]{2,1,0:T(8,128)}, f32[8,200,128]{2,1,0:T(8,128)}) custom-call(f32[4,256,768]{2,1,0:T(8,128)} %get-tuple-element.64.q_ref, f32[4,256,768]{2,1,0:T(8,128)} %get-tuple-element.65.k_ref, f32[4,256,768]{2,1,0:T(8,128)} %get-tuple-element.66.v_ref, ...), custom_call_target="tpu_custom_call" | custom-call | tf_op jit(solution)/shard_map/scores/pallas_call | solution.py:345
  61.6 1.1 slice_bitcast_fusion.3
  62.7 0.8 fusion.7
  63.5 0.6 copy-done.1
  64.1 0.1 slice_bitcast_fusion.9
  64.2 0.9 maximum_multiply_fusion.side_ref
  65.0 30.4 %exchange.1 = (f32[3,128,128]{2,1,0:T(8,128)}, f32[7,3,128,128]{3,2,1,0:T(8,128)}, f32[3,64,128]{2,1,0:T(8,128)}, f32[3,64,128]{2,1,0:T(8,128)}, f32[3,64,128]{2...) custom-call(f32[2,4,200,128]{3,2,1,0:T(8,128)} %bitcast.76, ...), custom_call_target="tpu_custom_call" | custom-call | tf_op jit(solution)/shard_map/exchange/pallas_call | solution.py:459
  95.5 1.7 copy.40.use_ref
  97.2 1.3 pad.7.taps_ref
  98.5 10.7 %mix.1 = f32[4,256,768]{2,1,0:T(8,128)} custom-call(f32[8,200,128]{2,1,0:T(8,128)} %bitcast.67, f32[4,768,256]{2,1,0:T(8,128)} %get-tuple-element.71.k1_ref, f32[4,256,768]{2,1,0:T(8,128)} %get-tuple-element.66.v_ref, f32[4,256,1]{2,1,0:T(8,128)} %copy.40.use_ref, f32[2,4,16,768]{3,2,1,0:T(8,128)} %get-tuple-element.72.left_ref.right_ref.vl_ref.vr_ref, ...), custom_call_target="tpu_custom_call" | custom-call | tf_op jit(solution)/shard_map/mix/pallas_call | solution.py:549
  109.2 8.9 %fusion.1 = (bf16[3072,768]{1,0:T(8,128)(2,1)}, bf16[3072,768]{1,0:T(8,128)(2,1)}) fusion(f32[3072,768]{1,0:T(8,128)} %param.35), kind=kLoop, calls=%fused_computation.5 | loop fusion | flops 9437184 | bytes 18874368 | tf_op jit(solution)/shard_map/convert_element_type | solution.py:1433
  118.1 5.7 fusion
  123.8 3.5 fusion.2
  127.4 0.7 stack.74.vec_ref
  128.0 123.5 %rows.1 = (f32[1024,768]{1,0:T(8,128)}, f32[1024,3072]{1,0:T(8,128)}, f32[1024,3072]{1,0:T(8,128)}, f32[1024,768]{1,0:T(8,128)}, f32[1024,768]{1,0:T(8,128)}, /*...) custom-call(f32[1024,768]{1,0:T(8,128)} %bitcast.59, f32[1024,768]{1,0:T(8,128)} %bitcast.57, ...), custom_call_target="tpu_custom_call" | custom-call | tf_op jit(solution)/shard_map/rows/pallas_call | solution.py:679
  251.6 1.1 slice_bitcast_fusion.1
  252.6 0.8 pad_maximum_fusion.side_ref
  253.4 12.9 %one_back.1 = (f32[4,256,768]{2,1,0:T(8,128)}, f32[8,384,128]{2,1,0:T(8,128)}) custom-call(f32[8,200,128]{2,1,0:T(8,128)} %bitcast.68, f32[4,768,256]{2,1,0:T(8,128)} %get-tuple-element.71.k1_ref, f32[4,256,768]{2,1,0:T(8,128)} %bitcast.62, f32[4,256,768]{2,1,0:T(8,128)} %get-tuple-element.64.q_ref, f32[4,64,768]{2,1,0:T(8,128)} %get-tuple-element.68.lk_ref), custom_call_target="tpu_custom_call" | custom-call | tf_op jit(solution)/shard_map/one_back/pallas_call | solution.py:731
  266.3 46.9 %exchange_back.1 = (f32[2,4,200,128]{3,2,1,0:T(8,128)}, f32[3,64,128]{2,1,0:T(8,128)}, f32[3,64,128]{2,1,0:T(8,128)}, f32[2,4,16,768]{3,2,1,0:T(8,128)}) custom-call(f32[2,4,384,128]{3,2,1,0:T(8,128)} %bitcast.75, f32[2,4,16,768]{3,2,1,0:T(8,128)} %pad_maximum_fusion.side_ref, f32[3,64,128]{2,1,0:T(8,128)} %get-tuple-element.81.ctx_ref, ...), custom_call_target="tpu_custom_call" | custom-call | tf_op jit(solution)/shard_map/exchange_back/pallas_call | solution.py:878
  313.2 0.8 rev.3
  314.0 0.6 pad.8.taps_ref
  314.6 17.5 %conv_back.1 = (f32[4,256,768]{2,1,0:T(8,128)}, f32[16,256]{1,0:T(8,128)}) custom-call(f32[4,256,768]{2,1,0:T(8,128)} %bitcast.63, f32[2,4,16,768]{3,2,1,0:T(8,128)} %get-tuple-element.89.gl_ref.gr_ref, f32[2,4,16,768]{3,2,1,0:T(8,128)} %get-tuple-element.89.gl_ref.gr_ref, f32[4,256,768]{2,1,0:T(8,128)} %get-tuple-element.66.v_ref, ...), custom_call_target="tpu_custom_call" | custom-call | tf_op jit(solution)/shard_map/conv_back/pallas_call | solution.py:795
  332.2 14.5 %three_back.1 = (f32[4,256,768]{2,1,0:T(8,128)}, f32[4,256,768]{2,1,0:T(8,128)}, f32[8,192,128]{2,1,0:T(8,128)}) custom-call(f32[8,200,128]{2,1,0:T(8,128)} %bitcast.77, f32[8,200,128]{2,1,0:T(8,128)} %bitcast.69, f32[4,768,256]{2,1,0:T(8,128)} %get-tuple-element.87.w3_ref, f32[4,8,128]{2,1,0:T(8,128)} %get-tuple-element.88.top_ref, ...), custom_call_target="tpu_custom_call" | custom-call | tf_op jit(solution)/shard_map/three_back/pallas_call | solution.py:930
  346.7 38.8 %land_exchange.1 = f32[2,4,384,128]{3,2,1,0:T(8,128)} custom-call(f32[2,4,192,128]{3,2,1,0:T(8,128)} %bitcast.80, f32[192,128]{1,0:T(8,128)} %bitcast.84, f32[192,128]{1,0:T(8,128)} %bitcast.85), custom_call_target="tpu_custom_call" | custom-call | tf_op jit(solution)/shard_map/land_exchange/pallas_call | solution.py:963
  385.4 8.5 %land_back.1 = (f32[4,256,768]{2,1,0:T(8,128)}, f32[4,256,768]{2,1,0:T(8,128)}, f32[8,768]{1,0:T(8,128)}) custom-call(f32[8,384,128]{2,1,0:T(8,128)} %bitcast.70, f32[4,256,768]{2,1,0:T(8,128)} %get-tuple-element.94.gq_ref, f32[4,256,768]{2,1,0:T(8,128)} %get-tuple-element.95.gk_ref, f32[4,256,768]{2,1,0:T(8,128)} %get-tuple-element.96.gv_ref, ...), custom_call_target="tpu_custom_call" | custom-call | tf_op jit(solution)/shard_map/land_back/pallas_call | solution.py:1002
  394.0 178.3 %grads.1 = (f32[3,96,128]{2,1,0:T(8,128)}, f32[3,192,128]{2,1,0:T(8,128)}, f32[3,192,128]{2,1,0:T(8,128)}, f32[3,96,128]{2,1,0:T(8,128)}, f32[1024,768]{1,0:T(8,128)}, /*index=5*/f32[40,768]{1,0:T(8,128)}) custom-call(f32[1024,768]{1,0:T(8,128)} %get-tuple-element.74.r2_ref, f32[1024,3072]{1,0:T(8,128)} %get-tuple-element.75.act_ref, ...), custom_call_target="tpu_custom_call" | custom-call | tf_op jit(solution)/shard_map/grads/pallas_call | solution.py:1316
  572.3 1.3 copy.45
  573.6 1.0 reshape.234
  574.6 1.0 copy.42
  575.6 0.7 slice_bitcast_fusion.6
  576.3 1.0 copy.43
  577.3 0.7 slice_bitcast_fusion.4
  578.0 1.7 copy_bitcast_fusion
  579.7 1.6 slice_reduce_fusion
  581.4 0.7 slice.86
  582.1 0.6 reshape.232
  582.7 1.4 slice.81
  584.1 1.7 copy.49
  (34 shorter events, 0.1 us)
Async XLA Ops:
  0.7 3.6 copy-start.3
  3.0 0.6 copy-start.2
  63.5 0.6 copy-start.1
  109.2 8.9 %slice-start = ((s8[9437184]{0:T(1024)(128)(4,1)}), s8[4194304]{0:T(1024)(128)(4,1)S(1)}, s32[]{:S(2)}) async-start(s8[9437184]{0:T(1024)(128)(4,1)} %bitcast.65), calls=%async_computation | async-start | bytes 8388608
  109.2 8.9 %slice-start.1 = ((s8[9437184]{0:T(1024)(128)(4,1)}), s8[4194304]{0:T(1024)(128)(4,1)S(1)}, s32[]{:S(2)}) async-start(s8[9437184]{0:T(1024)(128)(4,1)} %bitcast.65), calls=%async_computation.1 | async-start | bytes 8388608
  109.2 8.9 %slice-start.2 = ((s8[9437184]{0:T(1024)(128)(4,1)}), s8[1048576]{0:T(1024)(128)(4,1)S(1)}, s32[]{:S(2)}) async-start(s8[9437184]{0:T(1024)(128)(4,1)} %bitcast.65), calls=%async_computation.2 | async-start | bytes 2097152
  123.8 3.5 copy-start.4
  123.8 3.5 copy-start.5
  123.8 3.5 copy-start.6
  123.8 3.6 copy-start.7
  123.8 3.6 copy-start.8
  123.8 3.6 copy-start.9
  572.3 11.8 %copy-start = (f32[1024,768]{1,0:T(8,128)S(1)}, f32[1024,768]{1,0:T(8,128)}, u32[]{:S(2)}) copy-start(f32[1024,768]{1,0:T(8,128)} %get-tuple-element.104) | copy-start | bytes 9437188

commit v4 on v2

--- a/solution.py
+++ b/solution.py
@@ -106,13 +106,14 @@
     def at(self, z):
         return 2 * z + self.core
 
-    def hello(self, edges):
+    def hello(self, edges, more=()):
         others = [self.partner] + [self.at(self.ahead(j)) for j in range(1, self.nz)]
         if edges:
             others.append(self.extra)
+        others = [{"seq": other} for other in others] + list(more)
         barrier = pltpu.get_barrier_semaphore()
         for other in others:
-            pl.semaphore_signal(barrier, inc=1, device_id={"seq": other}, device_id_type=MESH)
+            pl.semaphore_signal(barrier, inc=1, device_id=other, device_id_type=MESH)
         pl.semaphore_wait(barrier, len(others))
 
 
@@ -231,18 +232,210 @@
     return functools.reduce(lambda x, y: x + y, [r[...] for r in refs])
 
 
+def partner_of(index, bit):
+    return index + bit - 2 * bit * lax.rem(index // bit, 2)
+
+
+class Loads:
+    def __init__(self, sources, slots, sems):
+        self.count = slots.shape[0]
+        self.views, self.copies = [], []
+        for i, src in enumerate(sources):
+            slot = i % self.count
+            view = slots.at[slot, : src.shape[-2]]
+            self.views.append(view)
+            if len(src.shape) == 2:
+                self.copies.append([pltpu.make_async_copy(src, view, sems.at[slot, 0])])
+                continue
+            size = src.shape[2]
+            self.copies.append(
+                [
+                    pltpu.make_async_copy(
+                        src.at[j], view.at[:, j * size : (j + 1) * size], sems.at[slot, j]
+                    )
+                    for j in range(src.shape[0])
+                ]
+            )
+        for i in range(min(self.count, len(sources))):
+            self.begin(i)
+
+    def begin(self, i):
+        for copy in self.copies[i]:
+            copy.start()
+
+    def get(self, i):
+        for copy in self.copies[i]:
+            copy.wait()
+        return self.views[i]
+
+    def release(self, i):
+        if i + self.count < len(self.copies):
+            self.begin(i + self.count)
+
+
+def halved(view, into):
+    rows, columns = into.shape[1:]
+    for r in range(0, rows, 2 * PAIR):
+        part = slice(r, r + 2 * PAIR)
+        into[0, part, :], into[1, part, :] = split(view[part, :])
+    return into
+
+
+ALL_LINKS = ((2, 3, 1, 0), (3, 2, 1, 0), (1, 3, 2, 0))
+EVEN = ((2, 1, 3, 0), (3, 2, 1, 0), (1, 3, 2, 0))
+
+
+class Links:
+    def __init__(self):
+        me, dp = lax.axis_index("seq"), lax.axis_index("dp")
+        z = me // 2
+        self.core = lax.rem(me, 2)
+        self.mine = (z // 2, lax.rem(z, 2), dp // 2, lax.rem(dp, 2))
+        self.partner = {"seq": partner_of(me, 1)}
+        self.devices = (
+            {"seq": partner_of(me, 4)},
+            {"seq": partner_of(me, 2)},
+            {"dp": partner_of(dp, 2)},
+            {"dp": partner_of(dp, 1)},
+        )
+        self.apart = (self.core, 1 - self.core)
+
+    def copy(self, k, src, dst, send, recv):
+        return pltpu.make_async_remote_copy(
+            src_ref=src, dst_ref=dst, send_sem=send.at[k], recv_sem=recv.at[k],
+            device_id=self.partner, device_id_type=MESH,
+        )
+
+
+class Scatter:
+    def __init__(self, base, links, buffers, send, recv, first=0, orders=ALL_LINKS):
+        self.orders = orders
+        self.links, self.buffers, self.first, self.stage = links, buffers, first, first
+        self.copies = {}
+        for stage in range(first, first + len(buffers) - 1):
+            for color, order in enumerate(self.orders):
+                dim = order[stage]
+                k = (base * 3 + color) * 4 + stage
+                self.copies[stage, color] = pltpu.make_async_remote_copy(
+                    src_ref=self.part(color, stage, 1 - links.mine[dim]),
+                    dst_ref=buffers[stage - first + 1].at[color],
+                    send_sem=send.at[k],
+                    recv_sem=recv.at[k],
+                    device_id=links.devices[dim],
+                    device_id_type=MESH,
+                )
+
+    def part(self, color, stage, index):
+        order = self.orders[color]
+        left = [dim for dim in range(4) if dim not in order[:stage]]
+        place = [index if dim == order[stage] else slice(None) for dim in left]
+        return self.buffers[stage - self.first].at[(color, *place)]
+
+    def start(self):
+        for color in range(3):
+            self.copies[self.stage, color].start()
+
+    def advance(self):
+        stage = self.stage
+        self.stage += 1
+        for color, order in enumerate(self.orders):
+            self.copies[stage, color].wait()
+            landed = self.buffers[stage - self.first + 1].at[color]
+            landed[...] = landed[...] + self.part(color, stage, self.links.mine[order[stage]])[...]
+            if (stage + 1, color) in self.copies:
+                self.copies[stage + 1, color].start()
+
+
+def times(s, t, lanes):
+    return dots((s[0], s[1]), split(t[:, lanes]), 1, 0)
+
+
+BIG = (192, PAIR)
+SMALL = (96, PAIR)
+
+
+def landing(block, stage):
+    return (3,) + (2,) * (3 - stage) + block
+
+
+class Tiles:
+    def __init__(self, links, down, s, t, buffer, scratch):
+        self.links, self.down = links, down
+        s_slots, self.s, t_slots, self.p_big, s_sem, t_sem, send, recv = scratch
+        self.s_loads = Loads([s], s_slots, s_sem)
+        self.t_loads = Loads([t.at[i] for i in range(4)], t_slots, t_sem)
+        self.places, self.copies = [], []
+        for i in range(4):
+            at = (slice(None),) * (3 if down else 1) + (i // 2, i % 2)
+            self.places.append(buffer.at[at])
+            self.copies.append(links.copy(i, self.p_big.at[i % 2, 1], self.places[i], send, recv))
+
+    def compute(self, i):
+        if i == 0:
+            halved(self.s_loads.get(0), self.s)
+        t, slot, apart = self.t_loads.get(i), i % 2, self.links.apart
+        for third in range(3):
+            g = times(self.s, t, slice(third * 256, (third + 1) * 256))
+            for side in range(2):
+                lanes = slice(side * PAIR, (side + 1) * PAIR)
+                if self.down:
+                    for j in range(8):
+                        at = (slot, apart[j % 2], third, j // 4, j // 2 % 2)
+                        self.p_big[(*at, slice(side * 96, side * 96 + 96))] = g[j * 96 : (j + 1) * 96, lanes]
+                else:
+                    parity, color = divmod(2 * third + side, 3)
+                    for j in range(4):
+                        at = (slot, apart[parity], color, j // 2, j % 2)
+                        self.p_big[at] = g[j * 192 : (j + 1) * 192, lanes]
+        self.t_loads.release(i)
+        self.copies[i].start()
+
+    def absorb(self, i):
+        self.copies[i].wait()
+        place = self.places[i]
+        place[...] = place[...] + self.p_big[i % 2, 0]
+
+    @staticmethod
+    def scratch(rows, width):
+        dma = pltpu.SemaphoreType.DMA
+        return [
+            VM((1, width, rows), f32),
+            VM((2, width, rows), bf16),
+            VM((2, rows, width), f32),
+            VM((2, 2, 3, 2, 2) + BIG, f32),
+            dma((1, 4)),
+            dma((2, 1)),
+            dma((4,)),
+            dma((4,)),
+        ]
+
+
 def project_kernel(n, items, factor, tok_ref, mem_ref, wq_ref, wk_ref, wv_ref, vec_ref,
-                   q_ref, k_ref, v_ref, lq_ref, lk_ref, inv_ref,
-                   sums, land, halves, *scratch):
+                   q_out, k_out, v_out, lq_ref, lk_ref, inv_ref,
+                   q_ref, k_ref, v_ref, tok_h, tok_l, halves, w_s, w_sem, out_sem,
+                   sums, land, *scratch):
     seat = Seat(n)
     rows = items * MARKS // n
     width = tok_ref.shape[2]
     reduce = Reduce(seat, sums, *scratch[:5])
     gather = Gather(seat, land, *scratch[5:])
+    fetches = [
+        pltpu.make_async_copy(ref, w_s.at[i], w_sem.at[i])
+        for i, ref in enumerate((wq_ref, wk_ref, wv_ref))
+    ]
+    for fetch in fetches:
+        fetch.start()
+    stores = [
+        pltpu.make_async_copy(src, dst, out_sem.at[i])
+        for i, (src, dst) in enumerate(
+            ((q_ref, q_out), (k_ref, k_out), (v_ref, v_out))
+        )
+    ]
     seat.hello(False)
     for item in range(items):
         member = mem_ref[item].astype(bf16)
         hi, lo = split(tok_ref[item])
+        tok_h[item], tok_l[item] = hi, lo
         total = dg(member, hi, 1, 0) + dg(member, lo, 1, 0)
         count = jnp.sum(mem_ref[item], axis=1, keepdims=True)
         for part in range(MARKS // rows):
@@ -254,13 +447,14 @@
             )
     reduce.start()
     b_query, b_value = vec_ref[0:1, :], vec_ref[1:2, :]
-    for place, w_ref in enumerate((wq_ref, wk_ref, wv_ref)):
-        hi, lo = split(w_ref[...])
+    for place in range(3):
+        fetches[place].wait()
+        hi, lo = split(w_s[place])
         halves[2 * place], halves[2 * place + 1] = hi, lo
 
     def project(place, out_ref, bias, scale):
         def lap(item, _):
-            x = split(tok_ref[item])
+            x = (tok_h[item], tok_l[item])
             y = dots(x, (halves[2 * place], halves[2 * place + 1]), 1, 0)
             y = y if bias is None else y + bias
             out_ref[item] = y if scale is None else y * scale
@@ -269,11 +463,14 @@
         lax.fori_loop(0, items, lap, 0)
 
     project(0, q_ref, b_query, factor)
+    stores[0].start()
     reduce.middle(add_all)
     project(1, k_ref, None, factor)
+    stores[1].start()
     land[seat.core, seat.z] = reduce.finish(add_all)
     gather.start()
     project(2, v_ref, b_value, None)
+    stores[2].start()
     gather.forward()
     gather.finish()
     whole_land = land[...].reshape(items * MARKS, width + PAIR)
@@ -285,6 +482,8 @@
     lk = dots(x, (halves[2], halves[3]), 1, 0) * factor
     lq_ref[...] = lq.reshape(items, MARKS, width)
     lk_ref[...] = lk.reshape(items, MARKS, width)
+    for store in stores:
+        store.wait()
 
 
 def project_call(tokens, member_t, w_query, w_key, w_value, vectors, n, factor):
@@ -292,15 +491,21 @@
     rows = items * MARKS // n
     big = jax.ShapeDtypeStruct((items, span, width), f32)
     small = jax.ShapeDtypeStruct((items, MARKS, width), f32)
+    vmem, any_space = pl.BlockSpec(memory_space=VM), pl.BlockSpec(memory_space=pl.ANY)
     return pl.pallas_call(
         functools.partial(project_kernel, n, items, factor),
         out_shape=[big, big, big, small, small, jax.ShapeDtypeStruct((items, MARKS, PAIR), f32)],
-        in_specs=[pl.BlockSpec(memory_space=VM)] * 6,
-        out_specs=[pl.BlockSpec(memory_space=VM)] * 6,
-        scratch_shapes=[
+        in_specs=[vmem] * 2 + [any_space] * 3 + [vmem],
+        out_specs=[any_space] * 3 + [vmem] * 3,
+        scratch_shapes=[VM((items, span, width), f32)] * 3
+        + [VM((items, span, width), bf16)] * 2
+        + [
+            VM((6, width, width), bf16),
+            VM((3, width, width), f32),
+            pltpu.SemaphoreType.DMA((3,)),
+            pltpu.SemaphoreType.DMA((3,)),
             VM((2, n // 2, rows, width + PAIR), f32),
             VM((2, n // 2, rows, width + PAIR), f32),
-            VM((6, width, width), bf16),
         ]
         + Reduce.scratch(n, (rows, width + PAIR))
         + Gather.scratch(n),
@@ -596,33 +801,50 @@
 
 
 def rows_kernel(
-    ff_tile,
-    x_ref,
-    tok_ref,
-    cot_ref,
-    wo_h,
-    wo_l,
-    wu_h,
-    wu_l,
-    wd_h,
-    wd_l,
-    vec_ref,
-    bup_ref,
-    out_ref,
-    act_ref,
-    u_ref,
-    r2_ref,
-    h1_ref,
-    r1_ref,
-    og_ref,
-    sums_ref,
-    bsum_ref,
-    slope,
+    x_ref, tok_ref, cot_ref, vec_ref, bup_ref, wo_ref, wu_ref, wd_ref,
+    out_ref, act_ref, u_ref, r2t_ref, h1t_ref, r1t_ref, r1_ref, og_ref, sums_ref, bsum_ref,
+    slope, wo_h, wo_l, wu_h, wu_l, wd_h, wd_l, staged, sems,
 ):
-    @pl.when(pl.program_id(0) == 0)
+    step = pl.program_id(0)
+    width = tok_ref.shape[1]
+    ff = wu_ref.shape[1]
+    tiles = [slice(c, c + width) for c in range(0, ff, width)]
+
+    @pl.when(step == 0)
     def _():
         sums_ref[...] = jnp.zeros_like(sums_ref)
         bsum_ref[...] = jnp.zeros_like(bsum_ref)
+        jobs = [(wo_ref, slice(None), slice(None), wo_h, wo_l)]
+        jobs += [(wu_ref, slice(None), c, wu_h, wu_l) for c in tiles]
+        jobs += [(wd_ref, c, slice(None), wd_h, wd_l) for c in tiles]
+        depth, pieces = sems.shape
+        size = width // pieces
+
+        def load(i):
+            w, r, c, _, _ = jobs[i]
+            start = r.start or 0
+            return [
+                pltpu.make_async_copy(
+                    w.at[pl.ds(start + k * size, size), c],
+                    staged.at[i % depth, pl.ds(k * size, size)],
+                    sems.at[i % depth, k],
+                )
+                for k in range(pieces)
+            ]
+
+        loads = [load(i) for i in range(len(jobs))]
+        for copies in loads[:depth]:
+            for copy in copies:
+                copy.start()
+        for i, (_, r, c, hi_ref, lo_ref) in enumerate(jobs):
+            for copy in loads[i]:
+                copy.wait()
+            hi, lo = split(staged[i % depth])
+            hi_ref[r, c] = hi
+            lo_ref[r, c] = lo
+            if i + depth < len(jobs):
+                for copy in loads[i + depth]:
+                    copy.start()
 
     b_out, gain_one, shift_one = vec_ref[0:1, :], vec_ref[1:2, :], vec_ref[2:3, :]
     b_down, gain_two, shift_two = vec_ref[3:4, :], vec_ref[4:5, :], vec_ref[5:6, :]
@@ -630,32 +852,33 @@
     attention = dots(split(x_ref[...]), wo, 1, 0) + b_out
     scaled_one, root_one = normalize(tok_ref[...] + attention)
     hidden = scaled_one * gain_one + shift_one
-    h1_ref[...] = hidden
+    h1t_ref[0] = jnp.transpose(hidden)
     hs = split(hidden)
-    ff = wu_h.shape[1]
-    tiles = [slice(c, c + ff_tile) for c in range(0, ff, ff_tile)]
     down = b_down
-    for c in tiles:
+    for i, c in enumerate(tiles):
         pre = dots(hs, (wu_h[:, c], wu_l[:, c]), 1, 0) + bup_ref[:, c]
         phi = 0.5 + 0.5 * erf(pre * 0.7071067811865476)
         slope[:, c] = phi + pre * (0.3989422804014327 * jnp.exp(-0.5 * pre * pre))
         act = pre * phi
-        act_ref[:, c] = act
-        down = down + dots(split(act), (wd_h[c, :], wd_l[c, :]), 1, 0)
+        act_ref[i] = act
+        act = split(act)
+        down = down + dots(act, (wd_h[c, :], wd_l[c, :]), 1, 0)
     scaled_two, root_two = normalize(hidden + down)
     out_ref[...] = scaled_two * gain_two + shift_two
     cot = cot_ref[...]
     r2 = norm_back(cot * gain_two, scaled_two, root_two)
-    r2_ref[...] = r2
+    r2t_ref[0] = jnp.transpose(r2)
     rs = split(r2)
     grad_hidden = r2
-    for c in tiles:
+    for i, c in enumerate(tiles):
         u = dots(rs, (wd_h[c, :], wd_l[c, :]), 1, 1) * slope[:, c]
-        u_ref[:, c] = u
+        halves = split(u)
+        u_ref[i] = u
         bsum_ref[:, c] += jnp.sum(u, axis=0, keepdims=True)
-        grad_hidden = grad_hidden + dots(split(u), (wu_h[:, c], wu_l[:, c]), 1, 1)
+        grad_hidden = grad_hidden + dots(halves, (wu_h[:, c], wu_l[:, c]), 1, 1)
     r1 = norm_back(grad_hidden * gain_one, scaled_one, root_one)
     r1_ref[...] = r1
+    r1t_ref[0] = jnp.transpose(r1)
     og_ref[...] = dots(split(r1), wo, 1, 1)
     for row, value in enumerate(
         (cot * scaled_two, cot, r2, grad_hidden * scaled_one, grad_hidden, r1)
@@ -663,42 +886,40 @@
         sums_ref[row : row + 1, :] += jnp.sum(value, axis=0, keepdims=True)
 
 
-def rows_call(x, tokens, cotangent, wo, wu, wd, vectors, b_up):
-    rows, width = x.shape
-    ff = wu[0].shape[1]
+def rows_call(x, tokens, cotangent, w_out, w_up, w_down, vectors, b_up):
+    rows, width = tokens.shape
+    ff = w_up.shape[1]
     tile = 256
-    ff_tile = 768
+    count = ff // width
     wide = pl.BlockSpec((tile, width), lambda i: (i, 0))
-    hidden = pl.BlockSpec((tile, ff), lambda i: (i, 0))
-
-    def fixed(a):
-        return pl.BlockSpec(a.shape, lambda i: (0, 0), pipeline_mode=pl.Buffered(1))
+    any_space = pl.BlockSpec(memory_space=pl.ANY)
+
+    def fixed(shape):
+        return pl.BlockSpec(shape, lambda i: (0, 0))
 
     narrow = jax.ShapeDtypeStruct((rows, width), f32)
-    broad = jax.ShapeDtypeStruct((rows, ff), f32)
+    broad = jax.ShapeDtypeStruct((count, rows, width), f32)
+    tall = jax.ShapeDtypeStruct((rows // tile, width, tile), f32)
     return pl.pallas_call(
-        functools.partial(rows_kernel, ff_tile),
-        out_shape=[
-            narrow,
-            broad,
-            broad,
-            narrow,
-            narrow,
-            narrow,
-            narrow,
-            jax.ShapeDtypeStruct((8, width), f32),
-            jax.ShapeDtypeStruct((1, ff), f32),
-        ],
+        rows_kernel,
+        out_shape=[narrow]
+        + [broad] * 2
+        + [tall] * 3
+        + [narrow, narrow, jax.ShapeDtypeStruct((8, width), f32), jax.ShapeDtypeStruct((1, ff), f32)],
         grid=(rows // tile,),
-        in_specs=[wide] * 3
-        + [fixed(a) for a in (*wo, *wu, *wd)]
-        + [fixed(vectors), fixed(b_up)],
-        out_specs=[wide, hidden, hidden, wide, wide, wide, wide]
-        + [pl.BlockSpec((8, width), lambda i: (0, 0)), pl.BlockSpec((1, ff), lambda i: (0, 0))],
-        scratch_shapes=[VM((tile, ff), f32)],
+        in_specs=[wide] * 3 + [fixed(vectors.shape), fixed(b_up.shape)] + [any_space] * 3,
+        out_specs=[wide]
+        + [pl.BlockSpec((count, tile, width), lambda i: (0, i, 0))] * 2
+        + [pl.BlockSpec((1, width, tile), lambda i: (i, 0, 0))] * 3
+        + [wide, wide, fixed((8, width)), fixed((1, ff))],
+        scratch_shapes=[VM((tile, ff), f32)]
+        + [VM((width, width), bf16)] * 2
+        + [VM((width, ff), bf16)] * 2
+        + [VM((ff, width), bf16)] * 2
+        + [VM((2, width, width), f32), pltpu.SemaphoreType.DMA((2, 6))],
         compiler_params=params(),
         name="rows",
-    )(x, tokens, cotangent, *wo, *wu, *wd, vectors, b_up)
+    )(x, tokens, cotangent, vectors, b_up, w_out, w_up, w_down)
 
 
 def one_back_kernel(per, pairs, held, k1_ref, og_ref, q_ref, lk_ref, gq_ref, chunk):
@@ -743,85 +964,94 @@
     )(blocks, k1, og, q, lk)
 
 
-def conv_back_kernel(pairs, margin, og_ref, gl_ref, gr_ref, v_ref, vl_ref, vr_ref, use_ref, taps_ref, *refs):
-    gv_ref, gtaps_ref, taps, gwin, vwin, acc = refs
-    item = pl.program_id(0)
-    span = v_ref.shape[1]
-    window = PAIR + 2 * margin
-
-    @pl.when(item == 0)
-    def _():
-        keep_taps(taps_ref, taps, 2 * pairs)
-        acc[...] = jnp.zeros_like(acc)
-
-    use = use_ref[0]
-    keep_window(gwin, gl_ref[0, 0], og_ref[0], gr_ref[0, 0], margin, span)
-    keep_window(vwin, vl_ref[0, 0], v_ref[0] * use, vr_ref[0, 0], margin, span)
-    for p in range(pairs):
-        lanes = slice(p * PAIR, (p + 1) * PAIR)
-        for block in range(span // PAIR):
-            rows = slice(block * PAIR, (block + 1) * PAIR)
-            gv_ref[0, rows, lanes] = convolve(taps, gwin, p, block, window) * use[rows]
-            inner = slice(margin + block * PAIR, margin + (block + 1) * PAIR)
-            outer = slice(block * PAIR, block * PAIR + window)
-            v = (vwin[0, outer, lanes], vwin[1, outer, lanes])
-            low = lane_low((PAIR, PAIR))
-            hi, lo = gwin[0, inner, lanes], gwin[1, inner, lanes]
-            zero = jnp.zeros_like(hi)
-            acc[2 * p] += dots((jnp.where(low, hi, zero), jnp.where(low, lo, zero)), v, 1, 1)
-            acc[2 * p + 1] += dots((jnp.where(low, zero, hi), jnp.where(low, zero, lo)), v, 1, 1)
-
-    @pl.when(item == pl.num_programs(0) - 1)
-    def _():
+class ConvBack:
+    def __init__(self, pairs, margin, og, ghalo, v, vhalo, use, taps_ref, gv, gtaps, scratch):
+        self.pairs, self.margin, self.ghalo, self.vhalo = pairs, margin, ghalo, vhalo
+        self.og, self.v, self.use, self.gv, self.gtaps = og, v, use, gv, gtaps
+        self.taps_ref = taps_ref
+        self.taps, self.gwin, self.vwin, self.acc = scratch
+        self.span = v.shape[1]
+        self.window = PAIR + 2 * margin
+
+    def begin(self):
+        keep_taps(self.taps_ref, self.taps, 2 * self.pairs)
+        self.acc[...] = jnp.zeros_like(self.acc)
+
+    def item(self, item):
+        margin, window, gwin, vwin = self.margin, self.window, self.gwin, self.vwin
+        use = self.use[item]
+        keep_window(gwin, self.ghalo[0, item], self.og[item], self.ghalo[1, item], margin, self.span)
+        values = self.v[item] * use
+        keep_window(vwin, self.vhalo[0, item], values, self.vhalo[1, item], margin, self.span)
+        for p in range(self.pairs):
+            lanes = slice(p * PAIR, (p + 1) * PAIR)
+            for block in range(self.span // PAIR):
+                rows = slice(block * PAIR, (block + 1) * PAIR)
+                self.gv[item, rows, lanes] = convolve(self.taps, gwin, p, block, window) * use[rows]
+                inner = slice(margin + block * PAIR, margin + (block + 1) * PAIR)
+                outer = slice(block * PAIR, block * PAIR + window)
+                v = (vwin[0, outer, lanes], vwin[1, outer, lanes])
+                low = lane_low((PAIR, PAIR))
+                hi, lo = gwin[0, inner, lanes], gwin[1, inner, lanes]
+                zero = jnp.zeros_like(hi)
+                first = (jnp.where(low, hi, zero), jnp.where(low, lo, zero))
+                second = (jnp.where(low, zero, hi), jnp.where(low, zero, lo))
+                self.acc[2 * p] += dots(first, v, 1, 1)
+                self.acc[2 * p + 1] += dots(second, v, 1, 1)
+
+    def end(self):
         rows = lax.broadcasted_iota(jnp.int32, (PAIR, PAIR), 0)
         flip = (rows + lax.broadcasted_iota(jnp.int32, (PAIR, PAIR), 1) == PAIR - 1).astype(bf16)
-        for h in range(2 * pairs):
-            c = acc[h]
-            c = jnp.concatenate([c, jnp.zeros((PAIR, 2 * PAIR - window), f32)], axis=1)
+        for h in range(2 * self.pairs):
+            c = self.acc[h]
+            c = jnp.concatenate([c, jnp.zeros((PAIR, 2 * PAIR - self.window), f32)], axis=1)
             hi = c.astype(bf16)
             rest = c - hi.astype(f32)
             mid = rest.astype(bf16)
             low = (rest - mid.astype(f32)).astype(bf16)
             c = dg(flip, hi, 1, 0) + dg(flip, mid, 1, 0) + dg(flip, low, 1, 0)
             c = pltpu.roll(c, 0, 1, stride=1, stride_axis=0)
-            gtaps_ref[h : h + 1, :] = jnp.sum(c, axis=0, keepdims=True)
-
-
-def conv_back_call(og, ghalos, v, vhalos, use_col, taps, pairs, margin):
-    items, span, width = v.shape
-    window = PAIR + 2 * margin
-    wide, edge = per_item((span, width)), halo_specs(margin, width)
-    rows = -(-2 * pairs // 8) * 8
-    return pl.pallas_call(
-        functools.partial(conv_back_kernel, pairs, margin),
-        out_shape=[
-            jax.ShapeDtypeStruct((items, span, width), f32),
-            jax.ShapeDtypeStruct((rows, 2 * PAIR), f32),
-        ],
-        grid=(items,),
-        in_specs=[wide, *edge, wide, *edge, per_item((span, 1)), whole(taps.shape)],
-        out_specs=[wide, whole((rows, 2 * PAIR))],
-        scratch_shapes=[
+            self.gtaps[h : h + 1, :] = jnp.sum(c, axis=0, keepdims=True)
+
+    @staticmethod
+    def scratch(pairs, margin, span, width):
+        return [
             VM((2, 2 * pairs, PAIR, 2 * PAIR), bf16),
             VM((2, span + 2 * margin, width), bf16),
             VM((2, span + 2 * margin, width), bf16),
-            VM((2 * pairs, PAIR, window), f32),
-        ],
-        compiler_params=params(),
-        name="conv_back",
-    )(og, ghalos, ghalos, v, vhalos, vhalos, use_col, taps)
-
-
-def exchange_back_kernel(n, per, chunk_ref, side_ref, ctx_ref, a_ref, z_ref, lq_ref, lk_ref,
-                         out_ref, gq_ref, gk_ref, halo_ref, gm, gz, ga, *scratch):
+            VM((2 * pairs, PAIR, PAIR + 2 * margin), f32),
+        ]
+
+
+def exchange_back_kernel(n, per, fused, *refs):
+    refs = list(refs)
+    chunk_ref, side_ref, ctx_ref, a_ref, z_ref, lq_ref, lk_ref = refs[:7]
+    r2_ref, act_ref = refs[7:9] if fused else [None] * 2
+    refs = refs[9:] if fused else refs[7:]
+    out_ref, gq_ref, gk_ref, halo_ref = refs[:4]
+    part_ref = refs[4] if fused else None
+    gm, gz, ga, *scratch = refs[5:] if fused else refs[4:]
     seat = Seat(n)
     reduce = Reduce(seat, chunk_ref, *scratch[:5])
     gather = Gather(seat, out_ref, *scratch[5:7])
-    edges = Edges(seat, side_ref, *scratch[7:])
-    seat.hello(True)
+    edges = Edges(seat, side_ref, *scratch[7:10])
+    if fused:
+        links = Links()
+        whole_ref, send, recv = scratch[10:13]
+        tiles = Tiles(links, True, r2_ref, act_ref, whole_ref, scratch[13:])
+        scatter = Scatter(0, links, [whole_ref, part_ref], send, recv)
+        seat.hello(True, links.devices[2:])
+    else:
+        seat.hello(True)
     reduce.start()
     edges.start()
     reduce.middle(add_all)
+    if fused:
+        tiles.compute(0)
+        tiles.compute(1)
+        tiles.absorb(0)
+        tiles.compute(2)
+        tiles.absorb(1)
     diagonal = diagonal_mask()
     eye = unit()
     stats = per * MARKS
@@ -853,9 +1083,17 @@
             gz[place] = dot3(g, n3, 1, 1) + dot3(jnp.transpose(a), grad)
         return 0
 
-    lax.fori_loop(0, NEWTON - 1, lap, 0)
-    gather.forward()
-    lax.fori_loop(NEWTON - 1, NEWTON, lap, 0)
+    if fused:
+        tiles.compute(3)
+        tiles.absorb(2)
+        tiles.absorb(3)
+        scatter.start()
+        gather.forward()
+        lax.fori_loop(0, NEWTON, lap, 0)
+    else:
+        lax.fori_loop(0, NEWTON - 1, lap, 0)
+        gather.forward()
+        lax.fori_loop(NEWTON - 1, NEWTON, lap, 0)
     for place in range(per):
         a, g = a_ref[place], jnp.transpose(gz[place])
         norm = head_total(a * a)
@@ -868,36 +1106,59 @@
         )
     edges.finish(halo_ref)
     gather.finish()
-
-
-def exchange_back_call(chunks, sides, ctx, a, z, lq, lk, n, rows):
+    if fused:
+        scatter.advance()
+
+
+def exchange_back_call(chunks, sides, ctx, a, z, lq, lk, n, rows, r2=None, act=None):
     per = ctx.shape[0]
     small = jax.ShapeDtypeStruct(ctx.shape, f32)
     chunk = chunks.shape[1:]
     blocks = (2, n // 2, rows, PAIR)
+    fused = r2 is not None
+    more_in, more_shapes, more_scratch = (), [], []
+    if fused:
+        more_in = (r2, act)
+        more_shapes = [jax.ShapeDtypeStruct(landing(BIG, 0), f32)]
+        more_scratch = [VM(landing(BIG, -1), f32)] + [pltpu.SemaphoreType.DMA((12,))] * 2
+        more_scratch += Tiles.scratch(*act.shape[1:])
     out = pl.pallas_call(
-        functools.partial(exchange_back_kernel, n, per),
+        functools.partial(exchange_back_kernel, n, per, fused),
         out_shape=[
             jax.ShapeDtypeStruct(blocks, f32),
             small,
             small,
             jax.ShapeDtypeStruct(sides.shape, f32),
-        ],
-        in_specs=[pl.BlockSpec(memory_space=VM)] * 7,
-        out_specs=[pl.BlockSpec(memory_space=VM)] * 4,
+        ]
+        + more_shapes,
+        in_specs=[pl.BlockSpec(memory_space=VM)] * 7
+        + [pl.BlockSpec(memory_space=pl.ANY)] * len(more_in),
+        out_specs=[pl.BlockSpec(memory_space=VM)] * (4 + len(more_shapes)),
         scratch_shapes=[VM(chunk, f32)]
         + [VM((per, PAIR, PAIR), f32)] * 2
         + Reduce.scratch(n, chunk)
         + Gather.scratch(n)
-        + Edges.scratch(sides.shape),
+        + Edges.scratch(sides.shape)
+        + more_scratch,
         compiler_params=params(collective_id=2, has_side_effects=True),
         name="exchange_back",
-    )(chunks.reshape((2, n // 2) + chunk), sides, ctx, a, z, lq, lk)
+    )(chunks.reshape((2, n // 2) + chunk), sides, ctx, a, z, lq, lk, *more_in)
     return [out[0].reshape(n, rows, PAIR)] + list(out[1:])
 
 
-def three_back_kernel(per, pairs, held, stat, w3_ref, top_ref, v_ref, k_ref, gvc_ref, lq_ref,
-                      gv_ref, gk_ref, chunk):
+def keep_both(value, lanes, out_ref, turned_ref):
+    out_ref[0, :, lanes] = value
+    turned_ref[0, lanes, :] = jnp.transpose(value)
+
+
+def both_specs(items, span, width):
+    shapes = [(items, span, width), (items, width, span)]
+    shapes = [jax.ShapeDtypeStruct(shape, f32) for shape in shapes]
+    return shapes, [per_item((span, width)), per_item((width, span))]
+
+
+def three_back_kernel(per, pairs, held, stat, w3_ref, top_ref, v_ref, k_ref, lq_ref,
+                      gk_ref, gv_ref, chunk):
     item = pl.program_id(0)
     stats = per * MARKS
 
@@ -916,13 +1177,13 @@
         k3 = w3_ref[0, lanes, :] * scale[:, 0:1]
         gk3 = dots(grad, split(v_ref[0, :, lanes]), 1, 1)
         scores = split(k3 * (gk3 - row_dot[:, 0:1]))
-        gv_ref[0, :, lanes] = gvc_ref[0, :, lanes] + dots(split(k3), grad, 0, 0)
+        gv_ref[0, :, lanes] = dots(split(k3), grad, 0, 0)
         gk_ref[0, :, lanes] = dots(scores, split(spread(lq_ref[0, :, lanes])), 0, 0)
         part = compacted(dots(scores, split(k_ref[0, :, lanes]), 1, 0))
         chunk[owner, pl.ds(pl.multiple_of(place * MARKS, MARKS), MARKS), :] = part
 
 
-def three_back_call(grads, blocks, w3, top, v, k, gv_conv, lq, per, pairs):
+def three_back_call(grads, blocks, w3, top, v, k, lq, per, pairs):
     items, span, width = v.shape
     out = (blocks.shape[0], per * MARKS, PAIR)
     wide = per_item((span, width))
@@ -932,48 +1193,111 @@
         out_shape=[shape, shape, jax.ShapeDtypeStruct(out, f32)],
         grid=(items,),
         in_specs=[whole(blocks.shape)] * 2
-        + [per_item((width, span)), per_item((8, PAIR)), wide, wide, wide]
+        + [per_item((width, span)), per_item((8, PAIR)), wide, wide]
         + [per_item((MARKS, width))],
         out_specs=[wide, wide, whole(out)],
         compiler_params=params(),
         name="three_back",
-    )(grads, blocks, w3, top, v, k, gv_conv, lq)
-
-
-def land_exchange_kernel(n, per, chunk_ref, q_ref, k_ref, out_ref, *scratch):
+    )(grads, blocks, w3, top, v, k, lq)
+
+
+def land_exchange_kernel(n, per, pairs, margin, fused, *refs):
+    refs = list(refs)
+    chunk_ref, q_ref, k_ref = refs[:3]
+    convolution, refs = refs[3:9], refs[9:]
+    if fused:
+        in_down, hid_ref, u_ref, out_ref, gv_ref, gtaps_ref, down_ref, part_ref, *scratch = refs
+    else:
+        out_ref, gv_ref, gtaps_ref, *scratch = refs
+    conv = ConvBack(pairs, margin, *convolution, gv_ref, gtaps_ref, scratch[:4])
+    scratch = scratch[4:]
+
+    def conv_lap(item, _):
+        conv.item(item)
+        return 0
+
     seat = Seat(n)
     reduce = Reduce(seat, chunk_ref, *scratch[:5])
-    gather = Gather(seat, out_ref, *scratch[5:])
-    seat.hello(False)
+    gather = Gather(seat, out_ref, *scratch[5:7])
+    if fused:
+        links = Links()
+        second, third, whole_ref, send, recv = scratch[7:12]
+        down = Scatter(0, links, [in_down, second, third, down_ref], send, recv, 1)
+        up = Scatter(1, links, [whole_ref, part_ref], send, recv)
+        tiles = Tiles(links, False, hid_ref, u_ref, whole_ref, scratch[12:])
+        seat.hello(False, links.devices[2:])
+    else:
+        seat.hello(False)
     reduce.start()
     reduce.middle(add_all)
+    if fused:
+        down.start()
+        tiles.compute(0)
     half = per * MARKS
     block = out_ref.at[seat.core, seat.z]
     block[half:, :] = k_ref[...]
     block[:half, :] = q_ref[...] + reduce.finish(add_all)
     gather.start()
+    if fused:
+        tiles.compute(1)
+        tiles.absorb(0)
+        down.advance()
+        tiles.compute(2)
+        tiles.absorb(1)
+        tiles.compute(3)
+        tiles.absorb(2)
+        down.advance()
+    conv.begin()
+    items = gv_ref.shape[0]
+    if fused:
+        tiles.absorb(3)
+        up.start()
+    lax.fori_loop(0, items // 2, conv_lap, 0)
     gather.forward()
+    lax.fori_loop(items // 2, items, conv_lap, 0)
+    conv.end()
     gather.finish()
-
-
-def land_exchange_call(chunks, own_q, own_k, n):
+    if fused:
+        down.advance()
+        up.advance()
+
+
+def land_exchange_call(chunks, own_q, own_k, convolution, n, pairs, margin, in_down=None, hidden=None, u=None):
     per = own_q.shape[0]
     half = per * MARKS
     blocks = (2, n // 2, 2 * half, PAIR)
-    return pl.pallas_call(
-        functools.partial(land_exchange_kernel, n, per),
-        out_shape=jax.ShapeDtypeStruct(blocks, f32),
-        in_specs=[pl.BlockSpec(memory_space=VM)] * 3,
-        out_specs=pl.BlockSpec(memory_space=VM),
-        scratch_shapes=Reduce.scratch(n, (half, PAIR)) + Gather.scratch(n),
+    fused = in_down is not None
+    conv_shapes = [convolution[0].shape, (-(-2 * pairs // 8) * 8, 2 * PAIR)]
+    vmem = pl.BlockSpec(memory_space=VM)
+    more_in, more_specs, more_shapes, more_scratch = (), [], [], []
+    if fused:
+        more_in = (in_down, hidden, u)
+        more_specs = [vmem] + [pl.BlockSpec(memory_space=pl.ANY)] * 2
+        more_shapes = [landing(BIG, 3), landing(BIG, 0)]
+        more_scratch = [VM(landing(BIG, stage), f32) for stage in (1, 2, -1)]
+        more_scratch += [pltpu.SemaphoreType.DMA((24,))] * 2
+        more_scratch += Tiles.scratch(*u.shape[1:])
+    out = pl.pallas_call(
+        functools.partial(land_exchange_kernel, n, per, pairs, margin, fused),
+        out_shape=[jax.ShapeDtypeStruct(shape, f32) for shape in [blocks, *conv_shapes] + more_shapes],
+        in_specs=[vmem] * 9 + more_specs,
+        out_specs=[vmem] * (3 + len(more_shapes)),
+        scratch_shapes=ConvBack.scratch(pairs, margin, *convolution[0].shape[1:])
+        + Reduce.scratch(n, (half, PAIR)) + Gather.scratch(n) + more_scratch,
         compiler_params=params(collective_id=3, has_side_effects=True),
         name="land_exchange",
-    )(chunks.reshape(2, n // 2, half, PAIR), own_q.reshape(half, PAIR), own_k.reshape(half, PAIR)).reshape(
-        n, 2 * half, PAIR
+    )(
+        chunks.reshape(2, n // 2, half, PAIR),
+        own_q.reshape(half, PAIR),
+        own_k.reshape(half, PAIR),
+        *convolution,
+        *more_in,
     )
-
-
-def land_back_kernel(per, pairs, factor, held, gq_ref, gk_ref, gv_ref, mem_ref, inv_ref, oq_ref, ok_ref, sums_ref):
+    return [out[0].reshape(n, 2 * half, PAIR)] + list(out[1:])
+
+
+def land_back_kernel(per, pairs, factor, held, gq_ref, gk_ref, gv_ref, gvc_ref, mem_ref, inv_ref, *outs):
+    sums_ref = outs[6]
     item = pl.program_id(0)
     half = per * MARKS
 
@@ -986,29 +1310,184 @@
     for p in range(pairs):
         lanes = slice(p * PAIR, (p + 1) * PAIR)
         slot, place = owned_by(item * pairs + p, per)
-        for ref, out, base in ((gq_ref, oq_ref, 0), (gk_ref, ok_ref, half)):
+        for ref, out, base in ((gq_ref, outs[:2], 0), (gk_ref, outs[2:4], half)):
             grad = held[slot, pl.ds(pl.multiple_of(base + place * MARKS, MARKS), MARKS), :]
             hi, lo = split(grad * inv)
             landed = dg(member, hi, 0, 0) + dg(member, lo, 0, 0)
-            out[0, :, lanes] = (ref[0, :, lanes] + landed) * factor
-        sums_ref[0:1, lanes] += jnp.sum(oq_ref[0, :, lanes], axis=0, keepdims=True)
-        sums_ref[1:2, lanes] += jnp.sum(gv_ref[0, :, lanes], axis=0, keepdims=True)
-
-
-def land_back_call(blocks, gq, gk, gv, member_t, inv, per, pairs, factor):
+            total = (ref[0, :, lanes] + landed) * factor
+            keep_both(total, lanes, *out)
+            if base == 0:
+                sums_ref[0:1, lanes] += jnp.sum(total, axis=0, keepdims=True)
+        total = gv_ref[0, :, lanes] + gvc_ref[0, :, lanes]
+        keep_both(total, lanes, *outs[4:6])
+        sums_ref[1:2, lanes] += jnp.sum(total, axis=0, keepdims=True)
+
+
+def land_back_call(blocks, gq, gk, gv, gv_conv, member_t, inv, per, pairs, factor):
     items, span, width = gq.shape
     wide = per_item((span, width))
-    shape = jax.ShapeDtypeStruct((items, span, width), f32)
-    return pl.pallas_call(
+    shapes, specs = both_specs(items, span, width)
+    out = pl.pallas_call(
         functools.partial(land_back_kernel, per, pairs, factor),
-        out_shape=[shape, shape, jax.ShapeDtypeStruct((8, width), f32)],
+        out_shape=shapes * 3 + [jax.ShapeDtypeStruct((8, width), f32)],
         grid=(items,),
-        in_specs=[whole(blocks.shape), wide, wide, wide]
+        in_specs=[whole(blocks.shape)] + [wide] * 4
         + [per_item((MARKS, span)), per_item((MARKS, PAIR))],
-        out_specs=[wide, wide, whole((8, width))],
+        out_specs=specs * 3 + [whole((8, width))],
         compiler_params=params(),
         name="land_back",
-    )(blocks, gq, gk, gv, member_t, inv)
+    )(blocks, gq, gk, gv, gv_conv, member_t, inv)
+    return out[:2], out[2:4], out[4:6], out[6]
+
+
+def grads_kernel(
+    r1t_ref, x_ref, gqt_ref, gkt_ref, gvt_ref, tok_ref, gq_ref, gk_ref, gv_ref, wq_ref, wk_ref, wv_ref, r1_ref,
+    in_up, sums_ref, late_ref, bsum_ref, taps_ref,
+    vo_ref, up_ref, qk_ref, gt_ref, total_ref,
+    s_slots, s_first, s_second, t_slots, w_s, p_pair, *scratch
+):
+    vo_bufs, qk_bufs, up_bufs = list(scratch[:4]), list(scratch[4:8]), list(scratch[8:10])
+    held, caught, load_sem, s_sem, t_sem, core_send, core_recv, send, recv, sum_send, sum_recv = scratch[10:]
+    links = Links()
+    width = tok_ref.shape[1]
+    ff = bsum_ref.shape[1]
+    s_loads = Loads([gvt_ref, r1t_ref, gqt_ref, gkt_ref], s_slots, s_sem)
+    t_loads = Loads(
+        [tok_ref, x_ref, gv_ref, wv_ref, gq_ref, wq_ref, gk_ref, wk_ref], t_slots, t_sem
+    )
+    residual = pltpu.make_async_copy(r1_ref, gt_ref, load_sem.at[0])
+    residual.start()
+    barrier = pltpu.get_barrier_semaphore()
+    for device in (links.partner, *links.devices):
+        pl.semaphore_signal(barrier, inc=1, device_id=device, device_id_type=MESH)
+    pl.semaphore_wait(barrier, 5)
+    up = Scatter(0, links, [in_up, *up_bufs, up_ref], send, recv, 1, EVEN)
+    vo = Scatter(1, links, [*vo_bufs, vo_ref], send, recv, orders=EVEN)
+    qk = Scatter(2, links, [*qk_bufs, qk_ref], send, recv, orders=EVEN)
+    up.start()
+
+    def halfway(step):
+        return pltpu.make_async_remote_copy(
+            src_ref=held.at[step], dst_ref=caught.at[step],
+            send_sem=sum_send.at[step], recv_sem=sum_recv.at[step],
+            device_id=(links.partner, *links.devices)[step], device_id_type=MESH,
+        )
+
+    held[0] = jnp.zeros(held.shape[1:], f32)
+    held[0, 0:8, :] = sums_ref[...]
+    held[0, 8:16, :] = late_ref[...]
+    for i, t in enumerate(range(0, ff, width)):
+        held[0, 16 + i : 17 + i, :] = bsum_ref[:, t : t + width]
+    held[0, 24:40, : 2 * PAIR] = taps_ref[...]
+    halfway(0).start()
+
+    def sums_on(step):
+        halfway(step).wait()
+        added = held[step] + caught[step]
+        if step < 4:
+            held[step + 1] = added
+            halfway(step + 1).start()
+        else:
+            total_ref[...] = added
+
+    def pair_job(first, second, t_first, t_second):
+        half = PAIR // 2
+        for which, (s, t) in enumerate(((first, t_first), (second, t_second))):
+            for third in range(3):
+                g = times(s, t, slice(third * 256, (third + 1) * 256))
+                for unit in range(4):
+                    block, k = divmod(4 * third + unit, 3)
+                    color, side = divmod(3 * which + k, 2)
+                    lanes = slice(side * half, (side + 1) * half)
+                    for j in range(8):
+                        at = (links.apart[j % 2], color, j // 4, j // 2 % 2, block // 2, block % 2)
+                        p_pair[(*at, slice(None), lanes)] = g[
+                            j * 96 : (j + 1) * 96, unit * half : (unit + 1) * half
+                        ]
+
+    def absorb(copy, buffer):
+        copy.wait()
+        buffer[...] = buffer[...] + p_pair[0]
+
+    def token_job(i):
+        x, w = t_loads.get(2 + 2 * i), t_loads.get(3 + 2 * i)
+        halved(w, w_s)
+        for c in range(0, gt_ref.shape[0], 2 * PAIR):
+            rows = slice(c, c + 2 * PAIR)
+            gt_ref[rows, :] += dots(split(x[rows, :]), (w_s[0], w_s[1]), 1, 1)
+        t_loads.release(2 + 2 * i)
+        t_loads.release(3 + 2 * i)
+
+    tokens = t_loads.get(0)
+    halved(s_loads.get(0), s_first)
+    s_loads.release(0)
+    halved(s_loads.get(1), s_second)
+    s_loads.release(1)
+    pair_job(s_first, s_second, tokens, t_loads.get(1))
+    t_loads.release(1)
+    vo_copy = links.copy(0, p_pair.at[1], vo_bufs[0], core_send, core_recv)
+    vo_copy.start()
+    sums_on(0)
+    up.advance()
+    residual.wait()
+    token_job(0)
+    absorb(vo_copy, vo_bufs[0])
+    vo.start()
+    halved(s_loads.get(2), s_first)
+    halved(s_loads.get(3), s_second)
+    pair_job(s_first, s_second, tokens, tokens)
+    t_loads.release(0)
+    qk_copy = links.copy(1, p_pair.at[1], qk_bufs[0], core_send, core_recv)
+    qk_copy.start()
+    vo.advance()
+    up.advance()
+    sums_on(1)
+    token_job(1)
+    absorb(qk_copy, qk_bufs[0])
+    qk.start()
+    vo.advance()
+    sums_on(2)
+    token_job(2)
+    up.advance()
+    qk.advance()
+    vo.advance()
+    sums_on(3)
+    qk.advance()
+    sums_on(4)
+    vo.advance()
+    qk.advance()
+    qk.advance()
+
+
+def grads_call(arrays, r1, in_up, sums):
+    rows, width = r1.shape
+    any_space = pl.BlockSpec(memory_space=pl.ANY)
+    vmem = pl.BlockSpec(memory_space=VM)
+    dma = pltpu.SemaphoreType.DMA
+    out_shapes = [
+        landing(SMALL, 3), landing(BIG, 3), landing(SMALL, 3), (rows, width), (40, width),
+    ]
+    return pl.pallas_call(
+        grads_kernel,
+        out_shape=[jax.ShapeDtypeStruct(shape, f32) for shape in out_shapes],
+        in_specs=[any_space] * (len(arrays) + 1) + [vmem] * (1 + len(sums)),
+        out_specs=[vmem] * 5,
+        scratch_shapes=[
+            VM((2, width, rows), f32),
+            VM((2, width, rows), bf16),
+            VM((2, width, rows), bf16),
+            VM((4, rows, width), f32),
+            VM((2, width, width), bf16),
+            VM((2, 3, 2, 2, 2, 2) + SMALL, f32),
+        ]
+        + [VM(landing(SMALL, stage), f32) for stage in (-1, 0, 1, 2)] * 2
+        + [VM(landing(BIG, stage), f32) for stage in (1, 2)]
+        + [VM((5, 40, width), f32)] * 2
+        + [dma((1,)), dma((2, 4)), dma((4, 1)), dma((2,)), dma((2,))]
+        + [dma((36,)), dma((36,)), dma((5,)), dma((5,))],
+        compiler_params=params(collective_id=4, has_side_effects=True),
+        name="grads",
+    )(*arrays, r1, in_up, *sums)
 
 
 def swap(x, axis, offset):
@@ -1082,11 +1561,6 @@
         for bit in powers(axis):
             x = x + swap(x, axis, bit)
     return x
-
-
-def rounded_pair(w):
-    hi = lax.reduce_precision(w, 8, 7)
-    return hi.astype(bf16), (w - hi).astype(bf16)
 
 
 def product(a, b, ca, cb):
@@ -1145,81 +1619,92 @@
     kernel_two, z, owned_q, owned_k, context, mixed, vhalos = exchange_call(
         chunks, land_q, land_k, both_sides(values, margin) * use_sides, n, per, pairs
     )
-    attn_input = mix_call(mixed, k1, values, use_col, vhalos, taps_forward, per, pairs, margin)
-
-    vectors = jnp.stack(
-        [b_out, gain_one, shift_one, b_down, gain_two, shift_two, b_out, b_out]
-    )
-    x = attn_input.reshape(items * span, width)
-    output, act, u, r2, hidden, r1, og, row_sums, up_sums = rows_call(
-        x,
-        rows,
-        cotangent.reshape(items * span, width),
-        rounded_pair(w_out),
-        rounded_pair(w_up),
-        rounded_pair(w_down),
-        vectors,
-        b_up[None, :],
+    x = mix_call(mixed, k1, values, use_col, vhalos, taps_forward, per, pairs, margin)
+
+    def flat(array):
+        return array.reshape(items * span, width)
+
+    x = flat(x)
+    vectors = jnp.stack([b_out, gain_one, shift_one, b_down, gain_two, shift_two])
+    output, act, u, r2_t, hidden_t, r1_t, r1, og, row_sums, up_sums = rows_call(
+        x, rows, cotangent.reshape(items * span, width), w_out, w_up, w_down, vectors, b_up[None, :]
     )
     og = og.reshape(items, span, width)
     grad_queries, chunks = one_back_call(mixed, k1, og, queries, land_k, per, pairs)
-    grad_context, own_q, own_k, ghalos = exchange_back_call(
-        chunks, both_sides(og, margin), context, kernel_two, z, owned_q, owned_k, n, chunk_rows
+    ff = w_up.shape[1]
+    fused = (n, lax.axis_size("dp"), width, ff) == (8, 4, 768, 3072)
+    grad_context, own_q, own_k, ghalos, *down_part = exchange_back_call(
+        chunks, both_sides(og, margin), context, kernel_two, z, owned_q, owned_k, n, chunk_rows,
+        *((r2_t, act) if fused else ()),
     )
-    gv_conv, grad_taps = conv_back_call(
-        og, ghalos, values, vhalos, use_col, taps_backward, pairs, margin
+    grad_keys, grad_values, chunks = three_back_call(
+        grad_context, mixed, w3, top, values, key_rows, land_q, per, pairs
     )
-    grad_values, grad_keys, chunks = three_back_call(
-        grad_context, mixed, w3, top, values, key_rows, gv_conv, land_q, per, pairs
+    land_grads, gv_conv, grad_taps, *ff_grads = land_exchange_call(
+        chunks, own_q, own_k, (og, ghalos, values, vhalos, use_col, taps_backward), n, pairs, margin,
+        *((*down_part, hidden_t, u) if fused else ()),
     )
-    land_grads = land_exchange_call(chunks, own_q, own_k, n)
-    grad_queries, grad_keys, late_sums = land_back_call(
-        land_grads, grad_queries, grad_keys, grad_values, member_t, inverse_divisor,
-        per, pairs, factor,
+    gq, gk, gv, late_sums = land_back_call(
+        land_grads, grad_queries, grad_keys, grad_values, gv_conv,
+        member_t, inverse_divisor, per, pairs, factor,
     )
-    grad_w_down = scatter_sum(product(r2, act, 0, 0), "yxzz")
-    grad_w_up = scatter_sum(product(u, hidden, 0, 0), "xzyz")
-    grad_w_out = scatter_sum(product(r1, x, 0, 0), "zyxz")
-    grad_queries = grad_queries.reshape(items * span, width)
-    grad_keys = grad_keys.reshape(items * span, width)
-    grad_values = grad_values.reshape(items * span, width)
-    grad_w_value = scatter_sum(product(grad_values, rows, 0, 0), "zyxz")
-    grad_w_query = scatter_sum(product(grad_queries, rows, 0, 0), "yxzz")
-    grad_w_key = scatter_sum(product(grad_keys, rows, 0, 0), "xzyz")
-    grad_tokens = (
-        r1
-        + product(grad_values, w_value, 1, 1)
-        + product(grad_queries, w_query, 1, 1)
-        + product(grad_keys, w_key, 1, 1)
-    )
-
-    early = sum_everywhere(
-        jnp.concatenate([row_sums.reshape(-1), up_sums.reshape(-1), grad_taps.reshape(-1)]).reshape(
-            -1, PAIR
+    if fused:
+        down, up_part = ff_grads
+        vo, up, qk, grad_tokens, totals = grads_call(
+            [r1_t, x, gq[1], gk[1], gv[1], rows, flat(gq[0]), flat(gk[0]), flat(gv[0])]
+            + [w_query, w_key, w_value],
+            r1,
+            up_part,
+            [row_sums, late_sums, up_sums, grad_taps],
         )
-    ).reshape(-1)
-    late = sum_everywhere(late_sums)
-    row_sums = early[: 8 * width].reshape(8, width)
-    ff = w_up.shape[1]
-    up_sums = early[8 * width : 8 * width + ff]
-    grad_taps = early[8 * width + ff :].reshape(-1, 2 * PAIR)
-    grad_conv = grad_taps[:heads, PAIR - 1 : PAIR - 1 + taps]
+        vo, qk = (jnp.transpose(both, (0, 2, 1)).reshape(2, -1, both.shape[1]) for both in (vo, qk))
+        grad_w_value, grad_w_out = vo[0], vo[1]
+        grad_w_query, grad_w_key = qk[0], qk[1]
+        down = down.reshape(3, 2, -1, PAIR)
+        grad_w_down = jnp.transpose(down, (0, 1, 3, 2)).reshape(-1, down.shape[2])
+        grad_w_up = jnp.transpose(up, (1, 0, 2)).reshape(up.shape[1], -1)
+    else:
+        def unturned(array):
+            return flat(jnp.swapaxes(array, 1, 2))
+
+        def untiled(array):
+            return jnp.swapaxes(array, 0, 1).reshape(items * span, ff)
+
+        gq, gk, gv = (flat(pair[0]) for pair in (gq, gk, gv))
+        grad_w_down = scatter_sum(product(unturned(r2_t), untiled(act), 0, 0), "yxzz").T
+        grad_w_up = scatter_sum(product(untiled(u), unturned(hidden_t), 0, 0), "xzyz").T
+        grad_w_out = scatter_sum(product(r1, x, 0, 0), "zyxz").T
+        grad_w_value = scatter_sum(product(gv, rows, 0, 0), "zyxz").T
+        grad_w_query = scatter_sum(product(gq, rows, 0, 0), "yxzz").T
+        grad_w_key = scatter_sum(product(gk, rows, 0, 0), "xzyz").T
+        grad_tokens = (
+            r1
+            + product(gv, w_value, 1, 1)
+            + product(gq, w_query, 1, 1)
+            + product(gk, w_key, 1, 1)
+        )
+        taps_rows = jnp.pad(grad_taps, ((0, 0), (0, width - grad_taps.shape[1])))
+        up_rows = jnp.pad(up_sums.reshape(-1, width), ((0, 8 - ff // width), (0, 0)))
+        totals = sum_everywhere(jnp.concatenate([row_sums, late_sums, up_rows, taps_rows]))
+    row_sums, late = totals[:8], totals[8:16]
+    up_sums = totals[16 : 16 + ff // width].reshape(ff)
+    grad_conv = totals[24 : 24 + heads, PAIR - 1 : PAIR - 1 + taps]
     return (
         output.reshape(tokens.shape),
         grad_tokens.reshape(tokens.shape),
-        grad_w_query.T,
+        grad_w_query,
         late[0],
-        grad_w_key.T,
-        grad_w_value.T,
+        grad_w_key,
+        grad_w_value,
         late[1],
         grad_conv,
-        grad_w_out.T,
+        grad_w_out,
         row_sums[5],
         row_sums[3],
         row_sums[4],
-        grad_w_up.T,
+        grad_w_up,
         up_sums,
-        grad_w_down.T,
+        grad_w_down,
         row_sums[2],
         row_sums[0],
         row_sums[1],

time: 747 us -> 527 us (0.71); the launches traced: 749 us -> 517 us
  waiting for transfers between devices: 136 us -> 0 us
  Pallas kernels: 359 us -> 481 us
  matrix products: 82.4 us -> 0 us
  other arithmetic: 56.7 us -> 6.05 us
  local copies, waits for them, and re-layouts: 74.1 us -> 28.1 us
  starting transfers between devices: 39.8 us -> 0 us
    ppermute x40 -> x0, waiting for transfers between devices: 136 us -> none  [swap(): return lax.ppermute(x, axis, [(i, i ^ offset) for i in range(count)])]
    pallas_call x4, Pallas kernels: 227 us -> 350 us  [the longest x1 143 us: rows_call(): pl.pallas_call(rows_kernel, out_shape=[narrow] + [broad] * 2 + [tall] * 3...]
    dot_general x9 -> x0, matrix products: 82.4 us -> none  [product(): return lax.dot_general(a, b, (((ca,), (cb,)), ((), ())), precision=HIGH)]
    ppermute x40 -> x0, starting transfers between devices: 39.8 us -> none  [swap(): return lax.ppermute(x, axis, [(i, i ^ offset) for i in range(count)])]
    add x34 -> x0, other arithmetic: 23.3 us -> none  [the longest x12 13.3 us: halve_rows(): return keep + swap(send, 'seq', bit)]
    convert_element_type x3 -> x0, other arithmetic: 18.2 us -> none  [rounded_pair(): return (hi.astype(bf16), (w - hi).astype(bf16))]
    squeeze x19 -> x2, local copies, waits for them, and re-layouts: 16.8 us -> 1.38 us  [the longest x1 0.69 us: on_device(): grad_w_query, grad_w_key = (qk[0], qk[1])]
    dot_general x4 -> x0, local copies, waits for them, and re-layouts: 14.9 us -> none  [product(): return lax.dot_general(a, b, (((ca,), (cb,)), ((), ())), precision=HIGH)]
  transfers between devices with their start and end apart: 40 -> 0, of which waited for: 15 -> 0; matrix products, arithmetic and copies ran while one was open for 19% -> 0% of each run, Pallas kernels for 19% -> 0%
where the time goes in v4:
time: 527 us; the launch traced here: 517 us
  Pallas kernels  481 us (91%)
  local copies, waits for them, and re-layouts  28.1 us (5%)
  other arithmetic  6.05 us (1%)
    pallas_call x1, Pallas kernels, rows_call(): pl.pallas_call(rows_kernel, out_shape=[narrow] + [broad] * 2 + [tall] * 3...  143 us
    pallas_call x1, Pallas kernels, grads_call(): pl.pallas_call(grads_kernel, out_shape=[jax.ShapeDtypeStruct(shape, f32)...  78.8 us
    pallas_call x1, Pallas kernels, land_exchange_call(): pl.pallas_call(functools.partial(land_exchange_kernel, n, per, pairs, mar...  68 us
    pallas_call x1, Pallas kernels, exchange_back_call(): pl.pallas_call(functools.partial(exchange_back_kernel, n, per, fused), ou...  60.3 us
    pallas_call x1, Pallas kernels, project_call(): pl.pallas_call(functools.partial(project_kernel, n, items, factor), out_s...  37.7 us
    pallas_call x1, Pallas kernels, exchange_call(): pl.pallas_call(functools.partial(exchange_kernel, n, per, pairs), out_sha...  29.8 us
    pallas_call x1, Pallas kernels, three_back_call(): pl.pallas_call(functools.partial(three_back_kernel, per, pairs), out_shap...  14.2 us
    pallas_call x1, Pallas kernels, land_back_call(): pl.pallas_call(functools.partial(land_back_kernel, per, pairs, factor), o...  13.6 us

profile of v4, /device:TPU:0, one launch (start us, length us, event | category | flops | bytes accessed | tf_op | source)
XLA Modules:
  0.0 516.8 jit_solution(18339133928803013423)
XLA Ops:
  0.7 0.8 fusion.2
  1.5 0.7 sign.15
  2.1 0.8 compare_select_fusion
  3.0 0.7 fusion.mem_ref
  3.7 0.7 stack.58
  4.4 0.7 stack.57
  5.1 0.6 pad_maximum_fusion.1.vec_ref
  5.7 37.7 %project.1 = (f32[4,256,768]{2,1,0:T(8,128)}, f32[4,256,768]{2,1,0:T(8,128)}, f32[4,256,768]{2,1,0:T(8,128)}, f32[4,64,768]{2,1,0:T(8,128)}, f32[4,64,768]{2,1,0:T(8,128)}, /*index=5*/f32[4,64,128]{2,1,0:T(8,128)}) custom-call(f32[4,256,768]{2,1,0:T(8,128)} %tok_ref.1, f32[4,64,256]{2,1,0:T(8,128)} %fusion.mem_ref, f32[768,768]{1,0:T(8,128)} %wq_ref.3, ...), custom_call_target="tpu_custom_call" | custom-call | tf_op jit(solution)/shard_map/project/pallas_call | solution.py:495
  43.4 1.3 broadcast_in_dim.20.use_ref
  44.7 12.8 %scores.1 = (f32[4,768,256]{2,1,0:T(8,128)}, f32[4,768,256]{2,1,0:T(8,128)}, f32[4,8,128]{2,1,0:T(8,128)}, f32[8,200,128]{2,1,0:T(8,128)}) custom-call(f32[4,256,768]{2,1,0:T(8,128)} %get-tuple-element.72.q_ref, f32[4,256,768]{2,1,0:T(8,128)} %get-tuple-element.73.k_ref, f32[4,256,768]{2,1,0:T(8,128)} %get-tuple-element.74.v_ref.refs_5_, ...), custom_call_target="tpu_custom_call" | custom-call | tf_op jit(solution)/shard_map/scores/pallas_call | solution.py:550
  57.5 1.1 slice_bitcast_fusion.3
  58.6 0.8 fusion.4
  59.4 0.6 copy-done.2
  60.1 0.9 maximum_multiply_fusion.side_ref
  60.9 29.8 %exchange.1 = (f32[3,128,128]{2,1,0:T(8,128)}, f32[7,3,128,128]{3,2,1,0:T(8,128)}, f32[3,64,128]{2,1,0:T(8,128)}, f32[3,64,128]{2,1,0:T(8,128)}, f32[3,64,128]{2...) custom-call(f32[2,4,200,128]{3,2,1,0:T(8,128)} %bitcast.75, ...), custom_call_target="tpu_custom_call" | custom-call | tf_op jit(solution)/shard_map/exchange/pallas_call | solution.py:664
  90.7 1.7 copy.40.use_ref.refs_7_
  92.5 1.3 pad.7.taps_ref
  93.8 10.7 %mix.1 = f32[4,256,768]{2,1,0:T(8,128)} custom-call(f32[8,200,128]{2,1,0:T(8,128)} %bitcast.64, f32[4,768,256]{2,1,0:T(8,128)} %get-tuple-element.79.k1_ref, f32[4,256,768]{2,1,0:T(8,128)} %get-tuple-element.74.v_ref.refs_5_, f32[4,256,1]{2,1,0:T(8,128)} %copy.40.use_ref.refs_7_, f32[2,4,16,768]{3,2,1,0:T(8,128)} %get-tuple-element.80.left_ref.right_ref.refs_6_, ...), custom_call_target="tpu_custom_call" | custom-call | tf_op jit(solution)/shard_map/mix/pallas_call | solution.py:754
  104.5 0.7 stack.66
  105.2 0.7 stack.67
  105.9 0.7 stack.68
  106.6 0.7 stack.69
  107.3 0.7 stack.70
  108.0 0.7 stack.71
  108.7 0.6 stack.72.vec_ref
  109.3 142.6 %rows.1 = (f32[1024,768]{1,0:T(8,128)}, f32[4,1024,768]{2,1,0:T(8,128)}, f32[4,1024,768]{2,1,0:T(8,128)}, f32[4,768,256]{2,1,0:T(8,128)}, f32[4,768,256]{2,1,0:T...) custom-call(f32[1024,768]{1,0:T(8,128)} %bitcast.59, ...), custom_call_target="tpu_custom_call" | custom-call | tf_op jit(solution)/shard_map/rows/pallas_call | solution.py:903
  251.9 12.9 %one_back.1 = (f32[4,256,768]{2,1,0:T(8,128)}, f32[8,384,128]{2,1,0:T(8,128)}) custom-call(f32[8,200,128]{2,1,0:T(8,128)} %bitcast.65, f32[4,768,256]{2,1,0:T(8,128)} %get-tuple-element.79.k1_ref, f32[4,256,768]{2,1,0:T(8,128)} %bitcast.61, f32[4,256,768]{2,1,0:T(8,128)} %get-tuple-element.72.q_ref, f32[4,64,768]{2,1,0:T(8,128)} %get-tuple-element.76.lk_ref), custom_call_target="tpu_custom_call" | custom-call | tf_op jit(solution)/shard_map/one_back/pallas_call | solution.py:952
  264.7 1.1 slice_bitcast_fusion.1
  265.8 0.8 pad_maximum_fusion.refs_1_
  266.6 60.3 %exchange_back.1 = (f32[2,4,200,128]{3,2,1,0:T(8,128)}, f32[3,64,128]{2,1,0:T(8,128)}, f32[3,64,128]{2,1,0:T(8,128)}, f32[2,4,16,768]{3,2,1,0:T(8,128)}, f32[3,2,2,2,192,128]{5,4,3,2,1,0:T(8,128)}) custom-call(f32[2,4,384,128]{3,2,1,0:T(8,128)} %bitcast.73, f32[2,4,16,768]{3,2,1,0:T(8,128)} %pad_maximum_fusion.refs_1_, ...), custom_call_target="tpu_custom_call" | custom-call | tf_op jit(solution)/shard_map/exchange_back/pallas_call | solution.py:1125
  326.8 14.2 %three_back.1 = (f32[4,256,768]{2,1,0:T(8,128)}, f32[4,256,768]{2,1,0:T(8,128)}, f32[8,192,128]{2,1,0:T(8,128)}) custom-call(f32[8,200,128]{2,1,0:T(8,128)} %bitcast.74, f32[8,200,128]{2,1,0:T(8,128)} %bitcast.66, f32[4,768,256]{2,1,0:T(8,128)} %get-tuple-element.93.w3_ref, f32[4,8,128]{2,1,0:T(8,128)} %get-tuple-element.94.top_ref, ...), custom_call_target="tpu_custom_call" | custom-call | tf_op jit(solution)/shard_map/three_back/pallas_call | solution.py:1191
  341.0 0.8 rev.3
  341.8 0.6 pad.8.refs_8_
  342.4 68.0 %land_exchange.1 = (f32[2,4,384,128]{3,2,1,0:T(8,128)}, f32[4,256,768]{2,1,0:T(8,128)}, f32[16,256]{1,0:T(8,128)}, f32[3,192,128]{2,1,0:T(8,128)}, f32[3,2,2,2,192,128]{5,4,3,2,1,0:T(8,128)}) custom-call(f32[2,4,192,128]{3,2,1,0:T(8,128)} %bitcast.76, f32[192,128]{1,0:T(8,128)} %bitcast.82, f32[192,128]{1,0:T(8,128)} %bitcast.83, f32[4,256,768]{2,1,0:T(8,128)} %bitcast.63, ...), custom_call_target="tpu_custom_call" | custom-call | tf_op jit(solution)/shard_map/land_exchange/pallas_call | solution.py:1280
  410.4 13.6 %land_back.1 = (f32[4,256,768]{2,1,0:T(8,128)}, f32[4,768,256]{2,1,0:T(8,128)}, f32[4,256,768]{2,1,0:T(8,128)}, f32[4,768,256]{2,1,0:T(8,128)}, f32[4,256,768]{2...) custom-call(f32[8,384,128]{2,1,0:T(8,128)} %bitcast.72, f32[4,256,768]{2,1,0:T(8,128)} %get-tuple-element.103.gq_ref, ...), custom_call_target="tpu_custom_call" | custom-call | tf_op jit(solution)/shard_map/land_back/pallas_call | solution.py:1330
  424.0 78.8 %grads.1 = (f32[3,96,128]{2,1,0:T(8,128)}, f32[3,192,128]{2,1,0:T(8,128)}, f32[3,96,128]{2,1,0:T(8,128)}, f32[1024,768]{1,0:T(8,128)}, f32[40,768]{1,0:T(8,128)}) custom-call(f32[4,768,256]{2,1,0:T(8,128)} %get-tuple-element.82.r1t_ref, f32[1024,768]{1,0:T(8,128)} %bitcast.60, f32[4,768,256]{2,1,0:T(8,128)} %get-tuple-element.108.gqt_ref, ...), custom_call_target="tpu_custom_call" | custom-call | tf_op jit(solution)/shard_map/grads/pallas_call | solution.py:1470
  502.8 1.2 copy.42
  504.0 0.7 slice_bitcast_fusion.6
  504.7 1.6 slice_reduce_fusion
  506.4 1.0 copy.43
  507.4 0.7 slice_bitcast_fusion.4
  508.1 1.4 slice.81
  509.5 1.7 copy_bitcast_fusion
  511.2 0.7 slice.86
  511.9 0.6 reshape.232
  512.5 1.2 copy.45
  513.7 1.0 reshape.234
  514.7 1.7 copy.49
  (11 shorter events, 0.1 us)
Async XLA Ops:
  0.7 3.0 copy-start.3
  1.4 1.5 copy-start.1
  59.4 0.6 copy-start.2
  502.8 11.8 %copy-start = (f32[1024,768]{1,0:T(8,128)S(1)}, f32[1024,768]{1,0:T(8,128)}, u32[]{:S(2)}) copy-start(f32[1024,768]{1,0:T(8,128)} %get-tuple-element.120) | copy-start | bytes 9437188
